TPU v7x, 128 devices: a whole 4x4x4 slice. The times are simulated.
128 devices in a mesh: gy: 8 (over x, core), gx: 16 (over z, y).
Axes of the slice: x: 4, y: 4, z: 4, core: 2. Of those that a mesh axis runs over, the one named last changes fastest.
Arguments:
- model_field: float32 [60, 2048, 2048], P(None, 'gy', 'gx'), may hold values from -160 to 160
- driver_field: float32 [60, 2048, 2048], P(None, 'gy', 'gx'), may hold values from -60 to 60
- nudge_rate: float32 [60], replicated, may hold values from 0.1 to 0.5
- increment_cap: float32 [60], replicated, may hold values from 1 to 3
Outputs:
- nudged: float32 [60, 2048, 2048], P(None, 'gy', 'gx')
All inputs are finite; a program needn't handle non-finite values.
Results may differ from a plain program's by a relative error of at most 0.00005.
Values sent between devices are 32-bit elements; how exact they have to be, the bound alone decides.
No kernel may reach another device: no remote copies, remote signals or barrier semaphores. Data moves between devices by JAX's collectives and lax.ppermute only.
A program may use at most 64 MiB of HBM per device.

v0:
```python
import math

import jax
import jax.numpy as jnp
from jax import lax
from jax.sharding import Mesh
from jax.sharding import PartitionSpec as P

MODES = 24
GY = ("gy_0", "gy_1")
GX = ("gx_0", "gx_1")


epsilon = 1e-06


def sent_to_all(value, axis):
    copies = jnp.broadcast_to(value, (lax.axis_size(axis), *value.shape))
    return lax.all_to_all(copies, axis, split_axis=0, concat_axis=0, tiled=True)


def over_copies(value, axis):
    everything = sent_to_all(value, axis)
    return jnp.sum(everything, axis=0)


def one_axis_at_a_time(value, axes):
    far, near = axes
    nearer = over_copies(value, near)
    return over_copies(nearer, far)


def padded_to(lines, count):
    spare = -lines.shape[0] % count
    if not spare:
        return lines
    return jnp.concatenate([lines, jnp.zeros((spare, *lines.shape[1:]), lines.dtype)])


def laid_out(tiles, dim):
    tiles = jnp.moveaxis(tiles, 0, dim)
    shape = tiles.shape
    return tiles.reshape(*shape[:dim], shape[dim] * shape[dim + 1], *shape[dim + 2 :])


def whole_of(value, axes, dim):
    far, near = axes
    first = sent_to_all(value, far)
    tiles = jnp.swapaxes(sent_to_all(first, near), 0, 1)
    return laid_out(tiles.reshape(-1, *value.shape), dim)


def in_blocks(value, dim, count):
    shape = value.shape
    tiles = value.reshape(*shape[:dim], count, shape[dim] // count, *shape[dim + 1 :])
    return jnp.moveaxis(tiles, dim, 0)


def sent_and_summed(value, axis, dim):
    count = lax.axis_size(axis)
    tiles = lax.all_to_all(in_blocks(value, dim, count), axis, 0, 0, tiled=True)
    return jnp.sum(tiles, axis=0)


def summed_rows(value, axes, dim):
    far, near = axes
    own = sent_and_summed(in_blocks(value, dim, lax.axis_size(far)), near, dim + 1)
    return jnp.sum(lax.all_to_all(own, far, 0, 0, tiled=True), axis=0)


def total_of(value, axes):
    lines = value.reshape(-1)
    padded = padded_to(lines, lax.axis_size(axes[0]) * lax.axis_size(axes[1]))
    whole = whole_of(summed_rows(padded, axes, 0), axes, 0)
    return lax.slice_in_dim(whole, 0, len(lines)).reshape(value.shape)


def basis_table(cell_count, start, length_all):
    positions = start + lax.iota(jnp.int32, cell_count)
    wavenumber = jnp.concatenate([lax.iota(jnp.int32, MODES), lax.iota(jnp.int32, MODES) + 1])
    phases = positions[:, None] * wavenumber[None, :] % length_all
    angles = phases.astype(jnp.float32) * (2.0 * math.pi / length_all)
    column = lax.iota(jnp.int32, 2 * MODES)
    weights = jnp.where(column == 0, math.sqrt(1.0 / length_all), math.sqrt(2.0 / length_all))
    return jnp.where(column[None, :] < MODES, jnp.cos(angles), jnp.sin(angles)) * weights[None, :]


def per_device(model_field, driver_field, nudge_rate, increment_cap):
    highest = lax.Precision.HIGHEST
    fields, rows, columns = model_field.shape
    row_total = rows * lax.axis_size(GY)
    column_total = columns * lax.axis_size(GX)
    basis_rows = basis_table(rows, lax.axis_index(GY) * rows, row_total)
    basis_columns = basis_table(columns, lax.axis_index(GX) * columns, column_total)
    difference = driver_field - model_field
    local_squares = jnp.sum(difference * difference, axis=(1, 2))
    squares = one_axis_at_a_time(local_squares, ("gy_0", ("gy_1", "gx_0", "gx_1")))
    extra = ()

    def over_columns(source):
        return jnp.einsum("fyx,xk->fyk", source, basis_columns, precision=highest)

    def over_rows(partial_value):
        return jnp.einsum("yj,fyk->fjk", basis_rows, partial_value, precision=highest)

    sources = (difference,)
    count = len(sources)
    summed = jax.tree.map(
        lambda part: total_of(part, (("gy_0", "gy_1", "gx_0"), "gx_1")),
        tuple((over_rows(over_columns(source)) for source in sources)) + extra,
    )
    coefficients = summed[0]
    spread = jnp.sqrt(squares / (row_total * column_total) + epsilon)
    strength = nudge_rate * jnp.minimum(1.0, increment_cap / spread)
    rows_part = jnp.einsum("yj,fjk->fyk", basis_rows, coefficients, precision=highest)
    large_scale = jnp.einsum("fyk,xk->fyx", rows_part, basis_columns, precision=highest)
    return model_field + strength[:, None, None] * large_scale


def solution(mesh):
    finer = Mesh(mesh.devices.reshape(4, 2, 4, 4), ("gy_0", "gy_1", "gx_0", "gx_1"))
    placed = (P(None, GY, GX), P(None, GY, GX), P(), P())
    return jax.shard_map(
        per_device, mesh=finer, in_specs=placed, out_specs=P(None, GY, GX), check_vma=False
    )
```

profile of v0, /device:TPU:1, one launch (start us, length us, event | category | flops | bytes accessed | tf_op | source)
XLA Modules:
  0.0 117.2 jit_solution(17111940243291722281)
XLA Ops:
  0.1 12.4 %fusion = f32[60,256,48]{1,2,0:T(8,128)S(1)} fusion(f32[60,256,128]{2,1,0:T(8,128)} %param.5, f32[60,256,128]{2,1,0:T(8,128)} %param.4, f32[48]{0:T(128)S(1)} %compare_select_fusion, s32[48]{0:T(128)S(1)} %pad_add_fusion, s32[128]{0:T(128)S(1)} %iota_add_fusion.2, pred[48]{0:T(512)(128)(4,1)S(1)} %iota_compare_fusion), kind=kOutput, calls=%fused_computation.2 | convolution fusion | flops 1134526464 | bytes 18678704 | tf_op jit(solution)/shard_map/fyx,xk->fyk/dot_general | solution.py:101
  12.6 2.7 %convolution_bitcast_fusion = f32[60,48,48]{1,2,0:T(8,128)S(1)} fusion(f32[60,256,48]{1,2,0:T(8,128)S(1)} %fusion, f32[48]{0:T(128)S(1)} %compare_select_fusion, s32[48]{0:T(128)S(1)} %pad_add_fusion, s32[256]{0:T(256)S(1)} %iota_add_fusion, pred[48]{0:T(512)(128)(4,1)S(1)} %iota_compare_fusion), kind=kOutput, calls=%fused_computation.5 | convolution fusion | flops 424869888 | bytes 3503536 | tf_op jit(solution)/shard_map/yj,fyk->fjk/dot_general | solution.py:104
  15.3 0.4 copy.16
  15.7 1.0 reshape_reshape_reshape.6
  16.8 13.8 %all_to_all.40 = f32[4,32,1080]{2,1,0:T(8,128)S(1)} all-to-all(f32[4,32,1080]{2,1,0:T(8,128)S(1)} %copy.17), channel_id=1, replica_groups=mesh['gy_0'=4,'gy_1'=2,'gx_0'=4,'gx_1'=4] {'gx_1'}, dimensions={0} | all-to-all | bytes 1105920 | tf_op jit(solution)/shard_map/all_to_all | solution.py:61
  30.6 0.8 all_to_all.29
  31.4 10.1 %all-to-all-start.3 = ((f32[32,1,1080]{2,1,0:T(1,128)}), f32[32,1,1080]{2,1,0:T(1,128)S(1)}, u32[]{:S(2)}, u32[]{:S(2)}) async-start(f32[32,1,1080]{2,1,0:T(1,128)} %all_to_all.29), calls=%async_computation.3 | async-start | bytes 294912 | tf_op jit(solution)/shard_map/all_to_all | solution.py:68
  41.5 6.7 %multiply_reduce_fusion = f32[60]{0:T(128)S(1)} fusion(f32[60,256,128]{2,1,0:T(8,128)} %param.5, f32[60,256,128]{2,1,0:T(8,128)} %param.4), kind=kLoop, calls=%fused_computation.1 | loop fusion | flops 5898180 | bytes 15728880 | tf_op jit(solution)/shard_map/reduce_sum | solution.py:96
  48.2 1.0 all-to-all-done.3
  49.2 0.6 broadcast_in_dim.47
  49.8 4.6 %all-to-all-start = ((f32[32,1,60]{2,1,0:T(1,128)}), f32[32,1,60]{2,1,0:T(1,128)S(1)}, u32[]{:S(2)}, u32[]{:S(2)}) async-start(f32[32,1,60]{2,1,0:T(1,128)} %broadcast_in_dim.47), calls=%async_computation | async-start | bytes 32768 | tf_op jit(solution)/shard_map/all_to_all | solution.py:19
  54.5 6.7 %all-to-all-done = f32[32,1,60]{2,1,0:T(1,128)S(1)} async-done(((f32[32,1,60]{2,1,0:T(1,128)}), f32[32,1,60]{2,1,0:T(1,128)S(1)}, u32[]{:S(2)}, u32[]{:S(2)}) %all-to-all-start) | async-done | bytes 7712 | tf_op jit(solution)/shard_map/all_to_all | solution.py:19
  61.2 0.7 broadcast_in_dim.53
  61.9 5.8 %all-to-all-start.4 = ((f32[32,1,1080]{2,1,0:T(1,128)}), f32[32,1,1080]{2,1,0:T(1,128)S(1)}, u32[]{:S(2)}, u32[]{:S(2)}) async-start(f32[32,1,1080]{2,1,0:T(1,128)} %broadcast_in_dim.53), calls=%async_computation.4 | async-start | bytes 294912 | tf_op jit(solution)/shard_map/all_to_all | solution.py:19
  67.7 7.7 %all-to-all-done.4 = f32[32,1,1080]{2,1,0:T(1,128)S(1)} async-done(((f32[32,1,1080]{2,1,0:T(1,128)}), f32[32,1,1080]{2,1,0:T(1,128)S(1)}, u32[]{:S(2)}, u32[]{:S(2)}) %all-to-all-start.4) | async-done | bytes 138272 | tf_op jit(solution)/shard_map/all_to_all | solution.py:19
  75.4 0.6 broadcast_in_dim.48
  76.0 3.2 %all-to-all-start.1 = ((f32[4,1,60]{2,1,0:T(1,128)}), f32[4,1,60]{2,1,0:T(1,128)S(1)}, u32[]{:S(2)}, u32[]{:S(2)}) async-start(f32[4,1,60]{2,1,0:T(1,128)} %broadcast_in_dim.48), calls=%async_computation.1 | async-start | bytes 4096 | tf_op jit(solution)/shard_map/all_to_all | solution.py:19
  79.3 4.0 %all-to-all-done.1 = f32[4,1,60]{2,1,0:T(1,128)S(1)} async-done(((f32[4,1,60]{2,1,0:T(1,128)}), f32[4,1,60]{2,1,0:T(1,128)S(1)}, u32[]{:S(2)}, u32[]{:S(2)}) %all-to-all-start.1) | async-done | bytes 992 | tf_op jit(solution)/shard_map/all_to_all | solution.py:19
  83.3 0.9 broadcast_in_dim.54
  84.1 3.7 %all-to-all-start.5 = ((f32[4,32,1080]{2,1,0:T(8,128)}), f32[4,32,1080]{2,1,0:T(8,128)S(1)}, u32[]{:S(2)}, u32[]{:S(2)}) async-start(f32[4,32,1080]{2,1,0:T(8,128)} %broadcast_in_dim.54), calls=%async_computation.5 | async-start | bytes 1179648 | tf_op jit(solution)/shard_map/all_to_all | solution.py:19
  87.8 8.0 %all-to-all-done.5 = f32[4,32,1080]{2,1,0:T(8,128)S(1)} async-done(((f32[4,32,1080]{2,1,0:T(8,128)}), f32[4,32,1080]{2,1,0:T(8,128)S(1)}, u32[]{:S(2)}, u32[]{:S(2)}) %all-to-all-start.5) | async-done | bytes 552992 | tf_op jit(solution)/shard_map/all_to_all | solution.py:19
  96.2 1.1 reshape_reshape_reshape.7
  97.3 2.8 %fusion.6 = f32[60,48,256]{2,1,0:T(8,128)S(1)} fusion(f32[60,48,48]{2,1,0:T(8,128)S(1)} %reshape_reshape_reshape.7, f32[48]{0:T(128)S(1)} %compare_select_fusion, s32[48]{0:T(128)S(1)} %pad_add_fusion, s32[256]{0:T(256)S(1)} %iota_add_fusion, pred[48]{0:T(512)(128)(4,1)S(1)} %iota_compare_fusion), kind=kOutput, calls=%fused_computation.15 | convolution fusion | flops 424869888 | bytes 3503536 | tf_op jit(solution)/shard_map/yj,fjk->fyk/dot_general | solution.py:115
  100.1 17.2 %multiply_add_fusion = f32[60,256,128]{2,1,0:T(8,128)} fusion(f32[60,256,128]{2,1,0:T(8,128)} %param.4, f32[60]{0:T(128)S(1)} %minimum_multiply_fusion, f32[60,48,256]{2,1,0:T(8,128)S(1)} %fusion.6, f32[48]{0:T(128)S(1)} %compare_select_fusion, s32[48]{0:T(128)S(1)} %pad_add_fusion, s32[128]{0:T(128)S(1)} %iota_add_fusion.2, pred[48]{0:T(512)(128)(4,1)S(1)} %iota_compare_fusion), kind=kOutput, calls=%fused_computation | convolution fusion | flops 1136492544 | bytes 18678944 | tf_op jit(solution)/shard_map/fyk,xk->fyx/dot_general | solution.py:116
  (19 shorter events, 0.7 us)
Async XLA Ops:
  31.4 17.8 %all-to-all-start.3 = ((f32[32,1,1080]{2,1,0:T(1,128)}), f32[32,1,1080]{2,1,0:T(1,128)S(1)}, u32[]{:S(2)}, u32[]{:S(2)}) async-start(f32[32,1,1080]{2,1,0:T(1,128)} %all_to_all.29), calls=%async_computation.3 | async-start | bytes 294912 | tf_op jit(solution)/shard_map/all_to_all | solution.py:68
  41.5 46.3 %copy-start = (f32[60]{0:T(128)S(1)}, f32[60]{0:T(128)}, u32[]{:S(2)}) copy-start(f32[60]{0:T(128)} %param.6) | copy-start | bytes 724
  41.5 46.3 %copy-start.1 = (f32[60]{0:T(128)S(1)}, f32[60]{0:T(128)}, u32[]{:S(2)}) copy-start(f32[60]{0:T(128)} %param.7) | copy-start | bytes 724
  49.8 11.4 %all-to-all-start = ((f32[32,1,60]{2,1,0:T(1,128)}), f32[32,1,60]{2,1,0:T(1,128)S(1)}, u32[]{:S(2)}, u32[]{:S(2)}) async-start(f32[32,1,60]{2,1,0:T(1,128)} %broadcast_in_dim.47), calls=%async_computation | async-start | bytes 32768 | tf_op jit(solution)/shard_map/all_to_all | solution.py:19
  61.9 13.5 %all-to-all-start.4 = ((f32[32,1,1080]{2,1,0:T(1,128)}), f32[32,1,1080]{2,1,0:T(1,128)S(1)}, u32[]{:S(2)}, u32[]{:S(2)}) async-start(f32[32,1,1080]{2,1,0:T(1,128)} %broadcast_in_dim.53), calls=%async_computation.4 | async-start | bytes 294912 | tf_op jit(solution)/shard_map/all_to_all | solution.py:19
  76.0 7.2 %all-to-all-start.1 = ((f32[4,1,60]{2,1,0:T(1,128)}), f32[4,1,60]{2,1,0:T(1,128)S(1)}, u32[]{:S(2)}, u32[]{:S(2)}) async-start(f32[4,1,60]{2,1,0:T(1,128)} %broadcast_in_dim.48), calls=%async_computation.1 | async-start | bytes 4096 | tf_op jit(solution)/shard_map/all_to_all | solution.py:19
  84.1 11.7 %all-to-all-start.5 = ((f32[4,32,1080]{2,1,0:T(8,128)}), f32[4,32,1080]{2,1,0:T(8,128)S(1)}, u32[]{:S(2)}, u32[]{:S(2)}) async-start(f32[4,32,1080]{2,1,0:T(8,128)} %broadcast_in_dim.54), calls=%async_computation.5 | async-start | bytes 1179648 | tf_op jit(solution)/shard_map/all_to_all | solution.py:19
where the time goes:
time: 119 us; the launch traced here: 117 us
  matrix products  35.1 us (29%)
  starting transfers between devices  27.3 us (23%)
  waiting for transfers between devices  27.3 us (23%)
  blocking collectives  13.8 us (12%)
  other arithmetic  7 us (6%)
  local copies, waits for them, and re-layouts  6.52 us (5%)
    all_to_all x4, waiting for transfers between devices, sent_to_all(): return lax.all_to_all(copies, axis, split_axis=0, concat_axis=0, tiled=True)  26.4 us
    all_to_all x4, starting transfers between devices, sent_to_all(): return lax.all_to_all(copies, axis, split_axis=0, concat_axis=0, tiled=True)  17.2 us
    dot_general x1, matrix products, per_device(): jnp.einsum('fyk,xk->fyx', rows_part, basis_columns, precision=highest)  17.2 us
    all_to_all x1, blocking collectives, sent_and_summed(): tiles = lax.all_to_all(in_blocks(value, dim, count), axis, 0, 0, tiled=True)  13.8 us
    dot_general x1, matrix products, over_columns(): return jnp.einsum('fyx,xk->fyk', source, basis_columns, precision=highest)  12.4 us
    all_to_all x1, starting transfers between devices, summed_rows(): return jnp.sum(lax.all_to_all(own, far, 0, 0, tiled=True), axis=0)  10.1 us
    reduce_sum x1, other arithmetic, per_device(): local_squares = jnp.sum(difference * difference, axis=(1, 2))  6.71 us
    broadcast_in_dim x4, local copies, waits for them, and re-layouts, sent_to_all(): copies = jnp.broadcast_to(value, (lax.axis_size(axis), *value.shape))  2.78 us
  transfers between devices with their start and end apart: 5, of which 5 were waited for; matrix products, arithmetic and copies ran while one was open for 6% of the time, Pallas kernels for 0%

commit v1 on v0

v1 whole, which is shorter than its diff:
```python
import numpy as np

import jax
import jax.numpy as jnp
import ml_dtypes
from jax import lax
from jax.experimental import pallas as pl
from jax.experimental.pallas import tpu as pltpu
from jax.sharding import Mesh
from jax.sharding import PartitionSpec as P

MODES = 24
WAVES = 2 * MODES
GROUP = 10
BLOCK = 5
TILES = 4
LANES = 128
SLOTS = 16
CHIP = ("x", "z", "y")
EPSILON = 1e-06


def basis_table(length):
    positions = np.arange(length)
    wavenumber = np.concatenate([np.arange(MODES), np.arange(MODES) + 1])
    phases = positions[:, None] * wavenumber[None, :] % length
    angles = phases * (2.0 * np.pi / length)
    column = np.arange(WAVES)
    weights = np.where(column == 0, np.sqrt(1.0 / length), np.sqrt(2.0 / length))
    return np.where(column[None, :] < MODES, np.cos(angles), np.sin(angles)) * weights[None, :]


def split_table(length, parts):
    table = basis_table(length).astype(np.float32)
    high = table.astype(ml_dtypes.bfloat16)
    low = (table - high.astype(np.float32)).astype(ml_dtypes.bfloat16)
    shape = (parts, length // parts, WAVES)
    return high.reshape(shape), low.reshape(shape)


def split(value):
    high = value.astype(jnp.bfloat16)
    low = (value - high.astype(jnp.float32)).astype(jnp.bfloat16)
    return high, low


def dot(left, right, contract):
    return lax.dot_general(left, right, (contract, ((), ())), preferred_element_type=jnp.float32)


def analysis_kernel(where, model, driver, rows, columns, mine, other, along_y, squares):
    step = pl.program_id(0)
    odd = step % 2

    @pl.when(step == 0)
    def _():
        along_y[...] = jnp.zeros_like(along_y)
        squares[...] = jnp.zeros_like(squares)

    for i in range(BLOCK):
        difference = driver[i] - model[i]
        field = odd * BLOCK + i
        squares[pl.ds(field, 1), :] = jnp.sum(difference * difference, axis=0, keepdims=True)
        parts = jnp.concatenate(split(difference), axis=1)
        product = dot(rows[0], parts, ((1,), (0,)))
        product = product[:WAVES] + product[WAVES:]
        high, low = split(product[:, :LANES] + product[:, LANES:])
        place = pl.ds(pl.multiple_of(field * WAVES, 16), WAVES)
        along_y[place, :LANES] = high
        along_y[place, LANES:] = low

    @pl.when(odd == 1)
    def _():
        both = dot(columns[0], along_y[...], ((1,), (1,)))
        both = both[:WAVES] + both[WAVES:]
        tiles = [both[:, t * LANES : (t + 1) * LANES] for t in range(TILES)]
        total = jnp.sum(squares[...], axis=1, keepdims=True)
        lane = lax.broadcasted_iota(jnp.int32, (SLOTS, LANES), 1)
        top = jnp.where(lane == LANES - 1, total, tiles[-1][:SLOTS])
        tiles[-1] = jnp.concatenate([top, tiles[-1][SLOTS:]], axis=0)
        group = step // 2
        half = group // 3
        first = pl.multiple_of((group % 3) * (TILES * WAVES), 8)

        def keep(ref):
            for t in range(TILES):
                ref[pl.ds(first + t * WAVES, WAVES), :] = tiles[t]

        pl.when(half == where[2])(lambda: keep(mine))
        pl.when(half != where[2])(lambda: keep(other))


def synthesis_kernel(
    cells, where, model, own, sibling, rate, cap, rows, columns, nudged, along_x, strength
):
    step = pl.program_id(0)
    odd = step % 2

    def prepare(ref):
        first = pl.multiple_of(((step // 2) % 3) * (TILES * WAVES), 8)
        tiles = [ref[pl.ds(first + t * WAVES, WAVES), :] for t in range(TILES)]
        total = tiles[-1][:SLOTS, LANES - 1 :]
        spread = jnp.sqrt(total / cells + EPSILON)
        strength[...] = rate[0] * jnp.minimum(1.0, cap[0] / spread)
        high, low = split(jnp.concatenate(tiles, axis=1))
        both = dot(high, columns[0], ((0,), (0,))) + dot(low, columns[0], ((0,), (0,)))
        along_x[...] = both[:, :LANES] + both[:, LANES:]

    pl.when((odd == 0) & (step < 6))(lambda: prepare(own))
    pl.when((odd == 0) & (step >= 6))(lambda: prepare(sibling))

    for i in range(BLOCK):
        field = odd * BLOCK + i
        place = pl.ds(pl.multiple_of(field * WAVES, 8), WAVES)
        high, low = split(along_x[place, :] * strength[pl.ds(field, 1), :])
        stack = jnp.concatenate([high, low, high], axis=0)
        nudged[i] = model[i] + dot(rows[0], stack, ((1,), (0,)))


def analysis(where, model, driver, rows, columns):
    fields, height, width = model.shape
    steps = fields // BLOCK
    half = fields // GROUP // 2 * TILES * WAVES
    block = pl.BlockSpec((BLOCK, height, width), lambda s, w: (s, 0, 0))
    whole = pl.BlockSpec((half, LANES), lambda s, w: (0, 0))
    return pl.pallas_call(
        analysis_kernel,
        out_shape=[jax.ShapeDtypeStruct((half, LANES), jnp.float32)] * 2,
        grid_spec=pltpu.PrefetchScalarGridSpec(
            num_scalar_prefetch=1,
            grid=(steps,),
            in_specs=[
                block,
                block,
                pl.BlockSpec((1, *rows.shape[1:]), lambda s, w: (w[0], 0, 0)),
                pl.BlockSpec((1, *columns.shape[1:]), lambda s, w: (w[1], 0, 0)),
            ],
            out_specs=[whole, whole],
            scratch_shapes=[
                pltpu.VMEM((TILES * LANES, 2 * LANES), jnp.bfloat16),
                pltpu.VMEM((SLOTS, LANES), jnp.float32),
            ],
        ),
        name="analysis",
    )(where, model, driver, rows, columns)


def synthesis(where, model, own, sibling, rate, cap, rows, columns, cells):
    fields, height, width = model.shape
    steps = fields // BLOCK
    groups = fields // GROUP

    def at(s, w):
        return ((s + w[2] * (steps // 2)) % steps, 0, 0)

    def group_at(s, w):
        return ((s // 2 + w[2] * (groups // 2)) % groups, 0, 0)

    block = pl.BlockSpec((BLOCK, height, width), at)
    whole = pl.BlockSpec(own.shape, lambda s, w: (0, 0))
    limits = pl.BlockSpec((1, SLOTS, LANES), group_at)
    return pl.pallas_call(
        lambda *refs: synthesis_kernel(cells, *refs),
        out_shape=jax.ShapeDtypeStruct(model.shape, jnp.float32),
        grid_spec=pltpu.PrefetchScalarGridSpec(
            num_scalar_prefetch=1,
            grid=(steps,),
            in_specs=[
                block,
                whole,
                whole,
                limits,
                limits,
                pl.BlockSpec((1, *rows.shape[1:]), lambda s, w: (w[0], 0, 0)),
                pl.BlockSpec((1, *columns.shape[1:]), lambda s, w: (w[1], 0, 0)),
            ],
            out_specs=block,
            scratch_shapes=[
                pltpu.VMEM((TILES * LANES, LANES), jnp.float32),
                pltpu.VMEM((SLOTS, LANES), jnp.float32),
            ],
        ),
        name="synthesis",
    )(where, model, own, sibling, rate, cap, rows, columns)


def per_group(value):
    rows = value.reshape(-1, GROUP, 1)
    rows = jnp.pad(rows, ((0, 0), (0, SLOTS - GROUP), (0, 0)), constant_values=1.0)
    return jnp.broadcast_to(rows, (rows.shape[0], SLOTS, LANES))


def per_device(model_field, driver_field, nudge_rate, increment_cap):
    fields, height, width = model_field.shape
    parts_y = lax.axis_size(("x", "c"))
    parts_x = lax.axis_size(("z", "y"))
    chips = lax.axis_size(CHIP)
    swap = [(0, 1), (1, 0)]
    where = jnp.stack(
        [lax.axis_index(("x", "c")), lax.axis_index(("z", "y")), lax.axis_index("c")]
    ).astype(jnp.int32)

    high_y, low_y = split_table(height * parts_y, parts_y)
    high_x, low_x = split_table(width * parts_x, parts_x)
    turned = lambda table: np.swapaxes(table, 1, 2)
    rows_in = np.concatenate([turned(high_y), turned(low_y)], axis=1)
    columns_in = np.concatenate([turned(high_x), turned(low_x)], axis=1)
    columns_in = np.concatenate([columns_in, columns_in], axis=2)
    rows_out = np.concatenate([high_y, high_y, low_y], axis=2)
    columns_out = np.concatenate([turned(high_x), turned(low_x)], axis=2)

    mine, other = analysis(where, model_field, driver_field, rows_in, columns_in)
    pair = mine + lax.ppermute(other, "c", swap)
    pieces = lax.all_to_all(pair.reshape(chips, 1, -1), CHIP, 0, 0, tiled=True)
    piece = jnp.sum(pieces, axis=0, keepdims=True)
    own = lax.all_to_all(jnp.broadcast_to(piece, pieces.shape), CHIP, 0, 0, tiled=True)
    own = own.reshape(mine.shape)
    sibling = lax.ppermute(own, "c", swap)
    cells = height * parts_y * width * parts_x
    return synthesis(
        where,
        model_field,
        own,
        sibling,
        per_group(nudge_rate),
        per_group(increment_cap),
        rows_out,
        columns_out,
        float(cells),
    )


def solution(mesh):
    finer = Mesh(mesh.devices.reshape(4, 2, 4, 4), ("x", "c", "z", "y"))
    field = P(None, ("x", "c"), ("z", "y"))
    return jax.shard_map(
        per_device,
        mesh=finer,
        in_specs=(field, field, P(), P()),
        out_specs=field,
        check_vma=False,
    )
```

time: 119 us -> 73.8 us (0.62)
  matrix products: 35.1 us -> 0 us
  Pallas kernels: 0 us -> 27.7 us
  waiting for transfers between devices: 27.3 us -> 2.45 us
  starting transfers between devices: 27.3 us -> 4.6 us
  blocking collectives: 13.8 us -> 34.9 us
  other arithmetic: 7 us -> 1.76 us
  local copies, waits for them, and re-layouts: 6.52 us -> 1.76 us
    dot_general x4 -> x0, matrix products: 35.1 us -> none  [the longest x1 17.2 us: per_device(): jnp.einsum('fyk,xk->fyx', rows_part, basis_columns, precision=highest)]
    pallas_call x0 -> x2, Pallas kernels: none -> 27.7 us  [the longest x1 14.4 us: synthesis(): pl.pallas_call(lambda *refs: synthesis_kernel(cells, *refs), out_shape=ja...]
    all_to_all x5 -> x0, waiting for transfers between devices: 27.3 us -> none  [the longest x4 26.4 us: sent_to_all(): return lax.all_to_all(copies, axis, split_axis=0, concat_axis=0, tiled=True)]
    all_to_all x5 -> x0, starting transfers between devices: 27.3 us -> none  [the longest x4 17.2 us: sent_to_all(): return lax.all_to_all(copies, axis, split_axis=0, concat_axis=0, tiled=True)]
    all_to_all x1 -> x2, blocking collectives: 13.8 us -> 34.9 us  [the longest x1 20.9 us: per_device(): pieces = lax.all_to_all(pair.reshape(chips, 1, -1), CHIP, 0, 0, tiled=True)]
    reduce_sum x5 -> x1, other arithmetic: 6.89 us -> 0.2 us  [per_device(): piece = jnp.sum(pieces, axis=0, keepdims=True)]
    ppermute x0 -> x2, starting transfers between devices: none -> 4.6 us  [the longest x1 3.17 us: per_device(): sibling = lax.ppermute(own, 'c', swap)]
    ppermute x0 -> x2, waiting for transfers between devices: none -> 2.45 us  [the longest x1 1.42 us: per_device(): pair = mine + lax.ppermute(other, 'c', swap)]
  transfers between devices with their start and end apart: 5 -> 2, of which waited for: 5 -> 2; matrix products, arithmetic and copies ran while one was open for 6% -> 0% of each run, Pallas kernels for 0% -> 0%
where the time goes in v1:
time: 73.8 us; the launch traced here: 73.2 us
  blocking collectives  34.9 us (47%)
  Pallas kernels  27.7 us (38%)
  starting transfers between devices  4.6 us (6%)
  waiting for transfers between devices  2.45 us (3%)
  other arithmetic  1.76 us (2%)
  local copies, waits for them, and re-layouts  1.76 us (2%)
    all_to_all x1, blocking collectives, per_device(): pieces = lax.all_to_all(pair.reshape(chips, 1, -1), CHIP, 0, 0, tiled=True)  20.9 us
    pallas_call x1, Pallas kernels, synthesis(): pl.pallas_call(lambda *refs: synthesis_kernel(cells, *refs), out_shape=ja...  14.4 us
    all_to_all x1, blocking collectives, per_device(): lax.all_to_all(jnp.broadcast_to(piece, pieces.shape), CHIP, 0, 0, tiled=T...  14 us
    pallas_call x1, Pallas kernels, analysis(): pl.pallas_call(analysis_kernel, out_shape=[jax.ShapeDtypeStruct((half, LA...  13.2 us
    ppermute x1, starting transfers between devices, per_device(): sibling = lax.ppermute(own, 'c', swap)  3.17 us
  transfers between devices with their start and end apart: 2, of which 2 were waited for; matrix products, arithmetic and copies ran while one was open for 0% of the time, Pallas kernels for 0%

profile of v1, /device:TPU:1, one launch (start us, length us, event | category | flops | bytes accessed | tf_op | source)
XLA Modules:
  0.0 73.2 jit_solution(558963051203444752)
XLA Ops:
  0.0 0.6 pad_add_fusion.where.refs_0_
  0.6 0.0 copy-start.2
  0.6 0.0 copy-start.3
  0.6 13.2 %analysis.1 = (f32[576,128]{1,0:T(8,128)}, f32[576,128]{1,0:T(8,128)}) custom-call(s32[3]{0:T(128)} %pad_add_fusion.where.refs_0_, f32[60,256,128]{2,1,0:T(8,128)} %refs_1_.1, f32[60,256,128]{2,1,0:T(8,128)} %driver.1, bf16[8,96,256]{2,1,0:T(8,128)(2,1)} %constant.33.clone.rows, bf16[16,96,256]{2,1,0:T(8,128)(2,1)} %constant.34.clone.columns), custom_call_target="tpu_custom_call" | custom-call | tf_op jit(solution)/shard_map/analysis/pallas_call | solution.py:126
  13.8 1.4 %collective-permute-start = (f32[576,128]{1,0:T(8,128)}, f32[576,128]{1,0:T(8,128)S(1)}, u32[]{:S(2)}, u32[]{:S(2)}) collective-permute-start(f32[576,128]{1,0:T(8,128)} %get-tuple-element.8), channel_id=1, source_target_pairs={{0,16},{16,0},{1,17},{17,1},{2,18},{18,2},{3,19},{19,3},{4,20},{20... | collective-permute-start | bytes 884744 | tf_op jit(solution)/shard_map/ppermute | solution.py:213
  15.2 1.4 %collective-permute-done = f32[576,128]{1,0:T(8,128)S(1)} collective-permute-done((f32[576,128]{1,0:T(8,128)}, f32[576,128]{1,0:T(8,128)S(1)}, u32[]{:S(2)}, u32[]{:S(2)}) %collective-permute-start) | collective-permute-done | bytes 294944 | tf_op jit(solution)/shard_map/ppermute | solution.py:213
  16.6 1.0 %add.15 = f32[576,128]{1,0:T(8,128)S(1)} add(f32[576,128]{1,0:T(8,128)} %get-tuple-element.7, f32[576,128]{1,0:T(8,128)S(1)} %collective-permute-done) | non-fusion elementwise | flops 73728 | bytes 884736 | tf_op jit(solution)/shard_map/add | solution.py:213
  17.6 20.9 %all_to_all.10 = f32[64,1,1152]{2,1,0:T(1,128)S(1)} all-to-all(f32[64,1,1152]{2,1,0:T(1,128)S(1)} %bitcast.9), channel_id=1, replica_groups=mesh['x'=4,'c'=2,'z'=4,'y'=4] {'x','z','y'}, dimensions={0} | all-to-all | bytes 589824 | tf_op jit(solution)/shard_map/all_to_all | solution.py:214
  38.5 0.2 reduce_sum.9
  38.7 0.2 broadcast_in_dim.20
  38.9 14.0 %all_to_all.11 = f32[64,1,1152]{2,1,0:T(1,128)S(1)} all-to-all(f32[64,1,1152]{2,1,0:T(1,128)S(1)} %broadcast_in_dim.20), channel_id=1, replica_groups=mesh['x'=4,'c'=2,'z'=4,'y'=4] {'x','z','y'}, dimensions={0} | all-to-all | bytes 589824 | tf_op jit(solution)/shard_map/all_to_all | solution.py:216
  52.9 0.0 copy-start
  52.9 3.2 %collective-permute-start.1 = (f32[576,128]{1,0:T(8,128)S(1)}, f32[576,128]{1,0:T(8,128)S(1)}, u32[]{:S(2)}, u32[]{:S(2)}) collective-permute-start(f32[576,128]{1,0:T(8,128)S(1)} %bitcast.10), channel_id=1, source_target_pairs={{0,16},{16,0},{1,17},{17,1},{2,18},{18,2},{3,19},{19,3},{4,20},{20... | collective-permute-start | bytes 884744 | tf_op jit(solution)/shard_map/ppermute | solution.py:218
  56.1 0.0 copy-done.2
  56.1 0.1 reshape.19
  56.2 0.0 copy-done.3
  56.2 0.1 reshape.20
  56.2 1.0 %collective-permute-done.1.refs_3_ = f32[576,128]{1,0:T(8,128)S(1)} collective-permute-done((f32[576,128]{1,0:T(8,128)S(1)}, f32[576,128]{1,0:T(8,128)S(1)}, u32[]{:S(2)}, u32[]{:S(2)}) %collective-permute-start.1) | collective-permute-done | bytes 294944 | tf_op jit(solution)/shard_map/ppermute | solution.py:218
  57.3 0.0 copy-start.1
  57.3 0.7 %broadcast_in_dim.24.refs_5_ = f32[6,16,128]{2,1,0:T(8,128)} broadcast(f32[6,16]{1,0:T(8,128)S(1)} %pad_bitcast_fusion), dimensions={0,1} | broadcast | bytes 49536 | tf_op jit(solution)/shard_map/broadcast_in_dim | solution.py:190
  58.0 0.7 broadcast_in_dim.22.refs_4_
  58.7 0.0 copy-done
  58.7 0.0 copy-done.1
  58.7 14.4 %synthesis.1 = f32[60,256,128]{2,1,0:T(8,128)} custom-call(s32[3]{0:T(128)} %pad_add_fusion.where.refs_0_, f32[60,256,128]{2,1,0:T(8,128)} %refs_1_.1, f32[576,128]{1,0:T(8,128)} %bitcast.11, f32[576,128]{1,0:T(8,128)} %copy-done.1, f32[6,16,128]{2,1,0:T(8,128)} %broadcast_in_dim.22.refs_4_, f32[6,16,128]{2,1,0:T(8,128)} %broadcast_in_dim.24.refs_5_, ...), custom_call_target="tpu_custom_call" | custom-call | tf_op jit(solution)/shard_map/synthesis/pallas_call | solution.py:162
  (2 shorter events, 0.0 us)
Async XLA Ops:
  0.6 55.5 %copy-start.2 = (f32[60]{0:T(128)S(1)}, f32[60]{0:T(128)}, u32[]{:S(2)}) copy-start(f32[60]{0:T(128)} %param.10) | copy-start | bytes 724
  0.6 55.6 %copy-start.3 = (f32[60]{0:T(128)S(1)}, f32[60]{0:T(128)}, u32[]{:S(2)}) copy-start(f32[60]{0:T(128)} %param.11) | copy-start | bytes 724
  13.8 2.8 %collective-permute-start = (f32[576,128]{1,0:T(8,128)}, f32[576,128]{1,0:T(8,128)S(1)}, u32[]{:S(2)}, u32[]{:S(2)}) collective-permute-start(f32[576,128]{1,0:T(8,128)} %get-tuple-element.8), channel_id=1, source_target_pairs={{0,16},{16,0},{1,17},{17,1},{2,18},{18,2},{3,19},{19,3},{4,20},{20... | collective-permute-start | bytes 884744 | tf_op jit(solution)/shard_map/ppermute | solution.py:213
  52.9 5.8 %copy-start = (f32[64,1,1152]{2,1,0:T(1,128)}, f32[64,1,1152]{2,1,0:T(1,128)S(1)}, u32[]{:S(2)}) copy-start(f32[64,1,1152]{2,1,0:T(1,128)S(1)} %all_to_all.11) | copy-start | bytes 884740
  52.9 4.4 %collective-permute-start.1 = (f32[576,128]{1,0:T(8,128)S(1)}, f32[576,128]{1,0:T(8,128)S(1)}, u32[]{:S(2)}, u32[]{:S(2)}) collective-permute-start(f32[576,128]{1,0:T(8,128)S(1)} %bitcast.10), channel_id=1, source_target_pairs={{0,16},{16,0},{1,17},{17,1},{2,18},{18,2},{3,19},{19,3},{4,20},{20... | collective-permute-start | bytes 884744 | tf_op jit(solution)/shard_map/ppermute | solution.py:218
  57.3 1.4 %copy-start.1 = (f32[576,128]{1,0:T(8,128)}, f32[576,128]{1,0:T(8,128)S(1)}, u32[]{:S(2)}) copy-start(f32[576,128]{1,0:T(8,128)S(1)} %collective-permute-done.1.refs_3_) | copy-start | bytes 884740

commit v2 on v1

v2 whole, which is shorter than its diff:
```python
import numpy as np

import jax
import jax.numpy as jnp
import ml_dtypes
from jax import lax
from jax.experimental import pallas as pl
from jax.experimental.pallas import tpu as pltpu
from jax.sharding import Mesh
from jax.sharding import PartitionSpec as P

MODES = 24
WAVES = 2 * MODES
GROUP = 10
TILES = 4
LANES = 128
SLOTS = 16
CHIP = ("x", "z", "y")
EPSILON = 1e-06


def basis_table(length):
    positions = np.arange(length)
    wavenumber = np.concatenate([np.arange(MODES), np.arange(MODES) + 1])
    phases = positions[:, None] * wavenumber[None, :] % length
    angles = phases * (2.0 * np.pi / length)
    column = np.arange(WAVES)
    weights = np.where(column == 0, np.sqrt(1.0 / length), np.sqrt(2.0 / length))
    return np.where(column[None, :] < MODES, np.cos(angles), np.sin(angles)) * weights[None, :]


def split_table(length, parts):
    table = basis_table(length).astype(np.float32)
    high = table.astype(ml_dtypes.bfloat16)
    low = (table - high.astype(np.float32)).astype(ml_dtypes.bfloat16)
    shape = (parts, length // parts, WAVES)
    return high.reshape(shape), low.reshape(shape)


def split(value):
    high = value.astype(jnp.bfloat16)
    low = (value - high.astype(jnp.float32)).astype(jnp.bfloat16)
    return high, low


def dot(left, right, contract):
    return lax.dot_general(left, right, (contract, ((), ())), preferred_element_type=jnp.float32)


def analysis_kernel(
    model_hbm, driver_hbm, rows_hbm, columns_hbm, mine, other, model,
    driver, rows, columns, along_y, squares, arrived, ready,
):
    gy, gx, core = lax.axis_index(("x", "c")), lax.axis_index(("z", "y")), lax.axis_index("c")
    groups = model.shape[0] // GROUP
    tables = [
        pltpu.make_async_copy(rows_hbm.at[gy], rows, ready.at[0]),
        pltpu.make_async_copy(columns_hbm.at[gx], columns, ready.at[1]),
    ]

    def chunks(group):
        span = pl.ds(group * GROUP, GROUP)
        return [
            pltpu.make_async_copy(model_hbm.at[span], model.at[span], arrived.at[0, group]),
            pltpu.make_async_copy(driver_hbm.at[span], driver.at[span], arrived.at[1, group]),
        ]

    for copy in tables:
        copy.start()
    for group in range(groups):
        for copy in chunks(group):
            copy.start()
    along_y[...] = jnp.zeros_like(along_y)
    squares[...] = jnp.zeros_like(squares)
    for copy in tables:
        copy.wait()

    def one_group(group, carry):
        for copy in chunks(group):
            copy.wait()
        for i in range(GROUP):
            field = group * GROUP + i
            difference = driver[field] - model[field]
            squares[i : i + 1, :] = jnp.sum(difference * difference, axis=0, keepdims=True)
            parts = jnp.concatenate(split(difference), axis=1)
            product = dot(rows[...], parts, ((1,), (0,)))
            product = product[:WAVES] + product[WAVES:]
            high, low = split(product[:, :LANES] + product[:, LANES:])
            along_y[i * WAVES : (i + 1) * WAVES, :LANES] = high
            along_y[i * WAVES : (i + 1) * WAVES, LANES:] = low
        both = dot(columns[...], along_y[...], ((1,), (1,)))
        both = both[:WAVES] + both[WAVES:]
        tiles = [both[:, t * LANES : (t + 1) * LANES] for t in range(TILES)]
        total = jnp.sum(squares[...], axis=1, keepdims=True)
        lane = lax.broadcasted_iota(jnp.int32, (SLOTS, LANES), 1)
        top = jnp.where(lane == LANES - 1, total, tiles[-1][:SLOTS])
        tiles[-1] = jnp.concatenate([top, tiles[-1][SLOTS:]], axis=0)
        first = pl.multiple_of((group % (groups // 2)) * (TILES * WAVES), 8)

        def keep(ref):
            for t in range(TILES):
                ref[pl.ds(first + t * WAVES, WAVES), :] = tiles[t]

        half = group // (groups // 2)
        pl.when(half == core)(lambda: keep(mine))
        pl.when(half != core)(lambda: keep(other))
        return carry

    lax.fori_loop(0, groups, one_group, 0)


def synthesis_kernel(
    cells, own, sibling, rate, cap, model, rows_hbm, columns_hbm, nudged_hbm,
    nudged, rows, columns, along_x, spread, leaving, ready,
):
    gy, gx, core = lax.axis_index(("x", "c")), lax.axis_index(("z", "y")), lax.axis_index("c")
    groups = model.shape[0] // GROUP
    tables = [
        pltpu.make_async_copy(rows_hbm.at[gy], rows, ready.at[0]),
        pltpu.make_async_copy(columns_hbm.at[gx], columns, ready.at[1]),
    ]

    def ordered(step):
        return lax.rem(step + core * (groups // 2), groups)

    def chunk_out(group):
        span = pl.ds(group * GROUP, GROUP)
        return pltpu.make_async_copy(nudged.at[span], nudged_hbm.at[span], leaving.at[group])

    for copy in tables:
        copy.start()
    for copy in tables:
        copy.wait()

    def one_group(step, carry):
        group = ordered(step)

        def prepare(ref):
            first = pl.multiple_of((step % (groups // 2)) * (TILES * WAVES), 8)
            tiles = [ref[pl.ds(first + t * WAVES, WAVES), :] for t in range(TILES)]
            total = tiles[-1][:SLOTS, LANES - 1 :]
            spread[...] = jnp.broadcast_to(jnp.sqrt(total / cells + EPSILON), spread.shape)
            high, low = split(jnp.concatenate(tiles, axis=1))
            both = dot(high, columns[...], ((0,), (0,))) + dot(low, columns[...], ((0,), (0,)))
            along_x[...] = both[:, :LANES] + both[:, LANES:]

        pl.when(step < groups // 2)(lambda: prepare(own))
        pl.when(step >= groups // 2)(lambda: prepare(sibling))
        for i in range(0, GROUP, 2):
            stacks = []
            for j in (i, i + 1):
                field = group * GROUP + j
                strength = rate[field] * jnp.minimum(1.0, cap[field] / spread[j : j + 1, :])
                high, low = split(along_x[j * WAVES : (j + 1) * WAVES, :] * strength)
                stacks.append(jnp.concatenate([high, low, high], axis=0))
            pair = dot(rows[...], jnp.concatenate(stacks, axis=1), ((1,), (0,)))
            for j in (0, 1):
                field = group * GROUP + i + j
                nudged[field] = model[field] + pair[:, j * LANES : (j + 1) * LANES]
        chunk_out(group).start()
        return carry

    lax.fori_loop(0, groups, one_group, 0)
    for group in range(groups):
        chunk_out(group).wait()


IN_HBM = pl.BlockSpec(memory_space=pltpu.HBM)
IN_VMEM = pl.BlockSpec(memory_space=pltpu.VMEM)
IN_SMEM = pl.BlockSpec(memory_space=pltpu.SMEM)


def share_kernel(chips, pieces, copies, rows):
    height = pieces.shape[0] // chips
    period = 8 * height
    total = pieces[:period, :]
    for first in range(period, pieces.shape[0], period):
        total = total + pieces[first : first + period, :]
    rows[...] = total
    for i in range(height):
        every = pl.ds(i, 8, stride=height)
        line = jnp.sum(rows[every, :], axis=0, keepdims=True)
        rows[every, :] = jnp.broadcast_to(line, (8, LANES))
    for first in range(0, pieces.shape[0], period):
        copies[first : first + period, :] = rows[...]


def share(pieces, chips):
    return pl.pallas_call(
        lambda *refs: share_kernel(chips, *refs),
        out_shape=pltpu.VMEM(pieces.shape, jnp.float32),
        in_specs=[IN_VMEM],
        out_specs=IN_VMEM,
        scratch_shapes=[pltpu.VMEM((8 * pieces.shape[0] // chips, LANES), jnp.float32)],
        compiler_params=pltpu.CompilerParams(vmem_limit_bytes=2 << 20),
        name="share",
    )(kept_in_vmem(pieces))


def kept_in_hbm(value):
    return pltpu.with_memory_space_constraint(value, pltpu.HBM)


def kept_in_vmem(value):
    return pltpu.with_memory_space_constraint(value, pltpu.VMEM)


def analysis(model, driver, rows, columns):
    groups = model.shape[0] // GROUP
    half = groups // 2 * TILES * WAVES
    return pl.pallas_call(
        analysis_kernel,
        out_shape=[
            pltpu.VMEM((half, LANES), jnp.float32),
            pltpu.VMEM((half, LANES), jnp.float32),
            pltpu.VMEM(model.shape, jnp.float32),
        ],
        in_specs=[IN_HBM] * 4,
        out_specs=[IN_VMEM] * 3,
        scratch_shapes=[
            pltpu.VMEM(model.shape, jnp.float32),
            pltpu.VMEM(rows.shape[1:], jnp.bfloat16),
            pltpu.VMEM(columns.shape[1:], jnp.bfloat16),
            pltpu.VMEM((TILES * LANES, 2 * LANES), jnp.bfloat16),
            pltpu.VMEM((SLOTS, LANES), jnp.float32),
            pltpu.SemaphoreType.DMA((2, groups)),
            pltpu.SemaphoreType.DMA((2,)),
        ],
        compiler_params=pltpu.CompilerParams(vmem_limit_bytes=24 << 20),
        name="analysis",
    )(*map(kept_in_hbm, (model, driver, rows, columns)))


def synthesis(model, own, sibling, rate, cap, rows, columns, cells):
    groups = model.shape[0] // GROUP
    return pl.pallas_call(
        lambda *refs: synthesis_kernel(cells, *refs),
        out_shape=pltpu.HBM(model.shape, jnp.float32),
        in_specs=[IN_VMEM] * 2 + [IN_SMEM] * 2 + [IN_VMEM] + [IN_HBM] * 2,
        out_specs=IN_HBM,
        scratch_shapes=[
            pltpu.VMEM(model.shape, jnp.float32),
            pltpu.VMEM(rows.shape[1:], jnp.bfloat16),
            pltpu.VMEM(columns.shape[1:], jnp.bfloat16),
            pltpu.VMEM((TILES * LANES, LANES), jnp.float32),
            pltpu.VMEM((SLOTS, LANES), jnp.float32),
            pltpu.SemaphoreType.DMA((groups,)),
            pltpu.SemaphoreType.DMA((2,)),
        ],
        compiler_params=pltpu.CompilerParams(vmem_limit_bytes=24 << 20),
        name="synthesis",
    )(
        kept_in_vmem(own),
        kept_in_vmem(sibling),
        rate,
        cap,
        kept_in_vmem(model),
        kept_in_hbm(rows),
        kept_in_hbm(columns),
    )


def per_device(model_field, driver_field, nudge_rate, increment_cap):
    fields, height, width = model_field.shape
    parts_y = lax.axis_size(("x", "c"))
    parts_x = lax.axis_size(("z", "y"))
    chips = lax.axis_size(CHIP)
    swap = [(0, 1), (1, 0)]

    high_y, low_y = split_table(height * parts_y, parts_y)
    high_x, low_x = split_table(width * parts_x, parts_x)
    turned = lambda table: np.swapaxes(table, 1, 2)
    rows_in = np.concatenate([turned(high_y), turned(low_y)], axis=1)
    columns_in = np.concatenate([turned(high_x), turned(low_x)], axis=1)
    columns_in = np.concatenate([columns_in, columns_in], axis=2)
    rows_out = np.concatenate([high_y, high_y, low_y], axis=2)
    columns_out = np.concatenate([turned(high_x), turned(low_x)], axis=2)

    mine, other, model_kept = analysis(model_field, driver_field, rows_in, columns_in)
    pair = mine + lax.ppermute(other, "c", swap)

    def exchanged(value):
        blocks = value.reshape(chips, 1, -1)
        return lax.all_to_all(blocks, CHIP, 0, 0, tiled=True).reshape(value.shape)

    own = exchanged(share(exchanged(pair), chips))
    sibling = lax.ppermute(own, "c", swap)
    cells = height * parts_y * width * parts_x
    return synthesis(
        model_kept,
        own,
        sibling,
        nudge_rate,
        increment_cap,
        rows_out,
        columns_out,
        float(cells),
    )


def solution(mesh):
    finer = Mesh(mesh.devices.reshape(4, 2, 4, 4), ("x", "c", "z", "y"))
    field = P(None, ("x", "c"), ("z", "y"))
    return jax.shard_map(
        per_device,
        mesh=finer,
        in_specs=(field, field, P(), P()),
        out_specs=field,
        check_vma=False,
    )
```

time: 73.8 us -> 58.7 us (0.80)
  Pallas kernels: 27.7 us -> 16.4 us
  local copies, waits for them, and re-layouts: 1.76 us -> 0.01 us
  other arithmetic: 1.76 us -> 0.04 us
    pallas_call x2 -> x3, Pallas kernels: 27.7 us -> 16.4 us  [the longest x1 9.59 us: analysis(): pl.pallas_call(analysis_kernel, out_shape=[pltpu.VMEM((half, LANES), jnp....]
    broadcast_in_dim x5 -> x0, local copies, waits for them, and re-layouts: 1.59 us -> none  [the longest x4 1.44 us: per_group(): return jnp.broadcast_to(rows, (rows.shape[0], SLOTS, LANES))]
    add x1, other arithmetic: 1.01 us -> 0.04 us  [per_device(): pair = mine + lax.ppermute(other, 'c', swap)]
where the time goes in v2:
time: 58.7 us; the launch traced here: 58.5 us
  blocking collectives  34.9 us (59%)
  Pallas kernels  16.4 us (28%)
  starting transfers between devices  4.66 us (8%)
  waiting for transfers between devices  2.42 us (4%)
    all_to_all x2, blocking collectives, exchanged(): return lax.all_to_all(blocks, CHIP, 0, 0, tiled=True).reshape(value.shape)  34.9 us
    pallas_call x1, Pallas kernels, analysis(): pl.pallas_call(analysis_kernel, out_shape=[pltpu.VMEM((half, LANES), jnp....  9.59 us
    pallas_call x1, Pallas kernels, synthesis(): pl.pallas_call(lambda *refs: synthesis_kernel(cells, *refs), out_shape=pl...  6.78 us
    ppermute x1, starting transfers between devices, per_device(): sibling = lax.ppermute(own, 'c', swap)  3.17 us
    ppermute x1, starting transfers between devices, per_device(): pair = mine + lax.ppermute(other, 'c', swap)  1.49 us
    ppermute x1, waiting for transfers between devices, per_device(): pair = mine + lax.ppermute(other, 'c', swap)  1.21 us
    ppermute x1, waiting for transfers between devices, per_device(): sibling = lax.ppermute(own, 'c', swap)  1.21 us
  transfers between devices with their start and end apart: 2, of which 2 were waited for; matrix products, arithmetic and copies ran while one was open for 0% of the time, Pallas kernels for 0%

profile of v2, /device:TPU:1, one launch (start us, length us, event | category | flops | bytes accessed | tf_op | source)
XLA Modules:
  0.0 58.5 jit_solution(707916467445911908)
XLA Ops:
  0.0 0.0 copy-start.1
  0.0 0.0 copy-start
  0.0 9.6 %analysis.1 = (f32[576,128]{1,0:T(8,128)S(1)}, f32[576,128]{1,0:T(8,128)S(1)}, f32[60,256,128]{2,1,0:T(8,128)S(1)}) custom-call(f32[60,256,128]{2,1,0:T(8,128)} %model_hbm.1, f32[60,256,128]{2,1,0:T(8,128)} %driver_hbm.1, bf16[8,96,256]{2,1,0:T(8,128)(2,1)} %constant.8.clone.rows_hbm, bf16[16,96,256]{2,1,0:T(8,128)(2,1)} %constant.9.clone.columns_hbm), custom_call_target="tpu_custom_call" | custom-call | tf_op jit(solution)/shard_map/analysis/pallas_call | solution.py:211
  9.6 1.5 %collective-permute-start = (f32[576,128]{1,0:T(8,128)S(1)}, f32[576,128]{1,0:T(8,128)S(1)}, u32[]{:S(2)}, u32[]{:S(2)}) collective-permute-start(f32[576,128]{1,0:T(8,128)S(1)} %get-tuple-element.9), channel_id=1, source_target_pairs={{0,16},{16,0},{1,17},{17,1},{2,18},{18,2},{3,19},{19,3},{4,20},{20... | collective-permute-start | bytes 884744 | tf_op jit(solution)/shard_map/ppermute | solution.py:280
  11.1 1.2 %collective-permute-done = f32[576,128]{1,0:T(8,128)S(1)} collective-permute-done((f32[576,128]{1,0:T(8,128)S(1)}, f32[576,128]{1,0:T(8,128)S(1)}, u32[]{:S(2)}, u32[]{:S(2)}) %collective-permute-start) | collective-permute-done | bytes 294944 | tf_op jit(solution)/shard_map/ppermute | solution.py:280
  12.3 20.9 %all_to_all.10 = f32[64,1,1152]{2,1,0:T(1,128)S(1)} all-to-all(f32[64,1,1152]{2,1,0:T(1,128)S(1)} %bitcast.8), channel_id=1, replica_groups=mesh['x'=4,'c'=2,'z'=4,'y'=4] {'x','z','y'}, dimensions={0} | all-to-all | bytes 589824 | tf_op jit(solution)/shard_map/all_to_all | solution.py:284
  33.3 0.1 share.1
  33.3 14.0 %all_to_all.11 = f32[64,1,1152]{2,1,0:T(1,128)S(1)} all-to-all(f32[64,1,1152]{2,1,0:T(1,128)S(1)} %bitcast.5), channel_id=1, replica_groups=mesh['x'=4,'c'=2,'z'=4,'y'=4] {'x','z','y'}, dimensions={0} | all-to-all | bytes 589824 | tf_op jit(solution)/shard_map/all_to_all | solution.py:284
  47.3 3.2 %collective-permute-start.1 = (f32[576,128]{1,0:T(8,128)S(1)}, f32[576,128]{1,0:T(8,128)S(1)}, u32[]{:S(2)}, u32[]{:S(2)}) collective-permute-start(f32[576,128]{1,0:T(8,128)S(1)} %bitcast.6), channel_id=1, source_target_pairs={{0,16},{16,0},{1,17},{17,1},{2,18},{18,2},{3,19},{19,3},{4,20},{20... | collective-permute-start | bytes 884744 | tf_op jit(solution)/shard_map/ppermute | solution.py:287
  50.5 1.2 %collective-permute-done.1.refs_1_ = f32[576,128]{1,0:T(8,128)S(1)} collective-permute-done((f32[576,128]{1,0:T(8,128)S(1)}, f32[576,128]{1,0:T(8,128)S(1)}, u32[]{:S(2)}, u32[]{:S(2)}) %collective-permute-start.1) | collective-permute-done | bytes 294944 | tf_op jit(solution)/shard_map/ppermute | solution.py:287
  51.7 0.0 copy-done.1
  51.7 0.0 copy-done
  51.7 6.8 %synthesis.1 = f32[60,256,128]{2,1,0:T(8,128)} custom-call(f32[576,128]{1,0:T(8,128)S(1)} %bitcast.7, f32[576,128]{1,0:T(8,128)S(1)} %collective-permute-done.1.refs_1_, f32[60]{0:T(128)S(1)} %copy-done, f32[60]{0:T(128)S(1)} %copy-done.1, f32[60,256,128]{2,1,0:T(8,128)S(1)} %get-tuple-element.10.refs_4_, bf16[8,256,144]{2,1,0:T(8,128)(2,1)} %constant.10.clone.refs_5_, ...), custom_call_target="tpu_custom_call" | custom-call | tf_op jit(solution)/shard_map/synthesis/pallas_call | solution.py:236
  (1 shorter events, 0.0 us)
Async XLA Ops:
  0.0 51.7 %copy-start.1 = (f32[60]{0:T(128)S(1)}, f32[60]{0:T(128)}, u32[]{:S(2)}) copy-start(f32[60]{0:T(128)} %refs_3_.1) | copy-start | bytes 724
  0.0 51.7 %copy-start = (f32[60]{0:T(128)S(1)}, f32[60]{0:T(128)}, u32[]{:S(2)}) copy-start(f32[60]{0:T(128)} %refs_2_.1) | copy-start | bytes 724
  9.6 2.7 %collective-permute-start = (f32[576,128]{1,0:T(8,128)S(1)}, f32[576,128]{1,0:T(8,128)S(1)}, u32[]{:S(2)}, u32[]{:S(2)}) collective-permute-start(f32[576,128]{1,0:T(8,128)S(1)} %get-tuple-element.9), channel_id=1, source_target_pairs={{0,16},{16,0},{1,17},{17,1},{2,18},{18,2},{3,19},{19,3},{4,20},{20... | collective-permute-start | bytes 884744 | tf_op jit(solution)/shard_map/ppermute | solution.py:280
  47.3 4.4 %collective-permute-start.1 = (f32[576,128]{1,0:T(8,128)S(1)}, f32[576,128]{1,0:T(8,128)S(1)}, u32[]{:S(2)}, u32[]{:S(2)}) collective-permute-start(f32[576,128]{1,0:T(8,128)S(1)} %bitcast.6), channel_id=1, source_target_pairs={{0,16},{16,0},{1,17},{17,1},{2,18},{18,2},{3,19},{19,3},{4,20},{20... | collective-permute-start | bytes 884744 | tf_op jit(solution)/shard_map/ppermute | solution.py:287

commit v3 on v2

v3 whole, which is shorter than its diff:
```python
import numpy as np

import jax
import jax.numpy as jnp
import ml_dtypes
from jax import lax
from jax.experimental import pallas as pl
from jax.experimental.pallas import tpu as pltpu
from jax.sharding import Mesh
from jax.sharding import PartitionSpec as P

MODES = 24
WAVES = 2 * MODES
GROUP = 10
TILES = 4
LANES = 128
AHEAD = 3
LAST_PIECES = (6, 4)
CHUNK = 10
SLOTS = 16
CHIP = ("x", "z", "y")
EPSILON = 1e-06


def basis_table(length):
    positions = np.arange(length)
    wavenumber = np.concatenate([np.arange(MODES), np.arange(MODES) + 1])
    phases = positions[:, None] * wavenumber[None, :] % length
    angles = phases * (2.0 * np.pi / length)
    column = np.arange(WAVES)
    weights = np.where(column == 0, np.sqrt(1.0 / length), np.sqrt(2.0 / length))
    return np.where(column[None, :] < MODES, np.cos(angles), np.sin(angles)) * weights[None, :]


def split_table(length, parts):
    table = basis_table(length).astype(np.float32)
    high = table.astype(ml_dtypes.bfloat16)
    low = (table - high.astype(np.float32)).astype(ml_dtypes.bfloat16)
    shape = (parts, length // parts, WAVES)
    return high.reshape(shape), low.reshape(shape)


def split(value):
    high = value.astype(jnp.bfloat16)
    low = (value - high.astype(jnp.float32)).astype(jnp.bfloat16)
    return high, low


def dot(left, right, contract):
    return lax.dot_general(left, right, (contract, ((), ())), preferred_element_type=jnp.float32)


def analysis_kernel(
    model_hbm, driver_hbm, rate_hbm, cap_hbm, rows_hbm, columns_hbm, rows_out_hbm, columns_out_hbm,
    mine, other, model, rate_rows, cap_rows, rows_out, columns_out,
    driver, rate, cap, rows, columns, along_y, squares, arrived, ready,
):
    gy, gx, core = lax.axis_index(("x", "c")), lax.axis_index(("z", "y")), lax.axis_index("c")
    groups = model.shape[0] // GROUP
    tables = [
        pltpu.make_async_copy(rows_hbm.at[gy], rows, ready.at[0]),
        pltpu.make_async_copy(columns_hbm.at[gx], columns, ready.at[1]),
    ]
    later = [
        pltpu.make_async_copy(rate_hbm, rate, ready.at[2]),
        pltpu.make_async_copy(cap_hbm, cap, ready.at[3]),
        pltpu.make_async_copy(rows_out_hbm.at[gy], rows_out, ready.at[4]),
        pltpu.make_async_copy(columns_out_hbm.at[gx], columns_out, ready.at[5]),
    ]

    def ordered(step):
        return lax.rem(step + (1 - core) * (groups // 2), groups)

    pieces = []
    for step in range(groups):
        sizes = LAST_PIECES if step == groups - 1 else (GROUP,)
        first = 0
        for size in sizes:
            pieces.append((step, first, size))
            first += size

    def fetch(piece):
        step, first, size = pieces[piece]
        span = pl.ds(ordered(step) * GROUP + first, size)
        return [
            pltpu.make_async_copy(model_hbm.at[span], model.at[span], arrived.at[0, piece]),
            pltpu.make_async_copy(driver_hbm.at[span], driver.at[span], arrived.at[1, piece]),
        ]

    for copy in tables + fetch(0) + later:
        copy.start()
    for piece in range(1, AHEAD):
        for copy in fetch(piece):
            copy.start()
    along_y[...] = jnp.zeros_like(along_y)
    squares[...] = jnp.zeros_like(squares)

    def first_contraction(step, i):
        field = ordered(step) * GROUP + i
        difference = driver[field] - model[field]
        folded = (difference * difference).reshape(-1, 8, LANES)
        squares[step % 2, i * 8 : i * 8 + 8, :] = jnp.sum(folded, axis=0)
        parts = jnp.concatenate(split(difference), axis=1)
        product = dot(rows[...], parts, ((1,), (0,)))
        product = product[:WAVES] + product[WAVES:]
        high, low = split(product[:, :LANES] + product[:, LANES:])
        along_y[step % 2, i * WAVES : (i + 1) * WAVES, :LANES] = high
        along_y[step % 2, i * WAVES : (i + 1) * WAVES, LANES:] = low

    def second_contraction(step):
        both = dot(columns[...], along_y[step % 2], ((1,), (1,)))
        both = both[:WAVES] + both[WAVES:]
        total = squares[step % 2, pl.ds(0, SLOTS, stride=8), :]
        for s in range(1, 8):
            total = total + squares[step % 2, pl.ds(s, SLOTS, stride=8), :]
        total = jnp.sum(total, axis=1, keepdims=True)
        tiles = [both[:, t * LANES : (t + 1) * LANES] for t in range(TILES)]
        lane = lax.broadcasted_iota(jnp.int32, (SLOTS, LANES), 1)
        top = jnp.where(lane == LANES - 1, total, tiles[-1][:SLOTS])
        tiles[-1] = jnp.concatenate([top, tiles[-1][SLOTS:]], axis=0)
        kept = other if step < groups // 2 else mine
        first = step % (groups // 2) * TILES * WAVES
        for t in range(TILES):
            kept[first + t * WAVES : first + (t + 1) * WAVES, :] = tiles[t]

    for piece, (step, first, size) in enumerate(pieces):
        if piece == 0:
            for copy in tables:
                copy.wait()
        for copy in fetch(piece):
            copy.wait()
        if piece + AHEAD < len(pieces):
            for copy in fetch(piece + AHEAD):
                copy.start()
        for i in range(first, first + size):
            first_contraction(step, i)
            if i == 2 and step > 0:
                second_contraction(step - 1)
        if step == 1:
            for copy in later:
                copy.wait()
            for field in range(model.shape[0]):
                place = field // GROUP * SLOTS + field % GROUP
                rate_rows[place : place + 1, :] = jnp.full((1, LANES), rate[field])
                cap_rows[place : place + 1, :] = jnp.full((1, LANES), cap[field])
    second_contraction(groups - 1)


def synthesis_kernel(
    cells, own, sibling, rate_rows, cap_rows, model, rows, columns, nudged_hbm,
    nudged, along_x, strength, leaving,
):
    core = lax.axis_index("c")
    groups = model.shape[0] // GROUP

    def ordered(step):
        return lax.rem(step + core * (groups // 2), groups)

    def chunk_out(step, first, size):
        span = pl.ds(ordered(step) * GROUP + first, size)
        place = leaving.at[step * (GROUP // CHUNK) + first // CHUNK]
        return pltpu.make_async_copy(nudged.at[span], nudged_hbm.at[span], place)

    def prepare(step):
        ref = own if step < groups // 2 else sibling
        first = step % (groups // 2) * TILES * WAVES
        tiles = [ref[first + t * WAVES : first + (t + 1) * WAVES, :] for t in range(TILES)]
        limits = pl.ds(pl.multiple_of(ordered(step) * SLOTS, SLOTS), SLOTS)
        spread = jnp.sqrt(tiles[-1][:SLOTS, LANES - 1 :] / cells + EPSILON)
        strength[step % 2] = rate_rows[limits, :] * jnp.minimum(1.0, cap_rows[limits, :] / spread)
        high, low = split(jnp.concatenate(tiles, axis=1))
        both = dot(high, columns[...], ((0,), (0,))) + dot(low, columns[...], ((0,), (0,)))
        along_x[step % 2] = both[:, :LANES] + both[:, LANES:]

    prepare(0)
    for step in range(groups):
        for i in range(0, GROUP, 2):
            stacks = []
            for j in (i, i + 1):
                scaled = along_x[step % 2, j * WAVES : (j + 1) * WAVES, :]
                high, low = split(scaled * strength[step % 2, j : j + 1, :])
                stacks.append(jnp.concatenate([high, low, high], axis=0))
            pair = dot(rows[...], jnp.concatenate(stacks, axis=1), ((1,), (0,)))
            for j in (0, 1):
                field = ordered(step) * GROUP + i + j
                nudged[field] = model[field] + pair[:, j * LANES : (j + 1) * LANES]
            if i == 0 and step + 1 < groups:
                prepare(step + 1)
            if (i + 2) % CHUNK == 0:
                chunk_out(step, i + 2 - CHUNK, CHUNK).start()
    for step in range(groups):
        for first in range(0, GROUP, CHUNK):
            chunk_out(step, first, CHUNK).wait()


IN_HBM = pl.BlockSpec(memory_space=pltpu.HBM)
IN_VMEM = pl.BlockSpec(memory_space=pltpu.VMEM)
IN_SMEM = pl.BlockSpec(memory_space=pltpu.SMEM)


def share_kernel(chips, pieces, copies, rows):
    height = pieces.shape[0] // chips
    period = 8 * height
    total = pieces[:period, :]
    for first in range(period, pieces.shape[0], period):
        total = total + pieces[first : first + period, :]
    rows[...] = total
    for i in range(height):
        every = pl.ds(i, 8, stride=height)
        line = jnp.sum(rows[every, :], axis=0, keepdims=True)
        rows[every, :] = jnp.broadcast_to(line, (8, LANES))
    for first in range(0, pieces.shape[0], period):
        copies[first : first + period, :] = rows[...]


def share(pieces, chips):
    return pl.pallas_call(
        lambda *refs: share_kernel(chips, *refs),
        out_shape=pltpu.VMEM(pieces.shape, jnp.float32),
        in_specs=[IN_VMEM],
        out_specs=IN_VMEM,
        scratch_shapes=[pltpu.VMEM((8 * pieces.shape[0] // chips, LANES), jnp.float32)],
        compiler_params=pltpu.CompilerParams(vmem_limit_bytes=2 << 20),
        name="share",
    )(kept_in_vmem(pieces))


def kept_in_hbm(value):
    return pltpu.with_memory_space_constraint(value, pltpu.HBM)


def kept_in_vmem(value):
    return pltpu.with_memory_space_constraint(value, pltpu.VMEM)


def analysis(model, driver, rate, cap, rows, columns, rows_out, columns_out):
    groups = model.shape[0] // GROUP
    half = groups // 2 * TILES * WAVES
    pieces = groups - 1 + len(LAST_PIECES)
    return pl.pallas_call(
        analysis_kernel,
        out_shape=[
            pltpu.VMEM((half, LANES), jnp.float32),
            pltpu.VMEM((half, LANES), jnp.float32),
            pltpu.VMEM(model.shape, jnp.float32),
            pltpu.VMEM((groups * SLOTS, LANES), jnp.float32),
            pltpu.VMEM((groups * SLOTS, LANES), jnp.float32),
            pltpu.VMEM(rows_out.shape[1:], jnp.bfloat16),
            pltpu.VMEM(columns_out.shape[1:], jnp.bfloat16),
        ],
        in_specs=[IN_HBM] * 8,
        out_specs=[IN_VMEM] * 7,
        scratch_shapes=[
            pltpu.VMEM(model.shape, jnp.float32),
            pltpu.SMEM(rate.shape, jnp.float32),
            pltpu.SMEM(cap.shape, jnp.float32),
            pltpu.VMEM(rows.shape[1:], jnp.bfloat16),
            pltpu.VMEM(columns.shape[1:], jnp.bfloat16),
            pltpu.VMEM((2, TILES * LANES, 2 * LANES), jnp.bfloat16),
            pltpu.VMEM((2, 8 * SLOTS, LANES), jnp.float32),
            pltpu.SemaphoreType.DMA((2, pieces)),
            pltpu.SemaphoreType.DMA((6,)),
        ],
        compiler_params=pltpu.CompilerParams(vmem_limit_bytes=24 << 20),
        name="analysis",
    )(*map(kept_in_hbm, (model, driver, rate, cap, rows, columns, rows_out, columns_out)))


def synthesis(own, sibling, rate_rows, cap_rows, model, rows, columns, cells):
    groups = model.shape[0] // GROUP
    return pl.pallas_call(
        lambda *refs: synthesis_kernel(cells, *refs),
        out_shape=pltpu.HBM(model.shape, jnp.float32),
        in_specs=[IN_VMEM] * 7,
        out_specs=IN_HBM,
        scratch_shapes=[
            pltpu.VMEM(model.shape, jnp.float32),
            pltpu.VMEM((2, TILES * LANES, LANES), jnp.float32),
            pltpu.VMEM((2, SLOTS, LANES), jnp.float32),
            pltpu.SemaphoreType.DMA((groups * (GROUP // CHUNK),)),
        ],
        compiler_params=pltpu.CompilerParams(vmem_limit_bytes=24 << 20),
        name="synthesis",
    )(*map(kept_in_vmem, (own, sibling, rate_rows, cap_rows, model, rows, columns)))


def per_device(model_field, driver_field, nudge_rate, increment_cap):
    fields, height, width = model_field.shape
    parts_y = lax.axis_size(("x", "c"))
    parts_x = lax.axis_size(("z", "y"))
    chips = lax.axis_size(CHIP)
    swap = [(0, 1), (1, 0)]

    high_y, low_y = split_table(height * parts_y, parts_y)
    high_x, low_x = split_table(width * parts_x, parts_x)
    turned = lambda table: np.swapaxes(table, 1, 2)
    rows_in = np.concatenate([turned(high_y), turned(low_y)], axis=1)
    columns_in = np.concatenate([turned(high_x), turned(low_x)], axis=1)
    columns_in = np.concatenate([columns_in, columns_in], axis=2)
    rows_out = np.concatenate([high_y, high_y, low_y], axis=2)
    columns_out = np.concatenate([turned(high_x), turned(low_x)], axis=2)

    mine, other, *kept = analysis(
        model_field,
        driver_field,
        nudge_rate,
        increment_cap,
        rows_in,
        columns_in,
        rows_out,
        columns_out,
    )
    model_kept, rate_rows, cap_rows, rows_kept, columns_kept = kept
    pair = mine + lax.ppermute(other, "c", swap)

    def exchanged(value):
        blocks = value.reshape(chips, 1, -1)
        return lax.all_to_all(blocks, CHIP, 0, 0, tiled=True).reshape(value.shape)

    own = exchanged(share(exchanged(pair), chips))
    sibling = lax.ppermute(own, "c", swap)
    cells = float(height * parts_y * width * parts_x)
    return synthesis(
        own, sibling, rate_rows, cap_rows, model_kept, rows_kept, columns_kept, cells
    )


def solution(mesh):
    finer = Mesh(mesh.devices.reshape(4, 2, 4, 4), ("x", "c", "z", "y"))
    field = P(None, ("x", "c"), ("z", "y"))
    return jax.shard_map(
        per_device,
        mesh=finer,
        in_specs=(field, field, P(), P()),
        out_specs=field,
        check_vma=False,
    )
```

time: 58.7 us -> 53.1 us (0.905)
  Pallas kernels: 16.4 us -> 10.8 us
    pallas_call x1, Pallas kernels: 9.59 us -> 6.6 us  [analysis(): pl.pallas_call(analysis_kernel, out_shape=[pltpu.VMEM((half, LANES), jnp....]
    pallas_call x1, Pallas kernels: 6.78 us -> 4.17 us  [synthesis(): pl.pallas_call(lambda *refs: synthesis_kernel(cells, *refs), out_shape=pl...]
where the time goes in v3:
time: 53.1 us; the launch traced here: 52.9 us
  blocking collectives  34.9 us (66%)
  Pallas kernels  10.8 us (20%)
  starting transfers between devices  4.67 us (9%)
  waiting for transfers between devices  2.42 us (5%)
    all_to_all x2, blocking collectives, exchanged(): return lax.all_to_all(blocks, CHIP, 0, 0, tiled=True).reshape(value.shape)  34.9 us
    pallas_call x1, Pallas kernels, analysis(): pl.pallas_call(analysis_kernel, out_shape=[pltpu.VMEM((half, LANES), jnp....  6.6 us
    pallas_call x1, Pallas kernels, synthesis(): pl.pallas_call(lambda *refs: synthesis_kernel(cells, *refs), out_shape=pl...  4.17 us
    ppermute x1, starting transfers between devices, per_device(): sibling = lax.ppermute(own, 'c', swap)  3.17 us
    ppermute x1, starting transfers between devices, per_device(): pair = mine + lax.ppermute(other, 'c', swap)  1.5 us
    ppermute x1, waiting for transfers between devices, per_device(): sibling = lax.ppermute(own, 'c', swap)  1.21 us
    ppermute x1, waiting for transfers between devices, per_device(): pair = mine + lax.ppermute(other, 'c', swap)  1.21 us
  transfers between devices with their start and end apart: 2, of which 2 were waited for; matrix products, arithmetic and copies ran while one was open for 0% of the time, Pallas kernels for 0%

profile of v3, /device:TPU:1, one launch (start us, length us, event | category | flops | bytes accessed | tf_op | source)
XLA Modules:
  0.0 52.9 jit_solution(15834711584777688175)
XLA Ops:
  0.0 6.6 %analysis.1 = (f32[576,128]{1,0:T(8,128)S(1)}, f32[576,128]{1,0:T(8,128)S(1)}, f32[60,256,128]{2,1,0:T(8,128)S(1)}, f32[96,128]{1,0:T(8,128)S(1)}, f32[96,128]{1...) custom-call(f32[60,256,128]{2,1,0:T(8,128)} %model_hbm.1, f32[60,256,128]{2,1,0:T(8,128)} %driver_hbm.1, ...), custom_call_target="tpu_custom_call" | custom-call | tf_op jit(solution)/shard_map/analysis/pallas_call | solution.py:240
  6.6 1.5 %collective-permute-start = (f32[576,128]{1,0:T(8,128)S(1)}, f32[576,128]{1,0:T(8,128)S(1)}, u32[]{:S(2)}, u32[]{:S(2)}) collective-permute-start(f32[576,128]{1,0:T(8,128)S(1)} %get-tuple-element.13), channel_id=1, source_target_pairs={{0,16},{16,0},{1,17},{17,1},{2,18},{18,2},{3,19},{19,3},{4,20},{20... | collective-permute-start | bytes 884744 | tf_op jit(solution)/shard_map/ppermute | solution.py:314
  8.1 1.2 %collective-permute-done = f32[576,128]{1,0:T(8,128)S(1)} collective-permute-done((f32[576,128]{1,0:T(8,128)S(1)}, f32[576,128]{1,0:T(8,128)S(1)}, u32[]{:S(2)}, u32[]{:S(2)}) %collective-permute-start) | collective-permute-done | bytes 294944 | tf_op jit(solution)/shard_map/ppermute | solution.py:314
  9.4 20.9 %all_to_all.10 = f32[64,1,1152]{2,1,0:T(1,128)S(1)} all-to-all(f32[64,1,1152]{2,1,0:T(1,128)S(1)} %bitcast.8), channel_id=1, replica_groups=mesh['x'=4,'c'=2,'z'=4,'y'=4] {'x','z','y'}, dimensions={0} | all-to-all | bytes 589824 | tf_op jit(solution)/shard_map/all_to_all | solution.py:318
  30.3 0.1 share.1
  30.3 14.0 %all_to_all.11 = f32[64,1,1152]{2,1,0:T(1,128)S(1)} all-to-all(f32[64,1,1152]{2,1,0:T(1,128)S(1)} %bitcast.5), channel_id=1, replica_groups=mesh['x'=4,'c'=2,'z'=4,'y'=4] {'x','z','y'}, dimensions={0} | all-to-all | bytes 589824 | tf_op jit(solution)/shard_map/all_to_all | solution.py:318
  44.3 3.2 %collective-permute-start.1 = (f32[576,128]{1,0:T(8,128)S(1)}, f32[576,128]{1,0:T(8,128)S(1)}, u32[]{:S(2)}, u32[]{:S(2)}) collective-permute-start(f32[576,128]{1,0:T(8,128)S(1)} %bitcast.6), channel_id=1, source_target_pairs={{0,16},{16,0},{1,17},{17,1},{2,18},{18,2},{3,19},{19,3},{4,20},{20... | collective-permute-start | bytes 884744 | tf_op jit(solution)/shard_map/ppermute | solution.py:321
  47.5 1.2 %collective-permute-done.1.refs_1_ = f32[576,128]{1,0:T(8,128)S(1)} collective-permute-done((f32[576,128]{1,0:T(8,128)S(1)}, f32[576,128]{1,0:T(8,128)S(1)}, u32[]{:S(2)}, u32[]{:S(2)}) %collective-permute-start.1) | collective-permute-done | bytes 294944 | tf_op jit(solution)/shard_map/ppermute | solution.py:321
  48.7 4.2 %synthesis.1 = f32[60,256,128]{2,1,0:T(8,128)} custom-call(f32[576,128]{1,0:T(8,128)S(1)} %bitcast.7, f32[576,128]{1,0:T(8,128)S(1)} %collective-permute-done.1.refs_1_, f32[96,128]{1,0:T(8,128)S(1)} %get-tuple-element.14.refs_2_, f32[96,128]{1,0:T(8,128)S(1)} %get-tuple-element.15.refs_3_, f32[60,256,128]{2,1,0:T(8,128)S(1)} %get-tuple-element.16.refs_4_, ...), custom_call_target="tpu_custom_call" | custom-call | tf_op jit(solution)/shard_map/synthesis/pallas_call | solution.py:271
  (1 shorter events, 0.0 us)
Async XLA Ops:
  6.6 2.7 %collective-permute-start = (f32[576,128]{1,0:T(8,128)S(1)}, f32[576,128]{1,0:T(8,128)S(1)}, u32[]{:S(2)}, u32[]{:S(2)}) collective-permute-start(f32[576,128]{1,0:T(8,128)S(1)} %get-tuple-element.13), channel_id=1, source_target_pairs={{0,16},{16,0},{1,17},{17,1},{2,18},{18,2},{3,19},{19,3},{4,20},{20... | collective-permute-start | bytes 884744 | tf_op jit(solution)/shard_map/ppermute | solution.py:314
  44.3 4.4 %collective-permute-start.1 = (f32[576,128]{1,0:T(8,128)S(1)}, f32[576,128]{1,0:T(8,128)S(1)}, u32[]{:S(2)}, u32[]{:S(2)}) collective-permute-start(f32[576,128]{1,0:T(8,128)S(1)} %bitcast.6), channel_id=1, source_target_pairs={{0,16},{16,0},{1,17},{17,1},{2,18},{18,2},{3,19},{19,3},{4,20},{20... | collective-permute-start | bytes 884744 | tf_op jit(solution)/shard_map/ppermute | solution.py:321

commit v4 on v3

--- a/solution.py
+++ b/solution.py
@@ -50,13 +50,30 @@
     return lax.dot_general(left, right, (contract, ((), ())), preferred_element_type=jnp.float32)
 
 
+def second_contraction(columns, along_y, squares, coefficients, step):
+    both = dot(columns[...], along_y[...], ((1,), (1,)))
+    both = both[:WAVES] + both[WAVES:]
+    total = squares[pl.ds(0, SLOTS, stride=8), :]
+    for s in range(1, 8):
+        total = total + squares[pl.ds(s, SLOTS, stride=8), :]
+    total = jnp.sum(total, axis=1, keepdims=True)
+    tiles = [both[:, t * LANES : (t + 1) * LANES] for t in range(TILES)]
+    lane = lax.broadcasted_iota(jnp.int32, (SLOTS, LANES), 1)
+    top = jnp.where(lane == LANES - 1, total, tiles[-1][:SLOTS])
+    tiles[-1] = jnp.concatenate([top, tiles[-1][SLOTS:]], axis=0)
+    first = step * TILES * WAVES
+    for t in range(TILES):
+        coefficients[first + t * WAVES : first + (t + 1) * WAVES, :] = tiles[t]
+
+
 def analysis_kernel(
     model_hbm, driver_hbm, rate_hbm, cap_hbm, rows_hbm, columns_hbm, rows_out_hbm, columns_out_hbm,
-    mine, other, model, rate_rows, cap_rows, rows_out, columns_out,
-    driver, rate, cap, rows, columns, along_y, squares, arrived, ready,
+    other, along_own, squares_own, columns, model, rate_rows, cap_rows, rows_out, columns_out,
+    driver, rate, cap, rows, along_y, squares, arrived, ready,
 ):
     gy, gx, core = lax.axis_index(("x", "c")), lax.axis_index(("z", "y")), lax.axis_index("c")
     groups = model.shape[0] // GROUP
+    half = groups // 2
     tables = [
         pltpu.make_async_copy(rows_hbm.at[gy], rows, ready.at[0]),
         pltpu.make_async_copy(columns_hbm.at[gx], columns, ready.at[1]),
@@ -69,7 +86,12 @@
     ]
 
     def ordered(step):
-        return lax.rem(step + (1 - core) * (groups // 2), groups)
+        return lax.rem(step + (1 - core) * half, groups)
+
+    def held(step):
+        if step < half:
+            return along_y.at[step % 2], squares.at[step % 2]
+        return along_own.at[step - half], squares_own.at[step - half]
 
     pieces = []
     for step in range(groups):
@@ -92,36 +114,23 @@
     for piece in range(1, AHEAD):
         for copy in fetch(piece):
             copy.start()
-    along_y[...] = jnp.zeros_like(along_y)
-    squares[...] = jnp.zeros_like(squares)
+    for step in [0, 1, *range(half, groups)]:
+        lines, sums = held(step)
+        lines[GROUP * WAVES :, :] = jnp.zeros((TILES * LANES - GROUP * WAVES, 2 * LANES), lines.dtype)
+        sums[GROUP * 8 :, :] = jnp.zeros((8 * (SLOTS - GROUP), LANES), jnp.float32)
 
     def first_contraction(step, i):
+        lines, sums = held(step)
         field = ordered(step) * GROUP + i
         difference = driver[field] - model[field]
         folded = (difference * difference).reshape(-1, 8, LANES)
-        squares[step % 2, i * 8 : i * 8 + 8, :] = jnp.sum(folded, axis=0)
+        sums[i * 8 : i * 8 + 8, :] = jnp.sum(folded, axis=0)
         parts = jnp.concatenate(split(difference), axis=1)
         product = dot(rows[...], parts, ((1,), (0,)))
         product = product[:WAVES] + product[WAVES:]
         high, low = split(product[:, :LANES] + product[:, LANES:])
-        along_y[step % 2, i * WAVES : (i + 1) * WAVES, :LANES] = high
-        along_y[step % 2, i * WAVES : (i + 1) * WAVES, LANES:] = low
-
-    def second_contraction(step):
-        both = dot(columns[...], along_y[step % 2], ((1,), (1,)))
-        both = both[:WAVES] + both[WAVES:]
-        total = squares[step % 2, pl.ds(0, SLOTS, stride=8), :]
-        for s in range(1, 8):
-            total = total + squares[step % 2, pl.ds(s, SLOTS, stride=8), :]
-        total = jnp.sum(total, axis=1, keepdims=True)
-        tiles = [both[:, t * LANES : (t + 1) * LANES] for t in range(TILES)]
-        lane = lax.broadcasted_iota(jnp.int32, (SLOTS, LANES), 1)
-        top = jnp.where(lane == LANES - 1, total, tiles[-1][:SLOTS])
-        tiles[-1] = jnp.concatenate([top, tiles[-1][SLOTS:]], axis=0)
-        kept = other if step < groups // 2 else mine
-        first = step % (groups // 2) * TILES * WAVES
-        for t in range(TILES):
-            kept[first + t * WAVES : first + (t + 1) * WAVES, :] = tiles[t]
+        lines[i * WAVES : (i + 1) * WAVES, :LANES] = high
+        lines[i * WAVES : (i + 1) * WAVES, LANES:] = low
 
     for piece, (step, first, size) in enumerate(pieces):
         if piece == 0:
@@ -134,27 +143,67 @@
                 copy.start()
         for i in range(first, first + size):
             first_contraction(step, i)
-            if i == 2 and step > 0:
-                second_contraction(step - 1)
-        if step == 1:
+            if i == 2 and 0 < step <= half:
+                second_contraction(columns, *held(step - 1), other, step - 1)
+        if piece == 1:
             for copy in later:
                 copy.wait()
             for field in range(model.shape[0]):
                 place = field // GROUP * SLOTS + field % GROUP
                 rate_rows[place : place + 1, :] = jnp.full((1, LANES), rate[field])
                 cap_rows[place : place + 1, :] = jnp.full((1, LANES), cap[field])
-    second_contraction(groups - 1)
+
+
+def contract_kernel(along_own, squares_own, columns, mine):
+    for step in range(along_own.shape[0]):
+        second_contraction(columns, along_own.at[step], squares_own.at[step], mine, step)
+
+
+def tiles_of(coefficients, step):
+    first = step * TILES * WAVES
+    return [coefficients[first + t * WAVES : first + (t + 1) * WAVES, :] for t in range(TILES)]
+
+
+def strengths(cells, tiles, rate_rows, cap_rows, group):
+    limits = pl.ds(pl.multiple_of(group * SLOTS, SLOTS), SLOTS)
+    spread = jnp.sqrt(tiles[-1][:SLOTS, LANES - 1 :] / cells + EPSILON)
+    return rate_rows[limits, :] * jnp.minimum(1.0, cap_rows[limits, :] / spread)
+
+
+def synthesized(tiles, columns):
+    high, low = split(jnp.concatenate(tiles, axis=1))
+    both = dot(high, columns[...], ((0,), (0,))) + dot(low, columns[...], ((0,), (0,)))
+    return both[:, :LANES] + both[:, LANES:]
+
+
+def stacked(lines, strength):
+    high, low = split(lines * strength)
+    return jnp.concatenate([high, low, high], axis=0)
+
+
+def begin_kernel(cells, own, rate_rows, cap_rows, columns, stacks):
+    groups = own.shape[0] // (TILES * WAVES)
+    base = lax.axis_index("c") * groups
+    for step in range(groups):
+        tiles = tiles_of(own, step)
+        strength = strengths(cells, tiles, rate_rows, cap_rows, base + step)
+        lines = synthesized(tiles, columns)
+        for j in range(GROUP):
+            stacks[step * GROUP + j] = stacked(
+                lines[j * WAVES : (j + 1) * WAVES, :], strength[j : j + 1, :]
+            )
 
 
 def synthesis_kernel(
-    cells, own, sibling, rate_rows, cap_rows, model, rows, columns, nudged_hbm,
+    cells, stacks, sibling, rate_rows, cap_rows, model, rows, columns, nudged_hbm,
     nudged, along_x, strength, leaving,
 ):
     core = lax.axis_index("c")
     groups = model.shape[0] // GROUP
+    half = groups // 2
 
     def ordered(step):
-        return lax.rem(step + core * (groups // 2), groups)
+        return lax.rem(step + core * half, groups)
 
     def chunk_out(step, first, size):
         span = pl.ds(ordered(step) * GROUP + first, size)
@@ -162,29 +211,24 @@
         return pltpu.make_async_copy(nudged.at[span], nudged_hbm.at[span], place)
 
     def prepare(step):
-        ref = own if step < groups // 2 else sibling
-        first = step % (groups // 2) * TILES * WAVES
-        tiles = [ref[first + t * WAVES : first + (t + 1) * WAVES, :] for t in range(TILES)]
-        limits = pl.ds(pl.multiple_of(ordered(step) * SLOTS, SLOTS), SLOTS)
-        spread = jnp.sqrt(tiles[-1][:SLOTS, LANES - 1 :] / cells + EPSILON)
-        strength[step % 2] = rate_rows[limits, :] * jnp.minimum(1.0, cap_rows[limits, :] / spread)
-        high, low = split(jnp.concatenate(tiles, axis=1))
-        both = dot(high, columns[...], ((0,), (0,))) + dot(low, columns[...], ((0,), (0,)))
-        along_x[step % 2] = both[:, :LANES] + both[:, LANES:]
-
-    prepare(0)
+        tiles = tiles_of(sibling, step - half)
+        strength[step % 2] = strengths(cells, tiles, rate_rows, cap_rows, ordered(step))
+        along_x[step % 2] = synthesized(tiles, columns)
+
+    def stack_of(step, j):
+        if step < half:
+            return stacks[step * GROUP + j]
+        lines = along_x[step % 2, j * WAVES : (j + 1) * WAVES, :]
+        return stacked(lines, strength[step % 2, j : j + 1, :])
+
     for step in range(groups):
         for i in range(0, GROUP, 2):
-            stacks = []
-            for j in (i, i + 1):
-                scaled = along_x[step % 2, j * WAVES : (j + 1) * WAVES, :]
-                high, low = split(scaled * strength[step % 2, j : j + 1, :])
-                stacks.append(jnp.concatenate([high, low, high], axis=0))
-            pair = dot(rows[...], jnp.concatenate(stacks, axis=1), ((1,), (0,)))
+            pair = jnp.concatenate([stack_of(step, i), stack_of(step, i + 1)], axis=1)
+            pair = dot(rows[...], pair, ((1,), (0,)))
             for j in (0, 1):
                 field = ordered(step) * GROUP + i + j
                 nudged[field] = model[field] + pair[:, j * LANES : (j + 1) * LANES]
-            if i == 0 and step + 1 < groups:
+            if i == 0 and half <= step + 1 < groups:
                 prepare(step + 1)
             if (i + 2) % CHUNK == 0:
                 chunk_out(step, i + 2 - CHUNK, CHUNK).start()
@@ -235,13 +279,17 @@
 
 def analysis(model, driver, rate, cap, rows, columns, rows_out, columns_out):
     groups = model.shape[0] // GROUP
-    half = groups // 2 * TILES * WAVES
+    half = groups // 2
     pieces = groups - 1 + len(LAST_PIECES)
+    lines = (TILES * LANES, 2 * LANES)
+    sums = (8 * SLOTS, LANES)
     return pl.pallas_call(
         analysis_kernel,
         out_shape=[
-            pltpu.VMEM((half, LANES), jnp.float32),
-            pltpu.VMEM((half, LANES), jnp.float32),
+            pltpu.VMEM((half * TILES * WAVES, LANES), jnp.float32),
+            pltpu.VMEM((half, *lines), jnp.bfloat16),
+            pltpu.VMEM((half, *sums), jnp.float32),
+            pltpu.VMEM(columns.shape[1:], jnp.bfloat16),
             pltpu.VMEM(model.shape, jnp.float32),
             pltpu.VMEM((groups * SLOTS, LANES), jnp.float32),
             pltpu.VMEM((groups * SLOTS, LANES), jnp.float32),
@@ -249,24 +297,50 @@
             pltpu.VMEM(columns_out.shape[1:], jnp.bfloat16),
         ],
         in_specs=[IN_HBM] * 8,
-        out_specs=[IN_VMEM] * 7,
+        out_specs=[IN_VMEM] * 9,
         scratch_shapes=[
             pltpu.VMEM(model.shape, jnp.float32),
             pltpu.SMEM(rate.shape, jnp.float32),
             pltpu.SMEM(cap.shape, jnp.float32),
             pltpu.VMEM(rows.shape[1:], jnp.bfloat16),
-            pltpu.VMEM(columns.shape[1:], jnp.bfloat16),
-            pltpu.VMEM((2, TILES * LANES, 2 * LANES), jnp.bfloat16),
-            pltpu.VMEM((2, 8 * SLOTS, LANES), jnp.float32),
+            pltpu.VMEM((2, *lines), jnp.bfloat16),
+            pltpu.VMEM((2, *sums), jnp.float32),
             pltpu.SemaphoreType.DMA((2, pieces)),
             pltpu.SemaphoreType.DMA((6,)),
         ],
-        compiler_params=pltpu.CompilerParams(vmem_limit_bytes=24 << 20),
+        compiler_params=pltpu.CompilerParams(vmem_limit_bytes=16 << 20),
+        cost_estimate=estimate(2 * model.size),
         name="analysis",
     )(*map(kept_in_hbm, (model, driver, rate, cap, rows, columns, rows_out, columns_out)))
 
 
-def synthesis(own, sibling, rate_rows, cap_rows, model, rows, columns, cells):
+def contract(along_own, squares_own, columns):
+    shape = (along_own.shape[0] * TILES * WAVES, LANES)
+    return pl.pallas_call(
+        contract_kernel,
+        out_shape=pltpu.VMEM(shape, jnp.float32),
+        in_specs=[IN_VMEM] * 3,
+        out_specs=IN_VMEM,
+        compiler_params=pltpu.CompilerParams(vmem_limit_bytes=2 << 20),
+        cost_estimate=estimate(along_own.size),
+        name="contract",
+    )(*map(kept_in_vmem, (along_own, squares_own, columns)))
+
+
+def begin(own, rate_rows, cap_rows, columns, cells):
+    fields = own.shape[0] // (TILES * WAVES) * GROUP
+    return pl.pallas_call(
+        lambda *refs: begin_kernel(cells, *refs),
+        out_shape=pltpu.VMEM((fields, 3 * WAVES, LANES), jnp.bfloat16),
+        in_specs=[IN_VMEM] * 4,
+        out_specs=IN_VMEM,
+        compiler_params=pltpu.CompilerParams(vmem_limit_bytes=2 << 20),
+        cost_estimate=estimate(fields * 3 * WAVES * LANES),
+        name="begin",
+    )(*map(kept_in_vmem, (own, rate_rows, cap_rows, columns)))
+
+
+def synthesis(stacks, sibling, rate_rows, cap_rows, model, rows, columns, cells):
     groups = model.shape[0] // GROUP
     return pl.pallas_call(
         lambda *refs: synthesis_kernel(cells, *refs),
@@ -279,9 +353,14 @@
             pltpu.VMEM((2, SLOTS, LANES), jnp.float32),
             pltpu.SemaphoreType.DMA((groups * (GROUP // CHUNK),)),
         ],
-        compiler_params=pltpu.CompilerParams(vmem_limit_bytes=24 << 20),
+        compiler_params=pltpu.CompilerParams(vmem_limit_bytes=12 << 20),
+        cost_estimate=estimate(2 * model.size),
         name="synthesis",
-    )(*map(kept_in_vmem, (own, sibling, rate_rows, cap_rows, model, rows, columns)))
+    )(*map(kept_in_vmem, (stacks, sibling, rate_rows, cap_rows, model, rows, columns)))
+
+
+def estimate(values):
+    return pl.CostEstimate(flops=600 * values, bytes_accessed=4 * values, transcendentals=0)
 
 
 def per_device(model_field, driver_field, nudge_rate, increment_cap):
@@ -300,7 +379,7 @@
     rows_out = np.concatenate([high_y, high_y, low_y], axis=2)
     columns_out = np.concatenate([turned(high_x), turned(low_x)], axis=2)
 
-    mine, other, *kept = analysis(
+    other, along_own, squares_own, columns_kept, *kept = analysis(
         model_field,
         driver_field,
         nudge_rate,
@@ -310,18 +389,21 @@
         rows_out,
         columns_out,
     )
-    model_kept, rate_rows, cap_rows, rows_kept, columns_kept = kept
-    pair = mine + lax.ppermute(other, "c", swap)
+    model_kept, rate_rows, cap_rows, rows_out_kept, columns_out_kept = kept
+    arriving = lax.ppermute(other, "c", swap)
+    mine = contract(along_own, squares_own, columns_kept)
 
     def exchanged(value):
         blocks = value.reshape(chips, 1, -1)
         return lax.all_to_all(blocks, CHIP, 0, 0, tiled=True).reshape(value.shape)
 
-    own = exchanged(share(exchanged(pair), chips))
+    own = exchanged(share(exchanged(mine + arriving), chips))
     sibling = lax.ppermute(own, "c", swap)
     cells = float(height * parts_y * width * parts_x)
+    limits = rate_rows, cap_rows
+    stacks = begin(own, *limits, columns_out_kept, cells)
     return synthesis(
-        own, sibling, rate_rows, cap_rows, model_kept, rows_kept, columns_kept, cells
+        stacks, sibling, *limits, model_kept, rows_out_kept, columns_out_kept, cells
     )
 
 

time: 53.1 us -> 52.3 us (0.985)
  waiting for transfers between devices: 2.42 us -> 1.4 us
    pallas_call x1 -> x3, Pallas kernels: 6.6 us -> 7.36 us  [the longest x1 6.35 us: analysis(): pl.pallas_call(analysis_kernel, out_shape=[pltpu.VMEM((half * TILES * WAV...]
    ppermute x1, waiting for transfers between devices: 1.21 us -> 0.56 us  [per_device(): sibling = lax.ppermute(own, 'c', swap)]
    pallas_call x1, Pallas kernels: 4.17 us -> 3.62 us  [synthesis(): pl.pallas_call(lambda *refs: synthesis_kernel(cells, *refs), out_shape=pl...]
  transfers between devices with their start and end apart: 2 -> 2, of which waited for: 2 -> 2; matrix products, arithmetic and copies ran while one was open for 0% -> 0% of each run, Pallas kernels for 0% -> 2%
where the time goes in v4:
time: 52.3 us; the launch traced here: 52.1 us
  blocking collectives  34.9 us (67%)
  Pallas kernels  11 us (21%)
  starting transfers between devices  4.67 us (9%)
  waiting for transfers between devices  1.4 us (3%)
    all_to_all x2, blocking collectives, exchanged(): return lax.all_to_all(blocks, CHIP, 0, 0, tiled=True).reshape(value.shape)  34.9 us
    pallas_call x1, Pallas kernels, analysis(): pl.pallas_call(analysis_kernel, out_shape=[pltpu.VMEM((half * TILES * WAV...  6.35 us
    pallas_call x1, Pallas kernels, synthesis(): pl.pallas_call(lambda *refs: synthesis_kernel(cells, *refs), out_shape=pl...  3.62 us
    ppermute x1, starting transfers between devices, per_device(): sibling = lax.ppermute(own, 'c', swap)  3.17 us
    ppermute x1, starting transfers between devices, per_device(): arriving = lax.ppermute(other, 'c', swap)  1.5 us
  transfers between devices with their start and end apart: 2, of which 2 were waited for; matrix products, arithmetic and copies ran while one was open for 0% of the time, Pallas kernels for 2%

profile of v4, /device:TPU:1, one launch (start us, length us, event | category | flops | bytes accessed | tf_op | source)
XLA Modules:
  0.0 52.1 jit_solution(746862056895082834)
XLA Ops:
  0.0 6.4 %analysis.1 = (f32[576,128]{1,0:T(8,128)S(1)}, bf16[3,512,256]{2,1,0:T(8,128)(2,1)S(1)}, f32[3,128,128]{2,1,0:T(8,128)S(1)}, bf16[96,256]{1,0:T(8,128)(2,1)S(1)}...) custom-call(f32[60,256,128]{2,1,0:T(8,128)} %model_hbm.1, ...), custom_call_target="tpu_custom_call" | custom-call | flops 2359296000 | bytes 15728640 | tf_op jit(solution)/shard_map/analysis/pallas_call | solution.py:286
  6.4 1.5 %collective-permute-start = (f32[576,128]{1,0:T(8,128)S(1)}, f32[576,128]{1,0:T(8,128)S(1)}, u32[]{:S(2)}, u32[]{:S(2)}) collective-permute-start(f32[576,128]{1,0:T(8,128)S(1)} %get-tuple-element.17), channel_id=1, source_target_pairs={{0,16},{16,0},{1,17},{17,1},{2,18},{18,2},{3,19},{19,3},{4,20},{20... | collective-permute-start | bytes 884744 | tf_op jit(solution)/shard_map/ppermute | solution.py:393
  7.9 0.4 contract.1
  8.2 0.8 %collective-permute-done = f32[576,128]{1,0:T(8,128)S(1)} collective-permute-done((f32[576,128]{1,0:T(8,128)S(1)}, f32[576,128]{1,0:T(8,128)S(1)}, u32[]{:S(2)}, u32[]{:S(2)}) %collective-permute-start) | collective-permute-done | bytes 294944 | tf_op jit(solution)/shard_map/ppermute | solution.py:393
  9.1 20.9 %all_to_all.10 = f32[64,1,1152]{2,1,0:T(1,128)S(1)} all-to-all(f32[64,1,1152]{2,1,0:T(1,128)S(1)} %bitcast.8), channel_id=1, replica_groups=mesh['x'=4,'c'=2,'z'=4,'y'=4] {'x','z','y'}, dimensions={0} | all-to-all | bytes 589824 | tf_op jit(solution)/shard_map/all_to_all | solution.py:398
  30.0 0.1 share.1
  30.1 14.0 %all_to_all.11 = f32[64,1,1152]{2,1,0:T(1,128)S(1)} all-to-all(f32[64,1,1152]{2,1,0:T(1,128)S(1)} %bitcast.5), channel_id=1, replica_groups=mesh['x'=4,'c'=2,'z'=4,'y'=4] {'x','z','y'}, dimensions={0} | all-to-all | bytes 589824 | tf_op jit(solution)/shard_map/all_to_all | solution.py:398
  44.1 3.2 %collective-permute-start.1 = (f32[576,128]{1,0:T(8,128)S(1)}, f32[576,128]{1,0:T(8,128)S(1)}, u32[]{:S(2)}, u32[]{:S(2)}) collective-permute-start(f32[576,128]{1,0:T(8,128)S(1)} %bitcast.6), channel_id=1, source_target_pairs={{0,16},{16,0},{1,17},{17,1},{2,18},{18,2},{3,19},{19,3},{4,20},{20... | collective-permute-start | bytes 884744 | tf_op jit(solution)/shard_map/ppermute | solution.py:401
  47.3 0.6 %begin.1.refs_0_ = bf16[30,144,128]{2,1,0:T(8,128)(2,1)S(1)} custom-call(f32[576,128]{1,0:T(8,128)S(1)} %bitcast.7, f32[96,128]{1,0:T(8,128)S(1)} %get-tuple-element.18.refs_1_.refs_2_, f32[96,128]{1,0:T(8,128)S(1)} %get-tuple-element.19.refs_2_.refs_3_, bf16[48,256]{1,0:T(8,128)(2,1)S(1)} %get-tuple-element.20.refs_3_.refs_6_), custom_call_target="tpu_custom_call" | custom-call | flops 331776000 | bytes 2211840 | tf_op jit(solution)/shard_map/begin/pallas_call | solution.py:332
  47.9 0.6 %collective-permute-done.1.refs_1_ = f32[576,128]{1,0:T(8,128)S(1)} collective-permute-done((f32[576,128]{1,0:T(8,128)S(1)}, f32[576,128]{1,0:T(8,128)S(1)}, u32[]{:S(2)}, u32[]{:S(2)}) %collective-permute-start.1) | collective-permute-done | bytes 294944 | tf_op jit(solution)/shard_map/ppermute | solution.py:401
  48.5 3.6 %synthesis.1 = f32[60,256,128]{2,1,0:T(8,128)} custom-call(bf16[30,144,128]{2,1,0:T(8,128)(2,1)S(1)} %begin.1.refs_0_, f32[576,128]{1,0:T(8,128)S(1)} %collective-permute-done.1.refs_1_, f32[96,128]{1,0:T(8,128)S(1)} %get-tuple-element.18.refs_1_.refs_2_, f32[96,128]{1,0:T(8,128)S(1)} %get-tuple-element.19.refs_2_.refs_3_, ...), custom_call_target="tpu_custom_call" | custom-call | flops 2359296000 | bytes 15728640 | tf_op jit(solution)/shard_map/synthesis/pallas_call | solution.py:345
  (1 shorter events, 0.0 us)
Async XLA Ops:
  6.4 2.7 %collective-permute-start = (f32[576,128]{1,0:T(8,128)S(1)}, f32[576,128]{1,0:T(8,128)S(1)}, u32[]{:S(2)}, u32[]{:S(2)}) collective-permute-start(f32[576,128]{1,0:T(8,128)S(1)} %get-tuple-element.17), channel_id=1, source_target_pairs={{0,16},{16,0},{1,17},{17,1},{2,18},{18,2},{3,19},{19,3},{4,20},{20... | collective-permute-start | bytes 884744 | tf_op jit(solution)/shard_map/ppermute | solution.py:393
  44.1 4.4 %collective-permute-start.1 = (f32[576,128]{1,0:T(8,128)S(1)}, f32[576,128]{1,0:T(8,128)S(1)}, u32[]{:S(2)}, u32[]{:S(2)}) collective-permute-start(f32[576,128]{1,0:T(8,128)S(1)} %bitcast.6), channel_id=1, source_target_pairs={{0,16},{16,0},{1,17},{17,1},{2,18},{18,2},{3,19},{19,3},{4,20},{20... | collective-permute-start | bytes 884744 | tf_op jit(solution)/shard_map/ppermute | solution.py:401

commit v5 on v4

--- a/solution.py
+++ b/solution.py
@@ -15,7 +15,6 @@
 TILES = 4
 LANES = 128
 AHEAD = 3
-LAST_PIECES = (6, 4)
 CHUNK = 10
 SLOTS = 16
 CHIP = ("x", "z", "y")
@@ -48,6 +47,22 @@
 
 def dot(left, right, contract):
     return lax.dot_general(left, right, (contract, ((), ())), preferred_element_type=jnp.float32)
+
+
+def first_contraction(difference, rows, lines, sums, i):
+    folded = (difference * difference).reshape(-1, 8, LANES)
+    sums[i * 8 : i * 8 + 8, :] = jnp.sum(folded, axis=0)
+    product = dot(rows[...], jnp.concatenate(split(difference), axis=1), ((1,), (0,)))
+    product = product[:WAVES] + product[WAVES:]
+    high, low = split(product[:, :LANES] + product[:, LANES:])
+    lines[i * WAVES : (i + 1) * WAVES, :LANES] = high
+    lines[i * WAVES : (i + 1) * WAVES, LANES:] = low
+
+
+def clear_spare(lines, sums):
+    spare = (TILES * LANES - GROUP * WAVES, 2 * LANES)
+    lines[GROUP * WAVES :, :] = jnp.zeros(spare, lines.dtype)
+    sums[GROUP * 8 :, :] = jnp.zeros((8 * (SLOTS - GROUP), LANES), jnp.float32)
 
 
 def second_contraction(columns, along_y, squares, coefficients, step):
@@ -68,8 +83,8 @@
 
 def analysis_kernel(
     model_hbm, driver_hbm, rate_hbm, cap_hbm, rows_hbm, columns_hbm, rows_out_hbm, columns_out_hbm,
-    other, along_own, squares_own, columns, model, rate_rows, cap_rows, rows_out, columns_out,
-    driver, rate, cap, rows, along_y, squares, arrived, ready,
+    other, along_own, squares_own, driver_last, rows, columns, model, rate_rows, cap_rows,
+    rows_out, columns_out, driver, rate, cap, along_y, squares, arrived, ready,
 ):
     gy, gx, core = lax.axis_index(("x", "c")), lax.axis_index(("z", "y")), lax.axis_index("c")
     groups = model.shape[0] // GROUP
@@ -93,59 +108,34 @@
             return along_y.at[step % 2], squares.at[step % 2]
         return along_own.at[step - half], squares_own.at[step - half]
 
-    pieces = []
-    for step in range(groups):
-        sizes = LAST_PIECES if step == groups - 1 else (GROUP,)
-        first = 0
-        for size in sizes:
-            pieces.append((step, first, size))
-            first += size
-
-    def fetch(piece):
-        step, first, size = pieces[piece]
-        span = pl.ds(ordered(step) * GROUP + first, size)
+    def fetch(step):
+        span = pl.ds(ordered(step) * GROUP, GROUP)
+        kept = driver_last if step == groups - 1 else driver.at[pl.ds(step * GROUP, GROUP)]
         return [
-            pltpu.make_async_copy(model_hbm.at[span], model.at[span], arrived.at[0, piece]),
-            pltpu.make_async_copy(driver_hbm.at[span], driver.at[span], arrived.at[1, piece]),
+            pltpu.make_async_copy(model_hbm.at[span], model.at[span], arrived.at[0, step]),
+            pltpu.make_async_copy(driver_hbm.at[span], kept, arrived.at[1, step]),
         ]
 
     for copy in tables + fetch(0) + later:
         copy.start()
-    for piece in range(1, AHEAD):
-        for copy in fetch(piece):
+    for step in range(1, AHEAD):
+        for copy in fetch(step):
             copy.start()
-    for step in [0, 1, *range(half, groups)]:
-        lines, sums = held(step)
-        lines[GROUP * WAVES :, :] = jnp.zeros((TILES * LANES - GROUP * WAVES, 2 * LANES), lines.dtype)
-        sums[GROUP * 8 :, :] = jnp.zeros((8 * (SLOTS - GROUP), LANES), jnp.float32)
-
-    def first_contraction(step, i):
-        lines, sums = held(step)
-        field = ordered(step) * GROUP + i
-        difference = driver[field] - model[field]
-        folded = (difference * difference).reshape(-1, 8, LANES)
-        sums[i * 8 : i * 8 + 8, :] = jnp.sum(folded, axis=0)
-        parts = jnp.concatenate(split(difference), axis=1)
-        product = dot(rows[...], parts, ((1,), (0,)))
-        product = product[:WAVES] + product[WAVES:]
-        high, low = split(product[:, :LANES] + product[:, LANES:])
-        lines[i * WAVES : (i + 1) * WAVES, :LANES] = high
-        lines[i * WAVES : (i + 1) * WAVES, LANES:] = low
-
-    for piece, (step, first, size) in enumerate(pieces):
-        if piece == 0:
-            for copy in tables:
-                copy.wait()
-        for copy in fetch(piece):
+    for step in [0, 1, *range(half, groups - 1)]:
+        clear_spare(*held(step))
+
+    for step in range(groups):
+        for copy in (tables if step == 0 else []) + fetch(step):
             copy.wait()
-        if piece + AHEAD < len(pieces):
-            for copy in fetch(piece + AHEAD):
+        if step + AHEAD < groups:
+            for copy in fetch(step + AHEAD):
                 copy.start()
-        for i in range(first, first + size):
-            first_contraction(step, i)
+        for i in range(GROUP) if step < groups - 1 else []:
+            difference = driver[step * GROUP + i] - model[ordered(step) * GROUP + i]
+            first_contraction(difference, rows, *held(step), i)
             if i == 2 and 0 < step <= half:
                 second_contraction(columns, *held(step - 1), other, step - 1)
-        if piece == 1:
+        if step == 1:
             for copy in later:
                 copy.wait()
             for field in range(model.shape[0]):
@@ -154,9 +144,20 @@
                 cap_rows[place : place + 1, :] = jnp.full((1, LANES), cap[field])
 
 
-def contract_kernel(along_own, squares_own, columns, mine):
-    for step in range(along_own.shape[0]):
-        second_contraction(columns, along_own.at[step], squares_own.at[step], mine, step)
+def contract_kernel(
+    along_own, squares_own, driver_last, model, rows, columns, mine, along_y, squares
+):
+    core = lax.axis_index("c")
+    groups = model.shape[0] // GROUP
+    half = groups // 2
+    base = lax.rem(groups - 1 + (1 - core) * half, groups) * GROUP
+    clear_spare(along_y, squares)
+    for i in range(GROUP):
+        first_contraction(driver_last[i] - model[base + i], rows, along_y, squares, i)
+        if i % 3 == 2 and i // 3 < half - 1:
+            step = i // 3
+            second_contraction(columns, along_own.at[step], squares_own.at[step], mine, step)
+    second_contraction(columns, along_y, squares, mine, half - 1)
 
 
 def tiles_of(coefficients, step):
@@ -181,21 +182,33 @@
     return jnp.concatenate([high, low, high], axis=0)
 
 
-def begin_kernel(cells, own, rate_rows, cap_rows, columns, stacks):
+def nudge_pair(rows, stacks, models):
+    pair = dot(rows[...], jnp.concatenate(stacks, axis=1), ((1,), (0,)))
+    return [model + pair[:, j * LANES : (j + 1) * LANES] for j, model in enumerate(models)]
+
+
+def begin_kernel(cells, own, rate_rows, cap_rows, model, rows, columns, stacks, first_nudged):
     groups = own.shape[0] // (TILES * WAVES)
     base = lax.axis_index("c") * groups
+    first = []
     for step in range(groups):
         tiles = tiles_of(own, step)
         strength = strengths(cells, tiles, rate_rows, cap_rows, base + step)
         lines = synthesized(tiles, columns)
         for j in range(GROUP):
-            stacks[step * GROUP + j] = stacked(
-                lines[j * WAVES : (j + 1) * WAVES, :], strength[j : j + 1, :]
-            )
+            stack = stacked(lines[j * WAVES : (j + 1) * WAVES, :], strength[j : j + 1, :])
+            if step > 0:
+                stacks[(step - 1) * GROUP + j] = stack
+                continue
+            first.append(stack)
+            if j % 2:
+                models = [model[base * GROUP + k] for k in (j - 1, j)]
+                pair = nudge_pair(rows, first[j - 1 : j + 1], models)
+                first_nudged[j - 1], first_nudged[j] = pair
 
 
 def synthesis_kernel(
-    cells, stacks, sibling, rate_rows, cap_rows, model, rows, columns, nudged_hbm,
+    cells, stacks, first_nudged, sibling, rate_rows, cap_rows, model, rows, columns, nudged_hbm,
     nudged, along_x, strength, leaving,
 ):
     core = lax.axis_index("c")
@@ -208,7 +221,9 @@
     def chunk_out(step, first, size):
         span = pl.ds(ordered(step) * GROUP + first, size)
         place = leaving.at[step * (GROUP // CHUNK) + first // CHUNK]
-        return pltpu.make_async_copy(nudged.at[span], nudged_hbm.at[span], place)
+        here = first_nudged if step == 0 else nudged.at[step - 1]
+        here = here.at[pl.ds(first, size)]
+        return pltpu.make_async_copy(here, nudged_hbm.at[span], place)
 
     def prepare(step):
         tiles = tiles_of(sibling, step - half)
@@ -217,17 +232,17 @@
 
     def stack_of(step, j):
         if step < half:
-            return stacks[step * GROUP + j]
+            return stacks[(step - 1) * GROUP + j]
         lines = along_x[step % 2, j * WAVES : (j + 1) * WAVES, :]
         return stacked(lines, strength[step % 2, j : j + 1, :])
 
-    for step in range(groups):
+    for first in range(0, GROUP, CHUNK):
+        chunk_out(0, first, CHUNK).start()
+    for step in range(1, groups):
         for i in range(0, GROUP, 2):
-            pair = jnp.concatenate([stack_of(step, i), stack_of(step, i + 1)], axis=1)
-            pair = dot(rows[...], pair, ((1,), (0,)))
-            for j in (0, 1):
-                field = ordered(step) * GROUP + i + j
-                nudged[field] = model[field] + pair[:, j * LANES : (j + 1) * LANES]
+            pair = [stack_of(step, j) for j in (i, i + 1)]
+            models = [model[ordered(step) * GROUP + j] for j in (i, i + 1)]
+            nudged[step - 1, i], nudged[step - 1, i + 1] = nudge_pair(rows, pair, models)
             if i == 0 and half <= step + 1 < groups:
                 prepare(step + 1)
             if (i + 2) % CHUNK == 0:
@@ -280,15 +295,16 @@
 def analysis(model, driver, rate, cap, rows, columns, rows_out, columns_out):
     groups = model.shape[0] // GROUP
     half = groups // 2
-    pieces = groups - 1 + len(LAST_PIECES)
     lines = (TILES * LANES, 2 * LANES)
     sums = (8 * SLOTS, LANES)
     return pl.pallas_call(
         analysis_kernel,
         out_shape=[
             pltpu.VMEM((half * TILES * WAVES, LANES), jnp.float32),
-            pltpu.VMEM((half, *lines), jnp.bfloat16),
-            pltpu.VMEM((half, *sums), jnp.float32),
+            pltpu.VMEM((half - 1, *lines), jnp.bfloat16),
+            pltpu.VMEM((half - 1, *sums), jnp.float32),
+            pltpu.VMEM((GROUP, *model.shape[1:]), jnp.float32),
+            pltpu.VMEM(rows.shape[1:], jnp.bfloat16),
             pltpu.VMEM(columns.shape[1:], jnp.bfloat16),
             pltpu.VMEM(model.shape, jnp.float32),
             pltpu.VMEM((groups * SLOTS, LANES), jnp.float32),
@@ -297,15 +313,14 @@
             pltpu.VMEM(columns_out.shape[1:], jnp.bfloat16),
         ],
         in_specs=[IN_HBM] * 8,
-        out_specs=[IN_VMEM] * 9,
+        out_specs=[IN_VMEM] * 11,
         scratch_shapes=[
-            pltpu.VMEM(model.shape, jnp.float32),
+            pltpu.VMEM((model.shape[0] - GROUP, *model.shape[1:]), jnp.float32),
             pltpu.SMEM(rate.shape, jnp.float32),
             pltpu.SMEM(cap.shape, jnp.float32),
-            pltpu.VMEM(rows.shape[1:], jnp.bfloat16),
             pltpu.VMEM((2, *lines), jnp.bfloat16),
             pltpu.VMEM((2, *sums), jnp.float32),
-            pltpu.SemaphoreType.DMA((2, pieces)),
+            pltpu.SemaphoreType.DMA((2, groups)),
             pltpu.SemaphoreType.DMA((6,)),
         ],
         compiler_params=pltpu.CompilerParams(vmem_limit_bytes=16 << 20),
@@ -314,41 +329,49 @@
     )(*map(kept_in_hbm, (model, driver, rate, cap, rows, columns, rows_out, columns_out)))
 
 
-def contract(along_own, squares_own, columns):
-    shape = (along_own.shape[0] * TILES * WAVES, LANES)
+def contract(along_own, squares_own, driver_last, model, rows, columns):
+    half = along_own.shape[0] + 1
     return pl.pallas_call(
         contract_kernel,
-        out_shape=pltpu.VMEM(shape, jnp.float32),
-        in_specs=[IN_VMEM] * 3,
+        out_shape=pltpu.VMEM((half * TILES * WAVES, LANES), jnp.float32),
+        in_specs=[IN_VMEM] * 6,
         out_specs=IN_VMEM,
-        compiler_params=pltpu.CompilerParams(vmem_limit_bytes=2 << 20),
-        cost_estimate=estimate(along_own.size),
+        scratch_shapes=[
+            pltpu.VMEM(along_own.shape[1:], jnp.bfloat16),
+            pltpu.VMEM(squares_own.shape[1:], jnp.float32),
+        ],
+        compiler_params=pltpu.CompilerParams(vmem_limit_bytes=4 << 20),
+        cost_estimate=estimate(2 * driver_last.size),
         name="contract",
-    )(*map(kept_in_vmem, (along_own, squares_own, columns)))
-
-
-def begin(own, rate_rows, cap_rows, columns, cells):
-    fields = own.shape[0] // (TILES * WAVES) * GROUP
+    )(*map(kept_in_vmem, (along_own, squares_own, driver_last, model, rows, columns)))
+
+
+def begin(own, rate_rows, cap_rows, model, rows, columns, cells):
+    fields = own.shape[0] // (TILES * WAVES) * GROUP - GROUP
     return pl.pallas_call(
         lambda *refs: begin_kernel(cells, *refs),
-        out_shape=pltpu.VMEM((fields, 3 * WAVES, LANES), jnp.bfloat16),
-        in_specs=[IN_VMEM] * 4,
-        out_specs=IN_VMEM,
-        compiler_params=pltpu.CompilerParams(vmem_limit_bytes=2 << 20),
+        out_shape=[
+            pltpu.VMEM((fields, 3 * WAVES, LANES), jnp.bfloat16),
+            pltpu.VMEM((GROUP, *model.shape[1:]), jnp.float32),
+        ],
+        in_specs=[IN_VMEM] * 6,
+        out_specs=[IN_VMEM] * 2,
+        compiler_params=pltpu.CompilerParams(vmem_limit_bytes=4 << 20),
         cost_estimate=estimate(fields * 3 * WAVES * LANES),
         name="begin",
-    )(*map(kept_in_vmem, (own, rate_rows, cap_rows, columns)))
-
-
-def synthesis(stacks, sibling, rate_rows, cap_rows, model, rows, columns, cells):
+    )(*map(kept_in_vmem, (own, rate_rows, cap_rows, model, rows, columns)))
+
+
+def synthesis(stacks, first_nudged, sibling, rate_rows, cap_rows, model, rows, columns, cells):
     groups = model.shape[0] // GROUP
+    values = stacks, first_nudged, sibling, rate_rows, cap_rows, model, rows, columns
     return pl.pallas_call(
         lambda *refs: synthesis_kernel(cells, *refs),
         out_shape=pltpu.HBM(model.shape, jnp.float32),
-        in_specs=[IN_VMEM] * 7,
+        in_specs=[IN_VMEM] * 8,
         out_specs=IN_HBM,
         scratch_shapes=[
-            pltpu.VMEM(model.shape, jnp.float32),
+            pltpu.VMEM((groups - 1, GROUP, *model.shape[1:]), jnp.float32),
             pltpu.VMEM((2, TILES * LANES, LANES), jnp.float32),
             pltpu.VMEM((2, SLOTS, LANES), jnp.float32),
             pltpu.SemaphoreType.DMA((groups * (GROUP // CHUNK),)),
@@ -356,7 +379,7 @@
         compiler_params=pltpu.CompilerParams(vmem_limit_bytes=12 << 20),
         cost_estimate=estimate(2 * model.size),
         name="synthesis",
-    )(*map(kept_in_vmem, (stacks, sibling, rate_rows, cap_rows, model, rows, columns)))
+    )(*map(kept_in_vmem, values))
 
 
 def estimate(values):
@@ -379,7 +402,7 @@
     rows_out = np.concatenate([high_y, high_y, low_y], axis=2)
     columns_out = np.concatenate([turned(high_x), turned(low_x)], axis=2)
 
-    other, along_own, squares_own, columns_kept, *kept = analysis(
+    other, along_own, squares_own, driver_last, rows_kept, columns_kept, *kept = analysis(
         model_field,
         driver_field,
         nudge_rate,
@@ -391,7 +414,7 @@
     )
     model_kept, rate_rows, cap_rows, rows_out_kept, columns_out_kept = kept
     arriving = lax.ppermute(other, "c", swap)
-    mine = contract(along_own, squares_own, columns_kept)
+    mine = contract(along_own, squares_own, driver_last, model_kept, rows_kept, columns_kept)
 
     def exchanged(value):
         blocks = value.reshape(chips, 1, -1)
@@ -401,10 +424,9 @@
     sibling = lax.ppermute(own, "c", swap)
     cells = float(height * parts_y * width * parts_x)
     limits = rate_rows, cap_rows
-    stacks = begin(own, *limits, columns_out_kept, cells)
-    return synthesis(
-        stacks, sibling, *limits, model_kept, rows_out_kept, columns_out_kept, cells
-    )
+    rest = model_kept, rows_out_kept, columns_out_kept, cells
+    stacks, first_nudged = begin(own, *limits, *rest)
+    return synthesis(stacks, first_nudged, sibling, *limits, *rest)
 
 
 def solution(mesh):

time: 52.3 us -> 51.5 us (0.985)
  waiting for transfers between devices: 1.4 us -> 0.61 us
    pallas_call x2, Pallas kernels: 1.01 us -> 1.8 us  [the longest x1 1.03 us: begin(): pl.pallas_call(lambda *refs: begin_kernel(cells, *refs), out_shape=[pltpu...]
  transfers between devices with their start and end apart: 2 -> 2, of which waited for: 2 -> 2; matrix products, arithmetic and copies ran while one was open for 0% -> 0% of each run, Pallas kernels for 2% -> 4%
where the time goes in v5:
time: 51.5 us; the launch traced here: 51.3 us
  blocking collectives  34.9 us (68%)
  Pallas kernels  11.1 us (22%)
  starting transfers between devices  4.67 us (9%)
  waiting for transfers between devices  0.61 us (1%)
    all_to_all x2, blocking collectives, exchanged(): return lax.all_to_all(blocks, CHIP, 0, 0, tiled=True).reshape(value.shape)  34.9 us
    pallas_call x1, Pallas kernels, analysis(): pl.pallas_call(analysis_kernel, out_shape=[pltpu.VMEM((half * TILES * WAV...  5.94 us
    pallas_call x1, Pallas kernels, synthesis(): pl.pallas_call(lambda *refs: synthesis_kernel(cells, *refs), out_shape=pl...  3.26 us
    ppermute x1, starting transfers between devices, per_device(): sibling = lax.ppermute(own, 'c', swap)  3.17 us
    ppermute x1, starting transfers between devices, per_device(): arriving = lax.ppermute(other, 'c', swap)  1.5 us
    pallas_call x1, Pallas kernels, begin(): pl.pallas_call(lambda *refs: begin_kernel(cells, *refs), out_shape=[pltpu...  1.03 us
  transfers between devices with their start and end apart: 2, of which 2 were waited for; matrix products, arithmetic and copies ran while one was open for 0% of the time, Pallas kernels for 4%

profile of v5, /device:TPU:1, one launch (start us, length us, event | category | flops | bytes accessed | tf_op | source)
XLA Modules:
  0.0 51.3 jit_solution(14352119967583667087)
XLA Ops:
  0.0 5.9 %analysis.1 = (f32[576,128]{1,0:T(8,128)S(1)}, bf16[2,512,256]{2,1,0:T(8,128)(2,1)S(1)}, f32[2,128,128]{2,1,0:T(8,128)S(1)}, f32[10,256,128]{2,1,0:T(8,128)S(1)}...) custom-call(f32[60,256,128]{2,1,0:T(8,128)} %model_hbm.1, ...), custom_call_target="tpu_custom_call" | custom-call | flops 2359296000 | bytes 15728640 | tf_op jit(solution)/shard_map/analysis/pallas_call | solution.py:300
  5.9 1.5 %collective-permute-start = (f32[576,128]{1,0:T(8,128)S(1)}, f32[576,128]{1,0:T(8,128)S(1)}, u32[]{:S(2)}, u32[]{:S(2)}) collective-permute-start(f32[576,128]{1,0:T(8,128)S(1)} %get-tuple-element.24), channel_id=1, source_target_pairs={{0,16},{16,0},{1,17},{17,1},{2,18},{18,2},{3,19},{19,3},{4,20},{20... | collective-permute-start | bytes 884744 | tf_op jit(solution)/shard_map/ppermute | solution.py:416
  7.4 0.8 %contract.1 = f32[576,128]{1,0:T(8,128)S(1)} custom-call(bf16[2,512,256]{2,1,0:T(8,128)(2,1)S(1)} %get-tuple-element.18.along_own, f32[2,128,128]{2,1,0:T(8,128)S(1)} %get-tuple-element.19.squares_own, f32[10,256,128]{2,1,0:T(8,128)S(1)} %get-tuple-element.20.driver_last, f32[60,256,128]{2,1,0:T(8,128)S(1)} %get-tuple-element.21.model.refs_3_.refs_5_, ...), custom_call_target="tpu_custom_call" | custom-call | flops 393216000 | bytes 2621440 | tf_op jit(solution)/shard_map/contract/pallas_call | solution.py:334
  8.2 0.4 collective-permute-done
  8.7 20.9 %all_to_all.10 = f32[64,1,1152]{2,1,0:T(1,128)S(1)} all-to-all(f32[64,1,1152]{2,1,0:T(1,128)S(1)} %bitcast.8), channel_id=1, replica_groups=mesh['x'=4,'c'=2,'z'=4,'y'=4] {'x','z','y'}, dimensions={0} | all-to-all | bytes 589824 | tf_op jit(solution)/shard_map/all_to_all | solution.py:421
  29.6 0.1 share.1
  29.7 14.0 %all_to_all.11 = f32[64,1,1152]{2,1,0:T(1,128)S(1)} all-to-all(f32[64,1,1152]{2,1,0:T(1,128)S(1)} %bitcast.7), channel_id=1, replica_groups=mesh['x'=4,'c'=2,'z'=4,'y'=4] {'x','z','y'}, dimensions={0} | all-to-all | bytes 589824 | tf_op jit(solution)/shard_map/all_to_all | solution.py:421
  43.7 3.2 %collective-permute-start.1 = (f32[576,128]{1,0:T(8,128)S(1)}, f32[576,128]{1,0:T(8,128)S(1)}, u32[]{:S(2)}, u32[]{:S(2)}) collective-permute-start(f32[576,128]{1,0:T(8,128)S(1)} %bitcast.4), channel_id=1, source_target_pairs={{0,16},{16,0},{1,17},{17,1},{2,18},{18,2},{3,19},{19,3},{4,20},{20... | collective-permute-start | bytes 884744 | tf_op jit(solution)/shard_map/ppermute | solution.py:424
  46.8 1.0 %begin.1 = (bf16[20,144,128]{2,1,0:T(8,128)(2,1)S(1)}, f32[10,256,128]{2,1,0:T(8,128)S(1)}) custom-call(f32[576,128]{1,0:T(8,128)S(1)} %bitcast.5, f32[96,128]{1,0:T(8,128)S(1)} %get-tuple-element.25.refs_1_.refs_3_, f32[96,128]{1,0:T(8,128)S(1)} %get-tuple-element.26.refs_2_.refs_4_, f32[60,256,128]{2,1,0:T(8,128)S(1)} %get-tuple-element.21.model.refs_3_.refs_5_, ...), custom_call_target="tpu_custom_call" | custom-call | flops 221184000 | bytes 1474560 | tf_op jit(solution)/shard_map/begin/pallas_call | solution.py:351
  47.9 0.2 collective-permute-done.1.refs_2_
  48.1 3.3 %synthesis.1 = f32[60,256,128]{2,1,0:T(8,128)} custom-call(bf16[20,144,128]{2,1,0:T(8,128)(2,1)S(1)} %get-tuple-element.29.refs_0_, f32[10,256,128]{2,1,0:T(8,128)S(1)} %get-tuple-element.30.refs_1_, f32[576,128]{1,0:T(8,128)S(1)} %collective-permute-done.1.refs_2_, f32[96,128]{1,0:T(8,128)S(1)} %get-tuple-element.25.refs_1_.refs_3_, ...), custom_call_target="tpu_custom_call" | custom-call | flops 2359296000 | bytes 15728640 | tf_op jit(solution)/shard_map/synthesis/pallas_call | solution.py:368
  (1 shorter events, 0.0 us)
Async XLA Ops:
  5.9 2.7 %collective-permute-start = (f32[576,128]{1,0:T(8,128)S(1)}, f32[576,128]{1,0:T(8,128)S(1)}, u32[]{:S(2)}, u32[]{:S(2)}) collective-permute-start(f32[576,128]{1,0:T(8,128)S(1)} %get-tuple-element.24), channel_id=1, source_target_pairs={{0,16},{16,0},{1,17},{17,1},{2,18},{18,2},{3,19},{19,3},{4,20},{20... | collective-permute-start | bytes 884744 | tf_op jit(solution)/shard_map/ppermute | solution.py:416
  43.7 4.4 %collective-permute-start.1 = (f32[576,128]{1,0:T(8,128)S(1)}, f32[576,128]{1,0:T(8,128)S(1)}, u32[]{:S(2)}, u32[]{:S(2)}) collective-permute-start(f32[576,128]{1,0:T(8,128)S(1)} %bitcast.4), channel_id=1, source_target_pairs={{0,16},{16,0},{1,17},{17,1},{2,18},{18,2},{3,19},{19,3},{4,20},{20... | collective-permute-start | bytes 884744 | tf_op jit(solution)/shard_map/ppermute | solution.py:424

commit v6 on v5

--- a/solution.py
+++ b/solution.py
@@ -15,6 +15,7 @@
 TILES = 4
 LANES = 128
 AHEAD = 3
+TAIL = 4
 CHUNK = 10
 SLOTS = 16
 CHIP = ("x", "z", "y")
@@ -109,8 +110,9 @@
         return along_own.at[step - half], squares_own.at[step - half]
 
     def fetch(step):
-        span = pl.ds(ordered(step) * GROUP, GROUP)
-        kept = driver_last if step == groups - 1 else driver.at[pl.ds(step * GROUP, GROUP)]
+        last = step == groups - 1
+        span = pl.ds(ordered(step) * GROUP, GROUP - TAIL if last else GROUP)
+        kept = driver_last if last else driver.at[pl.ds(step * GROUP, GROUP)]
         return [
             pltpu.make_async_copy(model_hbm.at[span], model.at[span], arrived.at[0, step]),
             pltpu.make_async_copy(driver_hbm.at[span], kept, arrived.at[1, step]),
@@ -145,18 +147,31 @@
 
 
 def contract_kernel(
-    along_own, squares_own, driver_last, model, rows, columns, mine, along_y, squares
+    along_own, squares_own, driver_last, model, rows, columns, model_hbm, driver_hbm,
+    mine, model_tail, driver_tail, along_y, squares, arrived,
 ):
     core = lax.axis_index("c")
     groups = model.shape[0] // GROUP
     half = groups // 2
     base = lax.rem(groups - 1 + (1 - core) * half, groups) * GROUP
+    span = pl.ds(base + GROUP - TAIL, TAIL)
+    copies = [
+        pltpu.make_async_copy(model_hbm.at[span], model_tail, arrived.at[0]),
+        pltpu.make_async_copy(driver_hbm.at[span], driver_tail, arrived.at[1]),
+    ]
+    for copy in copies:
+        copy.start()
     clear_spare(along_y, squares)
-    for i in range(GROUP):
+    for i in range(GROUP - TAIL):
         first_contraction(driver_last[i] - model[base + i], rows, along_y, squares, i)
-        if i % 3 == 2 and i // 3 < half - 1:
-            step = i // 3
+        if i % 2 and i // 2 < half - 1:
+            step = i // 2
             second_contraction(columns, along_own.at[step], squares_own.at[step], mine, step)
+    for copy in copies:
+        copy.wait()
+    for i in range(TAIL):
+        difference = driver_tail[i] - model_tail[i]
+        first_contraction(difference, rows, along_y, squares, GROUP - TAIL + i)
     second_contraction(columns, along_y, squares, mine, half - 1)
 
 
@@ -187,29 +202,42 @@
     return [model + pair[:, j * LANES : (j + 1) * LANES] for j, model in enumerate(models)]
 
 
-def begin_kernel(cells, own, rate_rows, cap_rows, model, rows, columns, stacks, first_nudged):
+def begin_kernel(
+    cells, own, rate_rows, cap_rows, model, rows, columns, stacks, second, nudged_hbm,
+    first, leaving,
+):
     groups = own.shape[0] // (TILES * WAVES)
     base = lax.axis_index("c") * groups
-    first = []
+
+    def pair_out(pair):
+        here = first.at[pl.ds(2 * pair, 2)]
+        there = nudged_hbm.at[pl.ds(base * GROUP + 2 * pair, 2)]
+        return pltpu.make_async_copy(here, there, leaving.at[pair])
+
     for step in range(groups):
         tiles = tiles_of(own, step)
         strength = strengths(cells, tiles, rate_rows, cap_rows, base + step)
         lines = synthesized(tiles, columns)
-        for j in range(GROUP):
-            stack = stacked(lines[j * WAVES : (j + 1) * WAVES, :], strength[j : j + 1, :])
-            if step > 0:
-                stacks[(step - 1) * GROUP + j] = stack
+        for i in range(0, GROUP, 2):
+            pair = [
+                stacked(lines[j * WAVES : (j + 1) * WAVES, :], strength[j : j + 1, :])
+                for j in (i, i + 1)
+            ]
+            if step == 2:
+                stacks[i], stacks[i + 1] = pair
                 continue
-            first.append(stack)
-            if j % 2:
-                models = [model[base * GROUP + k] for k in (j - 1, j)]
-                pair = nudge_pair(rows, first[j - 1 : j + 1], models)
-                first_nudged[j - 1], first_nudged[j] = pair
+            models = [model[(base + step) * GROUP + j] for j in (i, i + 1)]
+            nudged = first if step == 0 else second
+            nudged[i], nudged[i + 1] = nudge_pair(rows, pair, models)
+            if step == 0:
+                pair_out(i // 2).start()
+    for pair in range(GROUP // 2):
+        pair_out(pair).wait()
 
 
 def synthesis_kernel(
-    cells, stacks, first_nudged, sibling, rate_rows, cap_rows, model, rows, columns, nudged_hbm,
-    nudged, along_x, strength, leaving,
+    cells, stacks, second, sibling, rate_rows, cap_rows, model, model_tail, rows, columns, begun,
+    nudged_hbm, nudged, along_x, strength, leaving,
 ):
     core = lax.axis_index("c")
     groups = model.shape[0] // GROUP
@@ -220,8 +248,8 @@
 
     def chunk_out(step, first, size):
         span = pl.ds(ordered(step) * GROUP + first, size)
-        place = leaving.at[step * (GROUP // CHUNK) + first // CHUNK]
-        here = first_nudged if step == 0 else nudged.at[step - 1]
+        place = leaving.at[(step - 1) * (GROUP // CHUNK) + first // CHUNK]
+        here = second if step == 1 else nudged.at[step - 2]
         here = here.at[pl.ds(first, size)]
         return pltpu.make_async_copy(here, nudged_hbm.at[span], place)
 
@@ -231,23 +259,28 @@
         along_x[step % 2] = synthesized(tiles, columns)
 
     def stack_of(step, j):
-        if step < half:
-            return stacks[(step - 1) * GROUP + j]
+        if step == 2:
+            return stacks[j]
         lines = along_x[step % 2, j * WAVES : (j + 1) * WAVES, :]
         return stacked(lines, strength[step % 2, j : j + 1, :])
 
+    def model_of(step, j):
+        if step == half - 1 and j >= GROUP - TAIL:
+            return model_tail[j - GROUP + TAIL]
+        return model[ordered(step) * GROUP + j]
+
     for first in range(0, GROUP, CHUNK):
-        chunk_out(0, first, CHUNK).start()
-    for step in range(1, groups):
+        chunk_out(1, first, CHUNK).start()
+    for step in range(2, groups):
         for i in range(0, GROUP, 2):
             pair = [stack_of(step, j) for j in (i, i + 1)]
-            models = [model[ordered(step) * GROUP + j] for j in (i, i + 1)]
-            nudged[step - 1, i], nudged[step - 1, i + 1] = nudge_pair(rows, pair, models)
-            if i == 0 and half <= step + 1 < groups:
+            models = [model_of(step, j) for j in (i, i + 1)]
+            nudged[step - 2, i], nudged[step - 2, i + 1] = nudge_pair(rows, pair, models)
+            if i == 0 and step + 1 < groups:
                 prepare(step + 1)
             if (i + 2) % CHUNK == 0:
                 chunk_out(step, i + 2 - CHUNK, CHUNK).start()
-    for step in range(groups):
+    for step in range(1, groups):
         for first in range(0, GROUP, CHUNK):
             chunk_out(step, first, CHUNK).wait()
 
@@ -303,7 +336,7 @@
             pltpu.VMEM((half * TILES * WAVES, LANES), jnp.float32),
             pltpu.VMEM((half - 1, *lines), jnp.bfloat16),
             pltpu.VMEM((half - 1, *sums), jnp.float32),
-            pltpu.VMEM((GROUP, *model.shape[1:]), jnp.float32),
+            pltpu.VMEM((GROUP - TAIL, *model.shape[1:]), jnp.float32),
             pltpu.VMEM(rows.shape[1:], jnp.bfloat16),
             pltpu.VMEM(columns.shape[1:], jnp.bfloat16),
             pltpu.VMEM(model.shape, jnp.float32),
@@ -329,57 +362,70 @@
     )(*map(kept_in_hbm, (model, driver, rate, cap, rows, columns, rows_out, columns_out)))
 
 
-def contract(along_own, squares_own, driver_last, model, rows, columns):
+def contract(along_own, squares_own, driver_last, model, rows, columns, *fields):
     half = along_own.shape[0] + 1
+    tail = (TAIL, *model.shape[1:])
+    values = along_own, squares_own, driver_last, model, rows, columns
     return pl.pallas_call(
         contract_kernel,
-        out_shape=pltpu.VMEM((half * TILES * WAVES, LANES), jnp.float32),
-        in_specs=[IN_VMEM] * 6,
-        out_specs=IN_VMEM,
+        out_shape=[
+            pltpu.VMEM((half * TILES * WAVES, LANES), jnp.float32),
+            pltpu.VMEM(tail, jnp.float32),
+        ],
+        in_specs=[IN_VMEM] * 6 + [IN_HBM] * 2,
+        out_specs=[IN_VMEM] * 2,
         scratch_shapes=[
+            pltpu.VMEM(tail, jnp.float32),
             pltpu.VMEM(along_own.shape[1:], jnp.bfloat16),
             pltpu.VMEM(squares_own.shape[1:], jnp.float32),
+            pltpu.SemaphoreType.DMA((2,)),
         ],
         compiler_params=pltpu.CompilerParams(vmem_limit_bytes=4 << 20),
         cost_estimate=estimate(2 * driver_last.size),
         name="contract",
-    )(*map(kept_in_vmem, (along_own, squares_own, driver_last, model, rows, columns)))
+    )(*map(kept_in_vmem, values), *map(kept_in_hbm, fields))
 
 
 def begin(own, rate_rows, cap_rows, model, rows, columns, cells):
-    fields = own.shape[0] // (TILES * WAVES) * GROUP - GROUP
+    group = (GROUP, *model.shape[1:])
     return pl.pallas_call(
         lambda *refs: begin_kernel(cells, *refs),
         out_shape=[
-            pltpu.VMEM((fields, 3 * WAVES, LANES), jnp.bfloat16),
-            pltpu.VMEM((GROUP, *model.shape[1:]), jnp.float32),
+            pltpu.VMEM((GROUP, 3 * WAVES, LANES), jnp.bfloat16),
+            pltpu.VMEM(group, jnp.float32),
+            pltpu.HBM(model.shape, jnp.float32),
         ],
         in_specs=[IN_VMEM] * 6,
-        out_specs=[IN_VMEM] * 2,
+        out_specs=[IN_VMEM, IN_VMEM, IN_HBM],
+        scratch_shapes=[
+            pltpu.VMEM(group, jnp.float32),
+            pltpu.SemaphoreType.DMA((GROUP // 2,)),
+        ],
         compiler_params=pltpu.CompilerParams(vmem_limit_bytes=4 << 20),
-        cost_estimate=estimate(fields * 3 * WAVES * LANES),
+        cost_estimate=estimate(2 * GROUP * model.shape[1] * model.shape[2]),
         name="begin",
     )(*map(kept_in_vmem, (own, rate_rows, cap_rows, model, rows, columns)))
 
 
-def synthesis(stacks, first_nudged, sibling, rate_rows, cap_rows, model, rows, columns, cells):
+def synthesis(begun, stacks, second, sibling, limits, model, model_tail, rows, columns, cells):
     groups = model.shape[0] // GROUP
-    values = stacks, first_nudged, sibling, rate_rows, cap_rows, model, rows, columns
+    values = stacks, second, sibling, *limits, model, model_tail, rows, columns
     return pl.pallas_call(
         lambda *refs: synthesis_kernel(cells, *refs),
         out_shape=pltpu.HBM(model.shape, jnp.float32),
-        in_specs=[IN_VMEM] * 8,
+        in_specs=[IN_VMEM] * 9 + [IN_HBM],
         out_specs=IN_HBM,
+        input_output_aliases={9: 0},
         scratch_shapes=[
-            pltpu.VMEM((groups - 1, GROUP, *model.shape[1:]), jnp.float32),
+            pltpu.VMEM((groups - 2, GROUP, *model.shape[1:]), jnp.float32),
             pltpu.VMEM((2, TILES * LANES, LANES), jnp.float32),
             pltpu.VMEM((2, SLOTS, LANES), jnp.float32),
-            pltpu.SemaphoreType.DMA((groups * (GROUP // CHUNK),)),
+            pltpu.SemaphoreType.DMA(((groups - 1) * (GROUP // CHUNK),)),
         ],
         compiler_params=pltpu.CompilerParams(vmem_limit_bytes=12 << 20),
         cost_estimate=estimate(2 * model.size),
         name="synthesis",
-    )(*map(kept_in_vmem, values))
+    )(*map(kept_in_vmem, values), kept_in_hbm(begun))
 
 
 def estimate(values):
@@ -414,7 +460,11 @@
     )
     model_kept, rate_rows, cap_rows, rows_out_kept, columns_out_kept = kept
     arriving = lax.ppermute(other, "c", swap)
-    mine = contract(along_own, squares_own, driver_last, model_kept, rows_kept, columns_kept)
+    own_lines = along_own, squares_own, driver_last
+    tables_kept = rows_kept, columns_kept
+    mine, model_tail = contract(
+        *own_lines, model_kept, *tables_kept, model_field, driver_field
+    )
 
     def exchanged(value):
         blocks = value.reshape(chips, 1, -1)
@@ -424,9 +474,9 @@
     sibling = lax.ppermute(own, "c", swap)
     cells = float(height * parts_y * width * parts_x)
     limits = rate_rows, cap_rows
-    rest = model_kept, rows_out_kept, columns_out_kept, cells
-    stacks, first_nudged = begin(own, *limits, *rest)
-    return synthesis(stacks, first_nudged, sibling, *limits, *rest)
+    rest = rows_out_kept, columns_out_kept, cells
+    stacks, second, begun = begin(own, *limits, model_kept, *rest)
+    return synthesis(begun, stacks, second, sibling, limits, model_kept, model_tail, *rest)
 
 
 def solution(mesh):

time: 51.5 us -> 52.1 us (1.012)
  Pallas kernels: 11.1 us -> 12.2 us
  waiting for transfers between devices: 0.61 us -> 0.01 us
    pallas_call x1, Pallas kernels: 0.77 us -> 1.68 us  [contract(): pl.pallas_call(contract_kernel, out_shape=[pltpu.VMEM((half * TILES * WAV...]
    pallas_call x1, Pallas kernels: 1.03 us -> 1.65 us  [begin(): pl.pallas_call(lambda *refs: begin_kernel(cells, *refs), out_shape=[pltpu...]
  transfers between devices with their start and end apart: 2 -> 2, of which waited for: 2 -> 0; matrix products, arithmetic and copies ran while one was open for 0% -> 0% of each run, Pallas kernels for 4% -> 6%
where the time goes in v6:
time: 52.1 us; the launch traced here: 51.9 us
  blocking collectives  35.4 us (68%)
  Pallas kernels  12.2 us (23%)
  starting transfers between devices  4.22 us (8%)
    all_to_all x2, blocking collectives, exchanged(): return lax.all_to_all(blocks, CHIP, 0, 0, tiled=True).reshape(value.shape)  35.4 us
    pallas_call x1, Pallas kernels, analysis(): pl.pallas_call(analysis_kernel, out_shape=[pltpu.VMEM((half * TILES * WAV...  5.7 us
    pallas_call x1, Pallas kernels, synthesis(): pl.pallas_call(lambda *refs: synthesis_kernel(cells, *refs), out_shape=pl...  3.15 us
    ppermute x1, starting transfers between devices, per_device(): sibling = lax.ppermute(own, 'c', swap)  2.73 us
    pallas_call x1, Pallas kernels, contract(): pl.pallas_call(contract_kernel, out_shape=[pltpu.VMEM((half * TILES * WAV...  1.68 us
    pallas_call x1, Pallas kernels, begin(): pl.pallas_call(lambda *refs: begin_kernel(cells, *refs), out_shape=[pltpu...  1.65 us
    ppermute x1, starting transfers between devices, per_device(): arriving = lax.ppermute(other, 'c', swap)  1.5 us
  transfers between devices with their start and end apart: 2, of which 0 were waited for; matrix products, arithmetic and copies ran while one was open for 0% of the time, Pallas kernels for 6%

profile of v6, /device:TPU:1, one launch (start us, length us, event | category | flops | bytes accessed | tf_op | source)
XLA Modules:
  0.0 51.9 jit_solution(10199131227574413557)
XLA Ops:
  0.0 5.7 %analysis.1 = (f32[576,128]{1,0:T(8,128)S(1)}, bf16[2,512,256]{2,1,0:T(8,128)(2,1)S(1)}, f32[2,128,128]{2,1,0:T(8,128)S(1)}, f32[6,256,128]{2,1,0:T(8,128)S(1)},...) custom-call(f32[60,256,128]{2,1,0:T(8,128)} %model_hbm.3, ...), custom_call_target="tpu_custom_call" | custom-call | flops 2359296000 | bytes 15728640 | tf_op jit(solution)/shard_map/analysis/pallas_call | solution.py:333
  5.7 1.5 %collective-permute-start = (f32[576,128]{1,0:T(8,128)S(1)}, f32[576,128]{1,0:T(8,128)S(1)}, u32[]{:S(2)}, u32[]{:S(2)}) collective-permute-start(f32[576,128]{1,0:T(8,128)S(1)} %get-tuple-element.28), channel_id=1, source_target_pairs={{0,16},{16,0},{1,17},{17,1},{2,18},{18,2},{3,19},{19,3},{4,20},{20... | collective-permute-start | bytes 884744 | tf_op jit(solution)/shard_map/ppermute | solution.py:462
  7.2 1.7 %contract.1 = (f32[576,128]{1,0:T(8,128)S(1)}, f32[4,256,128]{2,1,0:T(8,128)S(1)}) custom-call(bf16[2,512,256]{2,1,0:T(8,128)(2,1)S(1)} %get-tuple-element.21.along_own, f32[2,128,128]{2,1,0:T(8,128)S(1)} %get-tuple-element.22.squares_own, f32[6,256,128]{2,1,0:T(8,128)S(1)} %get-tuple-element.23.driver_last, ...), custom_call_target="tpu_custom_call" | custom-call | flops 235929600 | bytes 1572864 | tf_op jit(solution)/shard_map/contract/pallas_call | solution.py:369
  8.9 0.0 collective-permute-done
  8.9 21.1 %all_to_all.10 = f32[64,1,1152]{2,1,0:T(1,128)S(1)} all-to-all(f32[64,1,1152]{2,1,0:T(1,128)S(1)} %bitcast.8), channel_id=1, replica_groups=mesh['x'=4,'c'=2,'z'=4,'y'=4] {'x','z','y'}, dimensions={0} | all-to-all | bytes 589824 | tf_op jit(solution)/shard_map/all_to_all | solution.py:471
  30.1 0.1 share.1
  30.1 14.2 %all_to_all.11 = f32[64,1,1152]{2,1,0:T(1,128)S(1)} all-to-all(f32[64,1,1152]{2,1,0:T(1,128)S(1)} %bitcast.7), channel_id=1, replica_groups=mesh['x'=4,'c'=2,'z'=4,'y'=4] {'x','z','y'}, dimensions={0} | all-to-all | bytes 589824 | tf_op jit(solution)/shard_map/all_to_all | solution.py:471
  44.4 2.7 %collective-permute-start.1 = (f32[576,128]{1,0:T(8,128)S(1)}, f32[576,128]{1,0:T(8,128)S(1)}, u32[]{:S(2)}, u32[]{:S(2)}) collective-permute-start(f32[576,128]{1,0:T(8,128)S(1)} %bitcast.4), channel_id=1, source_target_pairs={{0,16},{16,0},{1,17},{17,1},{2,18},{18,2},{3,19},{19,3},{4,20},{20... | collective-permute-start | bytes 884744 | tf_op jit(solution)/shard_map/ppermute | solution.py:474
  47.1 1.6 %begin.1 = (bf16[10,144,128]{2,1,0:T(8,128)(2,1)S(1)}, f32[10,256,128]{2,1,0:T(8,128)S(1)}, f32[60,256,128]{2,1,0:T(8,128)}) custom-call(f32[576,128]{1,0:T(8,128)S(1)} %bitcast.5, f32[96,128]{1,0:T(8,128)S(1)} %get-tuple-element.29.refs_1_.refs_3_, f32[96,128]{1,0:T(8,128)S(1)} %get-tuple-element.30.refs_2_.refs_4_, ...), custom_call_target="tpu_custom_call" | custom-call | flops 393216000 | bytes 2621440 | tf_op jit(solution)/shard_map/begin/pallas_call | solution.py:391
  48.8 0.0 collective-permute-done.1.refs_2_
  48.8 3.1 %synthesis.1 = f32[60,256,128]{2,1,0:T(8,128)} custom-call(bf16[10,144,128]{2,1,0:T(8,128)(2,1)S(1)} %get-tuple-element.33.refs_0_, f32[10,256,128]{2,1,0:T(8,128)S(1)} %get-tuple-element.34.refs_1_, f32[576,128]{1,0:T(8,128)S(1)} %collective-permute-done.1.refs_2_, f32[96,128]{1,0:T(8,128)S(1)} %get-tuple-element.29.refs_1_.refs_3_, ...), custom_call_target="tpu_custom_call", output_to_operand_aliasing={{}: (9, {})} | custom-call | flops 2359296000 | bytes 15728640 | tf_op jit(solution)/shard_map/synthesis/pallas_call | solution.py:413
  (1 shorter events, 0.0 us)
Async XLA Ops:
  5.7 3.2 %collective-permute-start = (f32[576,128]{1,0:T(8,128)S(1)}, f32[576,128]{1,0:T(8,128)S(1)}, u32[]{:S(2)}, u32[]{:S(2)}) collective-permute-start(f32[576,128]{1,0:T(8,128)S(1)} %get-tuple-element.28), channel_id=1, source_target_pairs={{0,16},{16,0},{1,17},{17,1},{2,18},{18,2},{3,19},{19,3},{4,20},{20... | collective-permute-start | bytes 884744 | tf_op jit(solution)/shard_map/ppermute | solution.py:462
  44.4 4.4 %collective-permute-start.1 = (f32[576,128]{1,0:T(8,128)S(1)}, f32[576,128]{1,0:T(8,128)S(1)}, u32[]{:S(2)}, u32[]{:S(2)}) collective-permute-start(f32[576,128]{1,0:T(8,128)S(1)} %bitcast.4), channel_id=1, source_target_pairs={{0,16},{16,0},{1,17},{17,1},{2,18},{18,2},{3,19},{19,3},{4,20},{20... | collective-permute-start | bytes 884744 | tf_op jit(solution)/shard_map/ppermute | solution.py:474

commit v7 on v6

--- a/solution.py
+++ b/solution.py
@@ -15,8 +15,8 @@
 TILES = 4
 LANES = 128
 AHEAD = 3
-TAIL = 4
-CHUNK = 10
+TAIL = 3
+LAST_CHUNKS = (6, 4)
 SLOTS = 16
 CHIP = ("x", "z", "y")
 EPSILON = 1e-06
@@ -246,12 +246,19 @@
     def ordered(step):
         return lax.rem(step + core * half, groups)
 
-    def chunk_out(step, first, size):
+    chunks = {}
+    for step in range(1, groups):
+        first = 0
+        for size in LAST_CHUNKS if step == groups - 1 else (GROUP,):
+            chunks[step, first + size] = first, size, len(chunks)
+            first += size
+
+    def chunk_out(step, end):
+        first, size, place = chunks[step, end]
         span = pl.ds(ordered(step) * GROUP + first, size)
-        place = leaving.at[(step - 1) * (GROUP // CHUNK) + first // CHUNK]
         here = second if step == 1 else nudged.at[step - 2]
         here = here.at[pl.ds(first, size)]
-        return pltpu.make_async_copy(here, nudged_hbm.at[span], place)
+        return pltpu.make_async_copy(here, nudged_hbm.at[span], leaving.at[place])
 
     def prepare(step):
         tiles = tiles_of(sibling, step - half)
@@ -269,8 +276,7 @@
             return model_tail[j - GROUP + TAIL]
         return model[ordered(step) * GROUP + j]
 
-    for first in range(0, GROUP, CHUNK):
-        chunk_out(1, first, CHUNK).start()
+    chunk_out(1, GROUP).start()
     for step in range(2, groups):
         for i in range(0, GROUP, 2):
             pair = [stack_of(step, j) for j in (i, i + 1)]
@@ -278,11 +284,10 @@
             nudged[step - 2, i], nudged[step - 2, i + 1] = nudge_pair(rows, pair, models)
             if i == 0 and step + 1 < groups:
                 prepare(step + 1)
-            if (i + 2) % CHUNK == 0:
-                chunk_out(step, i + 2 - CHUNK, CHUNK).start()
-    for step in range(1, groups):
-        for first in range(0, GROUP, CHUNK):
-            chunk_out(step, first, CHUNK).wait()
+            if (step, i + 2) in chunks:
+                chunk_out(step, i + 2).start()
+    for step, end in chunks:
+        chunk_out(step, end).wait()
 
 
 IN_HBM = pl.BlockSpec(memory_space=pltpu.HBM)
@@ -420,7 +425,7 @@
             pltpu.VMEM((groups - 2, GROUP, *model.shape[1:]), jnp.float32),
             pltpu.VMEM((2, TILES * LANES, LANES), jnp.float32),
             pltpu.VMEM((2, SLOTS, LANES), jnp.float32),
-            pltpu.SemaphoreType.DMA(((groups - 1) * (GROUP // CHUNK),)),
+            pltpu.SemaphoreType.DMA((groups - 2 + len(LAST_CHUNKS),)),
         ],
         compiler_params=pltpu.CompilerParams(vmem_limit_bytes=12 << 20),
         cost_estimate=estimate(2 * model.size),

time: 52.1 us -> 52.1 us (level)
  no operation moved by 1% of the time
where the time goes in v7:
time: 52.1 us; the launch traced here: 51.9 us
  blocking collectives  35.4 us (68%)
  Pallas kernels  12.2 us (23%)
  starting transfers between devices  4.23 us (8%)
    all_to_all x2, blocking collectives, exchanged(): return lax.all_to_all(blocks, CHIP, 0, 0, tiled=True).reshape(value.shape)  35.4 us
    pallas_call x1, Pallas kernels, analysis(): pl.pallas_call(analysis_kernel, out_shape=[pltpu.VMEM((half * TILES * WAV...  5.7 us
    pallas_call x1, Pallas kernels, synthesis(): pl.pallas_call(lambda *refs: synthesis_kernel(cells, *refs), out_shape=pl...  3.28 us
    ppermute x1, starting transfers between devices, per_device(): sibling = lax.ppermute(own, 'c', swap)  2.74 us
    pallas_call x1, Pallas kernels, begin(): pl.pallas_call(lambda *refs: begin_kernel(cells, *refs), out_shape=[pltpu...  1.65 us
    pallas_call x1, Pallas kernels, contract(): pl.pallas_call(contract_kernel, out_shape=[pltpu.VMEM((half * TILES * WAV...  1.55 us
    ppermute x1, starting transfers between devices, per_device(): arriving = lax.ppermute(other, 'c', swap)  1.5 us
  transfers between devices with their start and end apart: 2, of which 0 were waited for; matrix products, arithmetic and copies ran while one was open for 0% of the time, Pallas kernels for 6%

profile of v7, /device:TPU:1, one launch (start us, length us, event | category | flops | bytes accessed | tf_op | source)
XLA Modules:
  0.0 51.9 jit_solution(17484325144506438735)
XLA Ops:
  0.0 5.7 %analysis.1 = (f32[576,128]{1,0:T(8,128)S(1)}, bf16[2,512,256]{2,1,0:T(8,128)(2,1)S(1)}, f32[2,128,128]{2,1,0:T(8,128)S(1)}, f32[7,256,128]{2,1,0:T(8,128)S(1)},...) custom-call(f32[60,256,128]{2,1,0:T(8,128)} %model_hbm.3, ...), custom_call_target="tpu_custom_call" | custom-call | flops 2359296000 | bytes 15728640 | tf_op jit(solution)/shard_map/analysis/pallas_call | solution.py:338
  5.7 1.5 %collective-permute-start = (f32[576,128]{1,0:T(8,128)S(1)}, f32[576,128]{1,0:T(8,128)S(1)}, u32[]{:S(2)}, u32[]{:S(2)}) collective-permute-start(f32[576,128]{1,0:T(8,128)S(1)} %get-tuple-element.28), channel_id=1, source_target_pairs={{0,16},{16,0},{1,17},{17,1},{2,18},{18,2},{3,19},{19,3},{4,20},{20... | collective-permute-start | bytes 884744 | tf_op jit(solution)/shard_map/ppermute | solution.py:467
  7.2 1.6 %contract.1 = (f32[576,128]{1,0:T(8,128)S(1)}, f32[3,256,128]{2,1,0:T(8,128)S(1)}) custom-call(bf16[2,512,256]{2,1,0:T(8,128)(2,1)S(1)} %get-tuple-element.21.along_own, f32[2,128,128]{2,1,0:T(8,128)S(1)} %get-tuple-element.22.squares_own, f32[7,256,128]{2,1,0:T(8,128)S(1)} %get-tuple-element.23.driver_last, ...), custom_call_target="tpu_custom_call" | custom-call | flops 275251200 | bytes 1835008 | tf_op jit(solution)/shard_map/contract/pallas_call | solution.py:374
  8.8 0.0 collective-permute-done
  8.8 21.1 %all_to_all.10 = f32[64,1,1152]{2,1,0:T(1,128)S(1)} all-to-all(f32[64,1,1152]{2,1,0:T(1,128)S(1)} %bitcast.8), channel_id=1, replica_groups=mesh['x'=4,'c'=2,'z'=4,'y'=4] {'x','z','y'}, dimensions={0} | all-to-all | bytes 589824 | tf_op jit(solution)/shard_map/all_to_all | solution.py:476
  29.9 0.1 share.1
  30.0 14.2 %all_to_all.11 = f32[64,1,1152]{2,1,0:T(1,128)S(1)} all-to-all(f32[64,1,1152]{2,1,0:T(1,128)S(1)} %bitcast.7), channel_id=1, replica_groups=mesh['x'=4,'c'=2,'z'=4,'y'=4] {'x','z','y'}, dimensions={0} | all-to-all | bytes 589824 | tf_op jit(solution)/shard_map/all_to_all | solution.py:476
  44.2 2.7 %collective-permute-start.1 = (f32[576,128]{1,0:T(8,128)S(1)}, f32[576,128]{1,0:T(8,128)S(1)}, u32[]{:S(2)}, u32[]{:S(2)}) collective-permute-start(f32[576,128]{1,0:T(8,128)S(1)} %bitcast.4), channel_id=1, source_target_pairs={{0,16},{16,0},{1,17},{17,1},{2,18},{18,2},{3,19},{19,3},{4,20},{20... | collective-permute-start | bytes 884744 | tf_op jit(solution)/shard_map/ppermute | solution.py:479
  47.0 1.6 %begin.1 = (bf16[10,144,128]{2,1,0:T(8,128)(2,1)S(1)}, f32[10,256,128]{2,1,0:T(8,128)S(1)}, f32[60,256,128]{2,1,0:T(8,128)}) custom-call(f32[576,128]{1,0:T(8,128)S(1)} %bitcast.5, f32[96,128]{1,0:T(8,128)S(1)} %get-tuple-element.29.refs_1_.refs_3_, f32[96,128]{1,0:T(8,128)S(1)} %get-tuple-element.30.refs_2_.refs_4_, ...), custom_call_target="tpu_custom_call" | custom-call | flops 393216000 | bytes 2621440 | tf_op jit(solution)/shard_map/begin/pallas_call | solution.py:396
  48.6 0.0 collective-permute-done.1.refs_2_
  48.6 3.3 %synthesis.1 = f32[60,256,128]{2,1,0:T(8,128)} custom-call(bf16[10,144,128]{2,1,0:T(8,128)(2,1)S(1)} %get-tuple-element.33.refs_0_, f32[10,256,128]{2,1,0:T(8,128)S(1)} %get-tuple-element.34.refs_1_, f32[576,128]{1,0:T(8,128)S(1)} %collective-permute-done.1.refs_2_, f32[96,128]{1,0:T(8,128)S(1)} %get-tuple-element.29.refs_1_.refs_3_, ...), custom_call_target="tpu_custom_call", output_to_operand_aliasing={{}: (9, {})} | custom-call | flops 2359296000 | bytes 15728640 | tf_op jit(solution)/shard_map/synthesis/pallas_call | solution.py:418
  (1 shorter events, 0.0 us)
Async XLA Ops:
  5.7 3.1 %collective-permute-start = (f32[576,128]{1,0:T(8,128)S(1)}, f32[576,128]{1,0:T(8,128)S(1)}, u32[]{:S(2)}, u32[]{:S(2)}) collective-permute-start(f32[576,128]{1,0:T(8,128)S(1)} %get-tuple-element.28), channel_id=1, source_target_pairs={{0,16},{16,0},{1,17},{17,1},{2,18},{18,2},{3,19},{19,3},{4,20},{20... | collective-permute-start | bytes 884744 | tf_op jit(solution)/shard_map/ppermute | solution.py:467
  44.2 4.4 %collective-permute-start.1 = (f32[576,128]{1,0:T(8,128)S(1)}, f32[576,128]{1,0:T(8,128)S(1)}, u32[]{:S(2)}, u32[]{:S(2)}) collective-permute-start(f32[576,128]{1,0:T(8,128)S(1)} %bitcast.4), channel_id=1, source_target_pairs={{0,16},{16,0},{1,17},{17,1},{2,18},{18,2},{3,19},{19,3},{4,20},{20... | collective-permute-start | bytes 884744 | tf_op jit(solution)/shard_map/ppermute | solution.py:479

commit v8 on v5

--- a/solution.py
+++ b/solution.py
@@ -15,6 +15,7 @@
 TILES = 4
 LANES = 128
 AHEAD = 3
+TAIL = 3
 CHUNK = 10
 SLOTS = 16
 CHIP = ("x", "z", "y")
@@ -109,8 +110,9 @@
         return along_own.at[step - half], squares_own.at[step - half]
 
     def fetch(step):
-        span = pl.ds(ordered(step) * GROUP, GROUP)
-        kept = driver_last if step == groups - 1 else driver.at[pl.ds(step * GROUP, GROUP)]
+        last = step == groups - 1
+        span = pl.ds(ordered(step) * GROUP, GROUP - TAIL if last else GROUP)
+        kept = driver_last if last else driver.at[pl.ds(step * GROUP, GROUP)]
         return [
             pltpu.make_async_copy(model_hbm.at[span], model.at[span], arrived.at[0, step]),
             pltpu.make_async_copy(driver_hbm.at[span], kept, arrived.at[1, step]),
@@ -145,18 +147,31 @@
 
 
 def contract_kernel(
-    along_own, squares_own, driver_last, model, rows, columns, mine, along_y, squares
+    along_own, squares_own, driver_last, model, rows, columns, model_hbm, driver_hbm,
+    mine, model_tail, driver_tail, along_y, squares, arrived,
 ):
     core = lax.axis_index("c")
     groups = model.shape[0] // GROUP
     half = groups // 2
     base = lax.rem(groups - 1 + (1 - core) * half, groups) * GROUP
+    span = pl.ds(base + GROUP - TAIL, TAIL)
+    copies = [
+        pltpu.make_async_copy(model_hbm.at[span], model_tail, arrived.at[0]),
+        pltpu.make_async_copy(driver_hbm.at[span], driver_tail, arrived.at[1]),
+    ]
+    for copy in copies:
+        copy.start()
     clear_spare(along_y, squares)
-    for i in range(GROUP):
+    for i in range(GROUP - TAIL):
         first_contraction(driver_last[i] - model[base + i], rows, along_y, squares, i)
-        if i % 3 == 2 and i // 3 < half - 1:
-            step = i // 3
+        if i % 2 and i // 2 < half - 1:
+            step = i // 2
             second_contraction(columns, along_own.at[step], squares_own.at[step], mine, step)
+    for copy in copies:
+        copy.wait()
+    for i in range(TAIL):
+        difference = driver_tail[i] - model_tail[i]
+        first_contraction(difference, rows, along_y, squares, GROUP - TAIL + i)
     second_contraction(columns, along_y, squares, mine, half - 1)
 
 
@@ -208,8 +223,8 @@
 
 
 def synthesis_kernel(
-    cells, stacks, first_nudged, sibling, rate_rows, cap_rows, model, rows, columns, nudged_hbm,
-    nudged, along_x, strength, leaving,
+    cells, stacks, first_nudged, sibling, rate_rows, cap_rows, model, model_tail, rows, columns,
+    nudged_hbm, nudged, along_x, strength, leaving,
 ):
     core = lax.axis_index("c")
     groups = model.shape[0] // GROUP
@@ -236,12 +251,17 @@
         lines = along_x[step % 2, j * WAVES : (j + 1) * WAVES, :]
         return stacked(lines, strength[step % 2, j : j + 1, :])
 
+    def model_of(step, j):
+        if step == half - 1 and j >= GROUP - TAIL:
+            return model_tail[j - GROUP + TAIL]
+        return model[ordered(step) * GROUP + j]
+
     for first in range(0, GROUP, CHUNK):
         chunk_out(0, first, CHUNK).start()
     for step in range(1, groups):
         for i in range(0, GROUP, 2):
             pair = [stack_of(step, j) for j in (i, i + 1)]
-            models = [model[ordered(step) * GROUP + j] for j in (i, i + 1)]
+            models = [model_of(step, j) for j in (i, i + 1)]
             nudged[step - 1, i], nudged[step - 1, i + 1] = nudge_pair(rows, pair, models)
             if i == 0 and half <= step + 1 < groups:
                 prepare(step + 1)
@@ -303,7 +323,7 @@
             pltpu.VMEM((half * TILES * WAVES, LANES), jnp.float32),
             pltpu.VMEM((half - 1, *lines), jnp.bfloat16),
             pltpu.VMEM((half - 1, *sums), jnp.float32),
-            pltpu.VMEM((GROUP, *model.shape[1:]), jnp.float32),
+            pltpu.VMEM((GROUP - TAIL, *model.shape[1:]), jnp.float32),
             pltpu.VMEM(rows.shape[1:], jnp.bfloat16),
             pltpu.VMEM(columns.shape[1:], jnp.bfloat16),
             pltpu.VMEM(model.shape, jnp.float32),
@@ -329,21 +349,28 @@
     )(*map(kept_in_hbm, (model, driver, rate, cap, rows, columns, rows_out, columns_out)))
 
 
-def contract(along_own, squares_own, driver_last, model, rows, columns):
+def contract(along_own, squares_own, driver_last, model, rows, columns, *fields):
     half = along_own.shape[0] + 1
+    tail = (TAIL, *model.shape[1:])
+    values = along_own, squares_own, driver_last, model, rows, columns
     return pl.pallas_call(
         contract_kernel,
-        out_shape=pltpu.VMEM((half * TILES * WAVES, LANES), jnp.float32),
-        in_specs=[IN_VMEM] * 6,
-        out_specs=IN_VMEM,
+        out_shape=[
+            pltpu.VMEM((half * TILES * WAVES, LANES), jnp.float32),
+            pltpu.VMEM(tail, jnp.float32),
+        ],
+        in_specs=[IN_VMEM] * 6 + [IN_HBM] * 2,
+        out_specs=[IN_VMEM] * 2,
         scratch_shapes=[
+            pltpu.VMEM(tail, jnp.float32),
             pltpu.VMEM(along_own.shape[1:], jnp.bfloat16),
             pltpu.VMEM(squares_own.shape[1:], jnp.float32),
+            pltpu.SemaphoreType.DMA((2,)),
         ],
         compiler_params=pltpu.CompilerParams(vmem_limit_bytes=4 << 20),
         cost_estimate=estimate(2 * driver_last.size),
         name="contract",
-    )(*map(kept_in_vmem, (along_own, squares_own, driver_last, model, rows, columns)))
+    )(*map(kept_in_vmem, values), *map(kept_in_hbm, fields))
 
 
 def begin(own, rate_rows, cap_rows, model, rows, columns, cells):
@@ -362,13 +389,13 @@
     )(*map(kept_in_vmem, (own, rate_rows, cap_rows, model, rows, columns)))
 
 
-def synthesis(stacks, first_nudged, sibling, rate_rows, cap_rows, model, rows, columns, cells):
+def synthesis(stacks, first_nudged, sibling, limits, model, model_tail, rows, columns, cells):
     groups = model.shape[0] // GROUP
-    values = stacks, first_nudged, sibling, rate_rows, cap_rows, model, rows, columns
+    values = stacks, first_nudged, sibling, *limits, model, model_tail, rows, columns
     return pl.pallas_call(
         lambda *refs: synthesis_kernel(cells, *refs),
         out_shape=pltpu.HBM(model.shape, jnp.float32),
-        in_specs=[IN_VMEM] * 8,
+        in_specs=[IN_VMEM] * 9,
         out_specs=IN_HBM,
         scratch_shapes=[
             pltpu.VMEM((groups - 1, GROUP, *model.shape[1:]), jnp.float32),
@@ -414,7 +441,11 @@
     )
     model_kept, rate_rows, cap_rows, rows_out_kept, columns_out_kept = kept
     arriving = lax.ppermute(other, "c", swap)
-    mine = contract(along_own, squares_own, driver_last, model_kept, rows_kept, columns_kept)
+    own_lines = along_own, squares_own, driver_last
+    tables_kept = rows_kept, columns_kept
+    mine, model_tail = contract(
+        *own_lines, model_kept, *tables_kept, model_field, driver_field
+    )
 
     def exchanged(value):
         blocks = value.reshape(chips, 1, -1)
@@ -424,9 +455,9 @@
     sibling = lax.ppermute(own, "c", swap)
     cells = float(height * parts_y * width * parts_x)
     limits = rate_rows, cap_rows
-    rest = model_kept, rows_out_kept, columns_out_kept, cells
-    stacks, first_nudged = begin(own, *limits, *rest)
-    return synthesis(stacks, first_nudged, sibling, *limits, *rest)
+    rest = rows_out_kept, columns_out_kept, cells
+    stacks, first_nudged = begin(own, *limits, model_kept, *rest)
+    return synthesis(stacks, first_nudged, sibling, limits, model_kept, model_tail, *rest)
 
 
 def solution(mesh):

time: 51.5 us -> 51.6 us (level)
    pallas_call x1, Pallas kernels: 0.77 us -> 1.55 us  [contract(): pl.pallas_call(contract_kernel, out_shape=[pltpu.VMEM((half * TILES * WAV...]
  transfers between devices with their start and end apart: 2 -> 2, of which waited for: 2 -> 1; matrix products, arithmetic and copies ran while one was open for 0% -> 0% of each run, Pallas kernels for 4% -> 5%
where the time goes in v8:
time: 51.6 us; the launch traced here: 51.4 us
  blocking collectives  35.4 us (69%)
  Pallas kernels  11.6 us (22%)
  starting transfers between devices  4.23 us (8%)
    all_to_all x2, blocking collectives, exchanged(): return lax.all_to_all(blocks, CHIP, 0, 0, tiled=True).reshape(value.shape)  35.4 us
    pallas_call x1, Pallas kernels, analysis(): pl.pallas_call(analysis_kernel, out_shape=[pltpu.VMEM((half * TILES * WAV...  5.7 us
    pallas_call x1, Pallas kernels, synthesis(): pl.pallas_call(lambda *refs: synthesis_kernel(cells, *refs), out_shape=pl...  3.26 us
    ppermute x1, starting transfers between devices, per_device(): sibling = lax.ppermute(own, 'c', swap)  2.74 us
    pallas_call x1, Pallas kernels, contract(): pl.pallas_call(contract_kernel, out_shape=[pltpu.VMEM((half * TILES * WAV...  1.55 us
    ppermute x1, starting transfers between devices, per_device(): arriving = lax.ppermute(other, 'c', swap)  1.5 us
    pallas_call x1, Pallas kernels, begin(): pl.pallas_call(lambda *refs: begin_kernel(cells, *refs), out_shape=[pltpu...  1.03 us
  transfers between devices with their start and end apart: 2, of which 1 were waited for; matrix products, arithmetic and copies ran while one was open for 0% of the time, Pallas kernels for 5%

profile of v8, /device:TPU:1, one launch (start us, length us, event | category | flops | bytes accessed | tf_op | source)
XLA Modules:
  0.0 51.4 jit_solution(17091507916886240330)
XLA Ops:
  0.0 5.7 %analysis.1 = (f32[576,128]{1,0:T(8,128)S(1)}, bf16[2,512,256]{2,1,0:T(8,128)(2,1)S(1)}, f32[2,128,128]{2,1,0:T(8,128)S(1)}, f32[7,256,128]{2,1,0:T(8,128)S(1)},...) custom-call(f32[60,256,128]{2,1,0:T(8,128)} %model_hbm.3, ...), custom_call_target="tpu_custom_call" | custom-call | flops 2359296000 | bytes 15728640 | tf_op jit(solution)/shard_map/analysis/pallas_call | solution.py:320
  5.7 1.5 %collective-permute-start = (f32[576,128]{1,0:T(8,128)S(1)}, f32[576,128]{1,0:T(8,128)S(1)}, u32[]{:S(2)}, u32[]{:S(2)}) collective-permute-start(f32[576,128]{1,0:T(8,128)S(1)} %get-tuple-element.27), channel_id=1, source_target_pairs={{0,16},{16,0},{1,17},{17,1},{2,18},{18,2},{3,19},{19,3},{4,20},{20... | collective-permute-start | bytes 884744 | tf_op jit(solution)/shard_map/ppermute | solution.py:443
  7.2 1.6 %contract.1 = (f32[576,128]{1,0:T(8,128)S(1)}, f32[3,256,128]{2,1,0:T(8,128)S(1)}) custom-call(bf16[2,512,256]{2,1,0:T(8,128)(2,1)S(1)} %get-tuple-element.20.along_own, f32[2,128,128]{2,1,0:T(8,128)S(1)} %get-tuple-element.21.squares_own, f32[7,256,128]{2,1,0:T(8,128)S(1)} %get-tuple-element.22.driver_last, ...), custom_call_target="tpu_custom_call" | custom-call | flops 275251200 | bytes 1835008 | tf_op jit(solution)/shard_map/contract/pallas_call | solution.py:356
  8.8 0.0 collective-permute-done
  8.8 21.1 %all_to_all.10 = f32[64,1,1152]{2,1,0:T(1,128)S(1)} all-to-all(f32[64,1,1152]{2,1,0:T(1,128)S(1)} %bitcast.8), channel_id=1, replica_groups=mesh['x'=4,'c'=2,'z'=4,'y'=4] {'x','z','y'}, dimensions={0} | all-to-all | bytes 589824 | tf_op jit(solution)/shard_map/all_to_all | solution.py:452
  29.9 0.1 share.1
  30.0 14.2 %all_to_all.11 = f32[64,1,1152]{2,1,0:T(1,128)S(1)} all-to-all(f32[64,1,1152]{2,1,0:T(1,128)S(1)} %bitcast.7), channel_id=1, replica_groups=mesh['x'=4,'c'=2,'z'=4,'y'=4] {'x','z','y'}, dimensions={0} | all-to-all | bytes 589824 | tf_op jit(solution)/shard_map/all_to_all | solution.py:452
  44.2 2.7 %collective-permute-start.1 = (f32[576,128]{1,0:T(8,128)S(1)}, f32[576,128]{1,0:T(8,128)S(1)}, u32[]{:S(2)}, u32[]{:S(2)}) collective-permute-start(f32[576,128]{1,0:T(8,128)S(1)} %bitcast.4), channel_id=1, source_target_pairs={{0,16},{16,0},{1,17},{17,1},{2,18},{18,2},{3,19},{19,3},{4,20},{20... | collective-permute-start | bytes 884744 | tf_op jit(solution)/shard_map/ppermute | solution.py:455
  47.0 1.0 %begin.1 = (bf16[20,144,128]{2,1,0:T(8,128)(2,1)S(1)}, f32[10,256,128]{2,1,0:T(8,128)S(1)}) custom-call(f32[576,128]{1,0:T(8,128)S(1)} %bitcast.5, f32[96,128]{1,0:T(8,128)S(1)} %get-tuple-element.28.refs_1_.refs_3_, f32[96,128]{1,0:T(8,128)S(1)} %get-tuple-element.29.refs_2_.refs_4_, f32[60,256,128]{2,1,0:T(8,128)S(1)} %get-tuple-element.23.model.refs_3_.refs_5_, ...), custom_call_target="tpu_custom_call" | custom-call | flops 221184000 | bytes 1474560 | tf_op jit(solution)/shard_map/begin/pallas_call | solution.py:378
  48.0 0.2 collective-permute-done.1.refs_2_
  48.2 3.3 %synthesis.1 = f32[60,256,128]{2,1,0:T(8,128)} custom-call(bf16[20,144,128]{2,1,0:T(8,128)(2,1)S(1)} %get-tuple-element.32.refs_0_, f32[10,256,128]{2,1,0:T(8,128)S(1)} %get-tuple-element.33.refs_1_, f32[576,128]{1,0:T(8,128)S(1)} %collective-permute-done.1.refs_2_, f32[96,128]{1,0:T(8,128)S(1)} %get-tuple-element.28.refs_1_.refs_3_, ...), custom_call_target="tpu_custom_call" | custom-call | flops 2359296000 | bytes 15728640 | tf_op jit(solution)/shard_map/synthesis/pallas_call | solution.py:395
  (1 shorter events, 0.0 us)
Async XLA Ops:
  5.7 3.1 %collective-permute-start = (f32[576,128]{1,0:T(8,128)S(1)}, f32[576,128]{1,0:T(8,128)S(1)}, u32[]{:S(2)}, u32[]{:S(2)}) collective-permute-start(f32[576,128]{1,0:T(8,128)S(1)} %get-tuple-element.27), channel_id=1, source_target_pairs={{0,16},{16,0},{1,17},{17,1},{2,18},{18,2},{3,19},{19,3},{4,20},{20... | collective-permute-start | bytes 884744 | tf_op jit(solution)/shard_map/ppermute | solution.py:443
  44.2 3.9 %collective-permute-start.1 = (f32[576,128]{1,0:T(8,128)S(1)}, f32[576,128]{1,0:T(8,128)S(1)}, u32[]{:S(2)}, u32[]{:S(2)}) collective-permute-start(f32[576,128]{1,0:T(8,128)S(1)} %bitcast.4), channel_id=1, source_target_pairs={{0,16},{16,0},{1,17},{17,1},{2,18},{18,2},{3,19},{19,3},{4,20},{20... | collective-permute-start | bytes 884744 | tf_op jit(solution)/shard_map/ppermute | solution.py:455

commit v9 on v5

--- a/solution.py
+++ b/solution.py
@@ -190,21 +190,20 @@
 def begin_kernel(cells, own, rate_rows, cap_rows, model, rows, columns, stacks, first_nudged):
     groups = own.shape[0] // (TILES * WAVES)
     base = lax.axis_index("c") * groups
-    first = []
     for step in range(groups):
         tiles = tiles_of(own, step)
         strength = strengths(cells, tiles, rate_rows, cap_rows, base + step)
         lines = synthesized(tiles, columns)
-        for j in range(GROUP):
-            stack = stacked(lines[j * WAVES : (j + 1) * WAVES, :], strength[j : j + 1, :])
-            if step > 0:
-                stacks[(step - 1) * GROUP + j] = stack
+        for i in range(0, GROUP, 2):
+            pair = [
+                stacked(lines[j * WAVES : (j + 1) * WAVES, :], strength[j : j + 1, :])
+                for j in (i, i + 1)
+            ]
+            if step == groups - 1:
+                stacks[i], stacks[i + 1] = pair
                 continue
-            first.append(stack)
-            if j % 2:
-                models = [model[base * GROUP + k] for k in (j - 1, j)]
-                pair = nudge_pair(rows, first[j - 1 : j + 1], models)
-                first_nudged[j - 1], first_nudged[j] = pair
+            models = [model[(base + step) * GROUP + j] for j in (i, i + 1)]
+            first_nudged[step, i], first_nudged[step, i + 1] = nudge_pair(rows, pair, models)
 
 
 def synthesis_kernel(
@@ -221,7 +220,7 @@
     def chunk_out(step, first, size):
         span = pl.ds(ordered(step) * GROUP + first, size)
         place = leaving.at[step * (GROUP // CHUNK) + first // CHUNK]
-        here = first_nudged if step == 0 else nudged.at[step - 1]
+        here = first_nudged.at[step] if step < half - 1 else nudged.at[step - half + 1]
         here = here.at[pl.ds(first, size)]
         return pltpu.make_async_copy(here, nudged_hbm.at[span], place)
 
@@ -232,17 +231,19 @@
 
     def stack_of(step, j):
         if step < half:
-            return stacks[(step - 1) * GROUP + j]
+            return stacks[j]
         lines = along_x[step % 2, j * WAVES : (j + 1) * WAVES, :]
         return stacked(lines, strength[step % 2, j : j + 1, :])
 
-    for first in range(0, GROUP, CHUNK):
-        chunk_out(0, first, CHUNK).start()
-    for step in range(1, groups):
+    for step in range(half - 1):
+        for first in range(0, GROUP, CHUNK):
+            chunk_out(step, first, CHUNK).start()
+    for step in range(half - 1, groups):
         for i in range(0, GROUP, 2):
             pair = [stack_of(step, j) for j in (i, i + 1)]
             models = [model[ordered(step) * GROUP + j] for j in (i, i + 1)]
-            nudged[step - 1, i], nudged[step - 1, i + 1] = nudge_pair(rows, pair, models)
+            place = step - half + 1
+            nudged[place, i], nudged[place, i + 1] = nudge_pair(rows, pair, models)
             if i == 0 and half <= step + 1 < groups:
                 prepare(step + 1)
             if (i + 2) % CHUNK == 0:
@@ -347,17 +348,17 @@
 
 
 def begin(own, rate_rows, cap_rows, model, rows, columns, cells):
-    fields = own.shape[0] // (TILES * WAVES) * GROUP - GROUP
+    groups = own.shape[0] // (TILES * WAVES)
     return pl.pallas_call(
         lambda *refs: begin_kernel(cells, *refs),
         out_shape=[
-            pltpu.VMEM((fields, 3 * WAVES, LANES), jnp.bfloat16),
-            pltpu.VMEM((GROUP, *model.shape[1:]), jnp.float32),
+            pltpu.VMEM((GROUP, 3 * WAVES, LANES), jnp.bfloat16),
+            pltpu.VMEM((groups - 1, GROUP, *model.shape[1:]), jnp.float32),
         ],
         in_specs=[IN_VMEM] * 6,
         out_specs=[IN_VMEM] * 2,
         compiler_params=pltpu.CompilerParams(vmem_limit_bytes=4 << 20),
-        cost_estimate=estimate(fields * 3 * WAVES * LANES),
+        cost_estimate=estimate(groups * GROUP * 3 * WAVES * LANES),
         name="begin",
     )(*map(kept_in_vmem, (own, rate_rows, cap_rows, model, rows, columns)))
 
@@ -371,7 +372,7 @@
         in_specs=[IN_VMEM] * 8,
         out_specs=IN_HBM,
         scratch_shapes=[
-            pltpu.VMEM((groups - 1, GROUP, *model.shape[1:]), jnp.float32),
+            pltpu.VMEM((groups // 2 + 1, GROUP, *model.shape[1:]), jnp.float32),
             pltpu.VMEM((2, TILES * LANES, LANES), jnp.float32),
             pltpu.VMEM((2, SLOTS, LANES), jnp.float32),
             pltpu.SemaphoreType.DMA((groups * (GROUP // CHUNK),)),

time: 51.5 us -> 52.1 us (1.012)
  Pallas kernels: 11.1 us -> 11.9 us
  transfers between devices with their start and end apart: 2 -> 2, of which waited for: 2 -> 1; matrix products, arithmetic and copies ran while one was open for 0% -> 0% of each run, Pallas kernels for 4% -> 4%
where the time goes in v9:
time: 52.1 us; the launch traced here: 52 us
  blocking collectives  34.9 us (67%)
  Pallas kernels  11.9 us (23%)
  starting transfers between devices  4.67 us (9%)
    all_to_all x2, blocking collectives, exchanged(): return lax.all_to_all(blocks, CHIP, 0, 0, tiled=True).reshape(value.shape)  34.9 us
    pallas_call x1, Pallas kernels, analysis(): pl.pallas_call(analysis_kernel, out_shape=[pltpu.VMEM((half * TILES * WAV...  5.94 us
    pallas_call x1, Pallas kernels, synthesis(): pl.pallas_call(lambda *refs: synthesis_kernel(cells, *refs), out_shape=pl...  3.58 us
    ppermute x1, starting transfers between devices, per_device(): sibling = lax.ppermute(own, 'c', swap)  3.17 us
    pallas_call x1, Pallas kernels, begin(): pl.pallas_call(lambda *refs: begin_kernel(cells, *refs), out_shape=[pltpu...  1.51 us
    ppermute x1, starting transfers between devices, per_device(): arriving = lax.ppermute(other, 'c', swap)  1.5 us
  transfers between devices with their start and end apart: 2, of which 1 were waited for; matrix products, arithmetic and copies ran while one was open for 0% of the time, Pallas kernels for 4%

profile of v9, /device:TPU:1, one launch (start us, length us, event | category | flops | bytes accessed | tf_op | source)
XLA Modules:
  0.0 52.0 jit_solution(2692376920949398929)
XLA Ops:
  0.0 5.9 %analysis.1 = (f32[576,128]{1,0:T(8,128)S(1)}, bf16[2,512,256]{2,1,0:T(8,128)(2,1)S(1)}, f32[2,128,128]{2,1,0:T(8,128)S(1)}, f32[10,256,128]{2,1,0:T(8,128)S(1)}...) custom-call(f32[60,256,128]{2,1,0:T(8,128)} %model_hbm.1, ...), custom_call_target="tpu_custom_call" | custom-call | flops 2359296000 | bytes 15728640 | tf_op jit(solution)/shard_map/analysis/pallas_call | solution.py:301
  5.9 1.5 %collective-permute-start = (f32[576,128]{1,0:T(8,128)S(1)}, f32[576,128]{1,0:T(8,128)S(1)}, u32[]{:S(2)}, u32[]{:S(2)}) collective-permute-start(f32[576,128]{1,0:T(8,128)S(1)} %get-tuple-element.24), channel_id=1, source_target_pairs={{0,16},{16,0},{1,17},{17,1},{2,18},{18,2},{3,19},{19,3},{4,20},{20... | collective-permute-start | bytes 884744 | tf_op jit(solution)/shard_map/ppermute | solution.py:417
  7.4 0.8 %contract.1 = f32[576,128]{1,0:T(8,128)S(1)} custom-call(bf16[2,512,256]{2,1,0:T(8,128)(2,1)S(1)} %get-tuple-element.18.along_own, f32[2,128,128]{2,1,0:T(8,128)S(1)} %get-tuple-element.19.squares_own, f32[10,256,128]{2,1,0:T(8,128)S(1)} %get-tuple-element.20.driver_last, f32[60,256,128]{2,1,0:T(8,128)S(1)} %get-tuple-element.21.model.refs_3_.refs_5_, ...), custom_call_target="tpu_custom_call" | custom-call | flops 393216000 | bytes 2621440 | tf_op jit(solution)/shard_map/contract/pallas_call | solution.py:335
  8.2 0.4 collective-permute-done
  8.7 20.9 %all_to_all.10 = f32[64,1,1152]{2,1,0:T(1,128)S(1)} all-to-all(f32[64,1,1152]{2,1,0:T(1,128)S(1)} %bitcast.8), channel_id=1, replica_groups=mesh['x'=4,'c'=2,'z'=4,'y'=4] {'x','z','y'}, dimensions={0} | all-to-all | bytes 589824 | tf_op jit(solution)/shard_map/all_to_all | solution.py:422
  29.6 0.1 share.1
  29.7 14.0 %all_to_all.11 = f32[64,1,1152]{2,1,0:T(1,128)S(1)} all-to-all(f32[64,1,1152]{2,1,0:T(1,128)S(1)} %bitcast.7), channel_id=1, replica_groups=mesh['x'=4,'c'=2,'z'=4,'y'=4] {'x','z','y'}, dimensions={0} | all-to-all | bytes 589824 | tf_op jit(solution)/shard_map/all_to_all | solution.py:422
  43.7 3.2 %collective-permute-start.1 = (f32[576,128]{1,0:T(8,128)S(1)}, f32[576,128]{1,0:T(8,128)S(1)}, u32[]{:S(2)}, u32[]{:S(2)}) collective-permute-start(f32[576,128]{1,0:T(8,128)S(1)} %bitcast.4), channel_id=1, source_target_pairs={{0,16},{16,0},{1,17},{17,1},{2,18},{18,2},{3,19},{19,3},{4,20},{20... | collective-permute-start | bytes 884744 | tf_op jit(solution)/shard_map/ppermute | solution.py:425
  46.8 1.5 %begin.1 = (bf16[10,144,128]{2,1,0:T(8,128)(2,1)S(1)}, f32[2,10,256,128]{3,2,1,0:T(8,128)S(1)}) custom-call(f32[576,128]{1,0:T(8,128)S(1)} %bitcast.5, f32[96,128]{1,0:T(8,128)S(1)} %get-tuple-element.25.refs_1_.refs_3_, f32[96,128]{1,0:T(8,128)S(1)} %get-tuple-element.26.refs_2_.refs_4_, f32[60,256,128]{2,1,0:T(8,128)S(1)} %get-tuple-element.21.model.refs_3_.refs_5_, ...), custom_call_target="tpu_custom_call" | custom-call | flops 331776000 | bytes 2211840 | tf_op jit(solution)/shard_map/begin/pallas_call | solution.py:352
  48.4 0.0 collective-permute-done.1.refs_2_
  48.4 3.6 %synthesis.1 = f32[60,256,128]{2,1,0:T(8,128)} custom-call(bf16[10,144,128]{2,1,0:T(8,128)(2,1)S(1)} %get-tuple-element.29.refs_0_, f32[2,10,256,128]{3,2,1,0:T(8,128)S(1)} %get-tuple-element.30.refs_1_, f32[576,128]{1,0:T(8,128)S(1)} %collective-permute-done.1.refs_2_, f32[96,128]{1,0:T(8,128)S(1)} %get-tuple-element.25.refs_1_.refs_3_, ...), custom_call_target="tpu_custom_call" | custom-call | flops 2359296000 | bytes 15728640 | tf_op jit(solution)/shard_map/synthesis/pallas_call | solution.py:369
  (1 shorter events, 0.0 us)
Async XLA Ops:
  5.9 2.7 %collective-permute-start = (f32[576,128]{1,0:T(8,128)S(1)}, f32[576,128]{1,0:T(8,128)S(1)}, u32[]{:S(2)}, u32[]{:S(2)}) collective-permute-start(f32[576,128]{1,0:T(8,128)S(1)} %get-tuple-element.24), channel_id=1, source_target_pairs={{0,16},{16,0},{1,17},{17,1},{2,18},{18,2},{3,19},{19,3},{4,20},{20... | collective-permute-start | bytes 884744 | tf_op jit(solution)/shard_map/ppermute | solution.py:417
  43.7 4.7 %collective-permute-start.1 = (f32[576,128]{1,0:T(8,128)S(1)}, f32[576,128]{1,0:T(8,128)S(1)}, u32[]{:S(2)}, u32[]{:S(2)}) collective-permute-start(f32[576,128]{1,0:T(8,128)S(1)} %bitcast.4), channel_id=1, source_target_pairs={{0,16},{16,0},{1,17},{17,1},{2,18},{18,2},{3,19},{19,3},{4,20},{20... | collective-permute-start | bytes 884744 | tf_op jit(solution)/shard_map/ppermute | solution.py:425

commit v10 on v8

--- a/solution.py
+++ b/solution.py
@@ -14,7 +14,7 @@
 GROUP = 10
 TILES = 4
 LANES = 128
-AHEAD = 3
+AHEAD = 4
 TAIL = 3
 CHUNK = 10
 SLOTS = 16

time: 51.6 us -> 51.7 us (level)
  no operation moved by 1% of the time
where the time goes in v10:
time: 51.7 us; the launch traced here: 51.5 us
  blocking collectives  35.4 us (68%)
  Pallas kernels  11.6 us (22%)
  starting transfers between devices  4.23 us (8%)
    all_to_all x2, blocking collectives, exchanged(): return lax.all_to_all(blocks, CHIP, 0, 0, tiled=True).reshape(value.shape)  35.4 us
    pallas_call x1, Pallas kernels, analysis(): pl.pallas_call(analysis_kernel, out_shape=[pltpu.VMEM((half * TILES * WAV...  5.73 us
    pallas_call x1, Pallas kernels, synthesis(): pl.pallas_call(lambda *refs: synthesis_kernel(cells, *refs), out_shape=pl...  3.26 us
    ppermute x1, starting transfers between devices, per_device(): sibling = lax.ppermute(own, 'c', swap)  2.73 us
    pallas_call x1, Pallas kernels, contract(): pl.pallas_call(contract_kernel, out_shape=[pltpu.VMEM((half * TILES * WAV...  1.55 us
    ppermute x1, starting transfers between devices, per_device(): arriving = lax.ppermute(other, 'c', swap)  1.5 us
  transfers between devices with their start and end apart: 2, of which 1 were waited for; matrix products, arithmetic and copies ran while one was open for 0% of the time, Pallas kernels for 5%

profile of v10, /device:TPU:1, one launch (start us, length us, event | category | flops | bytes accessed | tf_op | source)
XLA Modules:
  0.0 51.5 jit_solution(8009244992565472256)
XLA Ops:
  0.0 5.7 %analysis.1 = (f32[576,128]{1,0:T(8,128)S(1)}, bf16[2,512,256]{2,1,0:T(8,128)(2,1)S(1)}, f32[2,128,128]{2,1,0:T(8,128)S(1)}, f32[7,256,128]{2,1,0:T(8,128)S(1)},...) custom-call(f32[60,256,128]{2,1,0:T(8,128)} %model_hbm.3, ...), custom_call_target="tpu_custom_call" | custom-call | flops 2359296000 | bytes 15728640 | tf_op jit(solution)/shard_map/analysis/pallas_call | solution.py:320
  5.7 1.5 %collective-permute-start = (f32[576,128]{1,0:T(8,128)S(1)}, f32[576,128]{1,0:T(8,128)S(1)}, u32[]{:S(2)}, u32[]{:S(2)}) collective-permute-start(f32[576,128]{1,0:T(8,128)S(1)} %get-tuple-element.27), channel_id=1, source_target_pairs={{0,16},{16,0},{1,17},{17,1},{2,18},{18,2},{3,19},{19,3},{4,20},{20... | collective-permute-start | bytes 884744 | tf_op jit(solution)/shard_map/ppermute | solution.py:443
  7.2 1.6 %contract.1 = (f32[576,128]{1,0:T(8,128)S(1)}, f32[3,256,128]{2,1,0:T(8,128)S(1)}) custom-call(bf16[2,512,256]{2,1,0:T(8,128)(2,1)S(1)} %get-tuple-element.20.along_own, f32[2,128,128]{2,1,0:T(8,128)S(1)} %get-tuple-element.21.squares_own, f32[7,256,128]{2,1,0:T(8,128)S(1)} %get-tuple-element.22.driver_last, ...), custom_call_target="tpu_custom_call" | custom-call | flops 275251200 | bytes 1835008 | tf_op jit(solution)/shard_map/contract/pallas_call | solution.py:356
  8.8 0.0 collective-permute-done
  8.8 21.1 %all_to_all.10 = f32[64,1,1152]{2,1,0:T(1,128)S(1)} all-to-all(f32[64,1,1152]{2,1,0:T(1,128)S(1)} %bitcast.8), channel_id=1, replica_groups=mesh['x'=4,'c'=2,'z'=4,'y'=4] {'x','z','y'}, dimensions={0} | all-to-all | bytes 589824 | tf_op jit(solution)/shard_map/all_to_all | solution.py:452
  30.0 0.1 share.1
  30.0 14.2 %all_to_all.11 = f32[64,1,1152]{2,1,0:T(1,128)S(1)} all-to-all(f32[64,1,1152]{2,1,0:T(1,128)S(1)} %bitcast.7), channel_id=1, replica_groups=mesh['x'=4,'c'=2,'z'=4,'y'=4] {'x','z','y'}, dimensions={0} | all-to-all | bytes 589824 | tf_op jit(solution)/shard_map/all_to_all | solution.py:452
  44.3 2.7 %collective-permute-start.1 = (f32[576,128]{1,0:T(8,128)S(1)}, f32[576,128]{1,0:T(8,128)S(1)}, u32[]{:S(2)}, u32[]{:S(2)}) collective-permute-start(f32[576,128]{1,0:T(8,128)S(1)} %bitcast.4), channel_id=1, source_target_pairs={{0,16},{16,0},{1,17},{17,1},{2,18},{18,2},{3,19},{19,3},{4,20},{20... | collective-permute-start | bytes 884744 | tf_op jit(solution)/shard_map/ppermute | solution.py:455
  47.0 1.0 %begin.1 = (bf16[20,144,128]{2,1,0:T(8,128)(2,1)S(1)}, f32[10,256,128]{2,1,0:T(8,128)S(1)}) custom-call(f32[576,128]{1,0:T(8,128)S(1)} %bitcast.5, f32[96,128]{1,0:T(8,128)S(1)} %get-tuple-element.28.refs_1_.refs_3_, f32[96,128]{1,0:T(8,128)S(1)} %get-tuple-element.29.refs_2_.refs_4_, f32[60,256,128]{2,1,0:T(8,128)S(1)} %get-tuple-element.23.model.refs_3_.refs_5_, ...), custom_call_target="tpu_custom_call" | custom-call | flops 221184000 | bytes 1474560 | tf_op jit(solution)/shard_map/begin/pallas_call | solution.py:378
  48.0 0.2 collective-permute-done.1.refs_2_
  48.2 3.3 %synthesis.1 = f32[60,256,128]{2,1,0:T(8,128)} custom-call(bf16[20,144,128]{2,1,0:T(8,128)(2,1)S(1)} %get-tuple-element.32.refs_0_, f32[10,256,128]{2,1,0:T(8,128)S(1)} %get-tuple-element.33.refs_1_, f32[576,128]{1,0:T(8,128)S(1)} %collective-permute-done.1.refs_2_, f32[96,128]{1,0:T(8,128)S(1)} %get-tuple-element.28.refs_1_.refs_3_, ...), custom_call_target="tpu_custom_call" | custom-call | flops 2359296000 | bytes 15728640 | tf_op jit(solution)/shard_map/synthesis/pallas_call | solution.py:395
  (1 shorter events, 0.0 us)
Async XLA Ops:
  5.7 3.1 %collective-permute-start = (f32[576,128]{1,0:T(8,128)S(1)}, f32[576,128]{1,0:T(8,128)S(1)}, u32[]{:S(2)}, u32[]{:S(2)}) collective-permute-start(f32[576,128]{1,0:T(8,128)S(1)} %get-tuple-element.27), channel_id=1, source_target_pairs={{0,16},{16,0},{1,17},{17,1},{2,18},{18,2},{3,19},{19,3},{4,20},{20... | collective-permute-start | bytes 884744 | tf_op jit(solution)/shard_map/ppermute | solution.py:443
  44.3 3.9 %collective-permute-start.1 = (f32[576,128]{1,0:T(8,128)S(1)}, f32[576,128]{1,0:T(8,128)S(1)}, u32[]{:S(2)}, u32[]{:S(2)}) collective-permute-start(f32[576,128]{1,0:T(8,128)S(1)} %bitcast.4), channel_id=1, source_target_pairs={{0,16},{16,0},{1,17},{17,1},{2,18},{18,2},{3,19},{19,3},{4,20},{20... | collective-permute-start | bytes 884744 | tf_op jit(solution)/shard_map/ppermute | solution.py:455
